TPU v7x, 32 devices: a whole 2x2x4 slice. The times are simulated.
32 devices in a mesh: clip: 16 (over z, x, core), seq: 2 (over y).
Axes of the slice: x: 2, y: 2, z: 4, core: 2. Of those that a mesh axis runs over, the one named last changes fastest.
Arguments:
- frames: float32 [16, 1024, 768], P('clip', 'seq'), may hold values from -6 to 6
- cotangent: float32 [16, 1024, 768], P('clip', 'seq'), may hold values from -6 to 6
- first_gain: float32 [2, 768], P(None, ('clip', 'seq')), may hold values from 0.5 to 1.5
- first_shift: float32 [2, 768], P(None, ('clip', 'seq')), may hold values from -2 to 2
- mixing_weight: float32 [2, 768, 2304], P(None, ('clip', 'seq')), may hold values from -0.3125 to 0.3125
- mixing_bias: float32 [2, 1536], P(None, ('clip', 'seq')), may hold values from -2 to 2
- output_weight: float32 [2, 768, 768], P(None, ('clip', 'seq')), may hold values from -0.625 to 0.625
- output_bias: float32 [2, 768], P(None, ('clip', 'seq')), may hold values from -2 to 2
- second_gain: float32 [2, 768], P(None, ('clip', 'seq')), may hold values from 0.5 to 1.5
- second_shift: float32 [2, 768], P(None, ('clip', 'seq')), may hold values from -2 to 2
- up_weight: float32 [2, 768, 3072], P(None, ('clip', 'seq')), may hold values from -0.21875 to 0.21875
- up_bias: float32 [2, 3072], P(None, ('clip', 'seq')), may hold values from -3 to 3
- down_weight: float32 [2, 3072, 768], P(None, ('clip', 'seq')), may hold values from -0.15625 to 0.15625
- down_bias: float32 [2, 768], P(None, ('clip', 'seq')), may hold values from -2 to 2
Outputs:
- activations: float32 [16, 1024, 768], P('clip', 'seq')
- input_grad: float32 [16, 1024, 768], P('clip', 'seq')
- first_gain_grad: float32 [2, 768], P(None, ('clip', 'seq'))
- first_shift_grad: float32 [2, 768], P(None, ('clip', 'seq'))
- mixing_weight_grad: float32 [2, 768, 2304], P(None, ('clip', 'seq'))
- mixing_bias_grad: float32 [2, 1536], P(None, ('clip', 'seq'))
- output_weight_grad: float32 [2, 768, 768], P(None, ('clip', 'seq'))
- output_bias_grad: float32 [2, 768], P(None, ('clip', 'seq'))
- second_gain_grad: float32 [2, 768], P(None, ('clip', 'seq'))
- second_shift_grad: float32 [2, 768], P(None, ('clip', 'seq'))
- up_weight_grad: float32 [2, 768, 3072], P(None, ('clip', 'seq'))
- up_bias_grad: float32 [2, 3072], P(None, ('clip', 'seq'))
- down_weight_grad: float32 [2, 3072, 768], P(None, ('clip', 'seq'))
- down_bias_grad: float32 [2, 768], P(None, ('clip', 'seq'))
All inputs are finite; a program needn't handle non-finite values.
Results may differ from a plain program's by a relative error of at most 0.017.
The roundings to bfloat16 on the way count: a program that leaves them out, or rounds other values in their place, can miss the bound.
Values may be sent and summed in bfloat16 or wider, within the bound.
No kernel may reach another device: no remote copies, remote signals or barrier semaphores. Data moves between devices by JAX's collectives and lax.ppermute only.
A program may use at most 320 MiB of HBM per device.

v0:
```python
import math

import jax
import jax.numpy as jnp
from jax import lax
from jax.sharding import PartitionSpec as P

HEAD_DIM = 64
LAYERS = 2


EPSILON = 1e-05


def layer_norm(rows, gain, shift):
    center = jnp.mean(rows, axis=-1, keepdims=True)
    spread = rows - center
    variance = jnp.mean(spread * spread, axis=-1, keepdims=True)
    return spread * lax.rsqrt(variance + EPSILON) * gain + shift


def normalize(rows, gain):
    return layer_norm(rows, gain, 0.0)


def gelu_exact(values):
    return jax.nn.gelu(values, approximate=False)


def project(left, right):
    return jnp.einsum("cfk,kn->cfn", left, right, preferred_element_type=jnp.float32)


def project_back(left, right):
    return jnp.einsum("cfn,kn->cfk", left, right, preferred_element_type=jnp.float32)


def outer_total(left, right):
    return jnp.einsum("cfk,cfn->kn", left, right, preferred_element_type=jnp.float32)


def column_total(values):
    return jnp.sum(values.astype(jnp.float32), axis=(0, 1))


def pack_own(arrays):
    return jnp.concatenate([array.reshape(1, -1) for array in arrays], axis=1)


def unpack_whole(packed, layouts):
    pieces = []
    offset = 0
    owners = packed.shape[0]
    for layout in layouts:
        amount = math.prod(layout)
        part = packed[:, offset : offset + amount]
        pieces.append(part.reshape((owners * layout[0],) + tuple(layout[1:])))
        offset = offset + amount
    return tuple(pieces)


def pack_owners(arrays, owners):
    return jnp.concatenate([array.reshape(owners, -1) for array in arrays], axis=1)


def unpack_own(packed, layouts):
    pieces = []
    offset = 0
    for layout in layouts:
        amount = math.prod(layout)
        pieces.append(packed[0, offset : offset + amount].reshape(layout))
        offset = offset + amount
    return pieces


def heads_of(array, index):
    piece = lax.dynamic_slice_in_dim(array, index * 128, 128, 2)
    return piece.reshape(piece.shape[0], piece.shape[1], 128 // HEAD_DIM, HEAD_DIM)


def join_heads(pieces, width):
    return jnp.moveaxis(pieces, 0, 2).reshape(pieces.shape[1], pieces.shape[2], width)


def attend_forward(query, keys, values):
    clips, frames_here, width = query.shape
    scale = HEAD_DIM ** (-0.5)

    def block(index):
        query_part = heads_of(query, index)
        key_part = heads_of(keys, index)
        value_part = heads_of(values, index)
        scores = (
            jnp.einsum("cfhd,clhd->chfl", query_part, key_part, preferred_element_type=jnp.float32)
            * scale
        )
        highest = jnp.max(scores, axis=-1, keepdims=True)
        weights = jnp.exp(scores - highest)
        total = jnp.sum(weights, axis=-1, keepdims=True)
        probs = (weights / total).astype(jnp.bfloat16)
        mixed = jnp.einsum("chfl,clhd->cfhd", probs, value_part, preferred_element_type=jnp.float32)
        return (mixed.reshape(clips, frames_here, 128), highest[..., 0] + jnp.log(total[..., 0]))

    pieces, logsum = lax.map(block, jnp.arange(width // 128))
    return (join_heads(pieces, width), logsum)


def attend_backward(query, keys, values, grad_mixed, logsum):
    clips, frames_here, width = query.shape
    length = keys.shape[1]
    scale = HEAD_DIM ** (-0.5)

    def block(pair):
        index, block_logsum = pair
        query_part = heads_of(query, index)
        key_part = heads_of(keys, index)
        value_part = heads_of(values, index)
        grad_part = heads_of(grad_mixed, index)
        scores = (
            jnp.einsum("cfhd,clhd->chfl", query_part, key_part, preferred_element_type=jnp.float32)
            * scale
        )
        probs = jnp.exp(scores - block_logsum[..., None])
        grad_probs = jnp.einsum(
            "cfhd,clhd->chfl", grad_part, value_part, preferred_element_type=jnp.float32
        )
        inner = jnp.sum(probs * grad_probs, axis=-1, keepdims=True)
        grad_scores = (probs * (grad_probs - inner)).astype(jnp.bfloat16)
        grad_query = (
            jnp.einsum("chfl,clhd->cfhd", grad_scores, key_part, preferred_element_type=jnp.float32)
            * scale
        )
        grad_keys = (
            jnp.einsum(
                "chfl,cfhd->clhd", grad_scores, query_part, preferred_element_type=jnp.float32
            )
            * scale
        )
        grad_values = jnp.einsum(
            "chfl,cfhd->clhd",
            probs.astype(jnp.bfloat16),
            grad_part,
            preferred_element_type=jnp.float32,
        )
        return (
            grad_query.reshape(clips, frames_here, 128),
            grad_keys.reshape(clips, length, 128),
            grad_values.reshape(clips, length, 128),
        )

    query_pieces, key_pieces, value_pieces = lax.map(block, (jnp.arange(width // 128), logsum))
    return (
        join_heads(query_pieces, width),
        join_heads(key_pieces, width),
        join_heads(value_pieces, width),
    )


def fetch_forward(layer, params):
    shards = [array[layer].astype(jnp.bfloat16) for array in params]
    packed = lax.all_gather(pack_own(shards), ("clip", "seq"), axis=0, tiled=True)
    return unpack_whole(packed, [shard.shape for shard in shards])


def fetch_backward(layer, params):
    shards = [params[slot][layer].astype(jnp.bfloat16) for slot in (0, 2, 4, 6, 8, 10)]
    packed = lax.all_gather(pack_own(shards), ("clip", "seq"), axis=0, tiled=True)
    return unpack_whole(packed, [shard.shape for shard in shards])


def layer_forward(hidden, gathered):
    (
        first_gain,
        first_shift,
        mixing_weight,
        mixing_bias,
        output_weight,
        output_bias,
        second_gain,
        second_shift,
        up_weight,
        up_bias,
        down_weight,
        down_bias,
    ) = gathered
    width = hidden.shape[2]
    normed = layer_norm(
        hidden, first_gain.astype(jnp.float32), first_shift.astype(jnp.float32)
    ).astype(jnp.bfloat16)
    mixed = project(normed, mixing_weight)
    offsets = mixing_bias.astype(jnp.float32)
    query = (mixed[:, :, :width] + offsets[:width]).astype(jnp.bfloat16)
    keys_here = mixed[:, :, width : 2 * width].astype(jnp.bfloat16)
    values_here = (mixed[:, :, 2 * width :] + offsets[width:]).astype(jnp.bfloat16)
    keys, values = (
        lax.all_gather(keys_here, "seq", axis=1, tiled=True),
        lax.all_gather(values_here, "seq", axis=1, tiled=True),
    )
    attended_full, logsum = attend_forward(query, keys, values)
    attended = attended_full.astype(jnp.bfloat16)
    middle = hidden + (project(attended, output_weight) + output_bias.astype(jnp.float32))
    normed_two = layer_norm(
        middle, second_gain.astype(jnp.float32), second_shift.astype(jnp.float32)
    ).astype(jnp.bfloat16)
    before = project(normed_two, up_weight) + up_bias.astype(jnp.float32)
    active = gelu_exact(before).astype(jnp.bfloat16)
    output = middle + (project(active, down_weight) + down_bias.astype(jnp.float32))
    return (
        output,
        (hidden, normed, query, keys, values, logsum, attended, middle, normed_two, before, active),
    )


def layer_backward(grad_hidden, kept, matrices, layouts):
    hidden, normed, query, keys, values, logsum, attended, middle, normed_two, before, active = kept
    first_gain, mixing_weight, output_weight, second_gain, up_weight, down_weight = matrices
    grad_down = grad_hidden.astype(jnp.bfloat16)
    down_weight_grad = outer_total(active, grad_down)
    down_bias_grad = column_total(grad_down)
    grad_active = project_back(grad_down, down_weight)
    gelu_pull = jax.vjp(gelu_exact, before)[1]
    grad_before = gelu_pull(grad_active)[0].astype(jnp.bfloat16)
    up_weight_grad = outer_total(normed_two, grad_before)
    up_bias_grad = column_total(grad_before)
    grad_normed_two = project_back(grad_before, up_weight)
    second_pull = jax.vjp(normalize, middle, second_gain.astype(jnp.float32))[1]
    grad_middle_norm, second_gain_grad = second_pull(grad_normed_two)
    second_shift_grad = jnp.sum(grad_normed_two, axis=(0, 1))
    grad_middle = grad_hidden + grad_middle_norm
    grad_branch = grad_middle.astype(jnp.bfloat16)
    output_weight_grad = outer_total(attended, grad_branch)
    output_bias_grad = column_total(grad_branch)
    grad_attended = project_back(grad_branch, output_weight).astype(jnp.bfloat16)
    grad_query_full, grad_keys_full, grad_values_full = attend_backward(
        query, keys, values, grad_attended, logsum
    )
    grad_keys_own, grad_values_own = (
        lax.psum_scatter(
            grad_keys_full.astype(jnp.bfloat16), "seq", scatter_dimension=1, tiled=True
        ).astype(jnp.float32),
        lax.psum_scatter(
            grad_values_full.astype(jnp.bfloat16), "seq", scatter_dimension=1, tiled=True
        ).astype(jnp.float32),
    )
    grad_query = grad_query_full.astype(jnp.bfloat16)
    grad_keys = grad_keys_own.astype(jnp.bfloat16)
    grad_values = grad_values_own.astype(jnp.bfloat16)
    grad_mixed = jnp.concatenate([grad_query, grad_keys, grad_values], axis=2)
    mixing_weight_grad = outer_total(normed, grad_mixed)
    mixing_bias_grad = jnp.concatenate([column_total(grad_query), column_total(grad_values)])
    grad_normed = project_back(grad_mixed, mixing_weight)
    first_pull = jax.vjp(normalize, hidden, first_gain.astype(jnp.float32))[1]
    grad_hidden_norm, first_gain_grad = first_pull(grad_normed)
    first_shift_grad = jnp.sum(grad_normed, axis=(0, 1))
    owners = lax.axis_size(("clip", "seq"))
    terms = pack_owners(
        (
            first_gain_grad,
            first_shift_grad,
            mixing_weight_grad,
            mixing_bias_grad,
            output_weight_grad,
            output_bias_grad,
            second_gain_grad,
            second_shift_grad,
            up_weight_grad,
            up_bias_grad,
            down_weight_grad,
            down_bias_grad,
        ),
        owners,
    )
    owned = lax.psum_scatter(terms, ("clip", "seq"), scatter_dimension=0, tiled=True)
    return (grad_middle + grad_hidden_norm, unpack_own(owned, layouts))


def body(
    frames,
    cotangent,
    first_gain,
    first_shift,
    mixing_weight,
    mixing_bias,
    output_weight,
    output_bias,
    second_gain,
    second_shift,
    up_weight,
    up_bias,
    down_weight,
    down_bias,
):
    params = (
        first_gain,
        first_shift,
        mixing_weight,
        mixing_bias,
        output_weight,
        output_bias,
        second_gain,
        second_shift,
        up_weight,
        up_bias,
        down_weight,
        down_bias,
    )
    layouts = [array.shape[1:] for array in params]
    hidden = frames
    records = []
    for layer in range(LAYERS):
        gathered = fetch_forward(layer, params)
        hidden, kept = layer_forward(hidden, gathered)
        records.append(kept)
    grad_hidden = cotangent
    shares = [None] * LAYERS
    for layer in reversed(range(LAYERS)):
        matrices = fetch_backward(layer, params)
        grad_hidden, layer_shares = layer_backward(grad_hidden, records[layer], matrices, layouts)
        shares[layer] = layer_shares
    stacked = [jnp.stack([entry[slot] for entry in shares]) for slot in range(12)]
    return tuple([hidden, grad_hidden] + stacked)


def solution(mesh):
    return jax.shard_map(
        body,
        mesh=mesh,
        in_specs=(
            P("clip", "seq", None),
            P("clip", "seq", None),
            P(None, ("clip", "seq")),
            P(None, ("clip", "seq")),
            P(None, ("clip", "seq"), None),
            P(None, ("clip", "seq")),
            P(None, ("clip", "seq"), None),
            P(None, ("clip", "seq")),
            P(None, ("clip", "seq")),
            P(None, ("clip", "seq")),
            P(None, ("clip", "seq"), None),
            P(None, ("clip", "seq")),
            P(None, ("clip", "seq"), None),
            P(None, ("clip", "seq")),
        ),
        out_specs=(
            P("clip", "seq", None),
            P("clip", "seq", None),
            P(None, ("clip", "seq")),
            P(None, ("clip", "seq")),
            P(None, ("clip", "seq"), None),
            P(None, ("clip", "seq")),
            P(None, ("clip", "seq"), None),
            P(None, ("clip", "seq")),
            P(None, ("clip", "seq")),
            P(None, ("clip", "seq")),
            P(None, ("clip", "seq"), None),
            P(None, ("clip", "seq")),
            P(None, ("clip", "seq"), None),
            P(None, ("clip", "seq")),
        ),
        check_vma=False,
    )
```

profile of v0, /device:TPU:0, one launch (start us, length us, event | category | flops | bytes accessed | tf_op | source)
XLA Modules:
  0.0 2205.9 jit_solution(3040056849272548786)
XLA Ops:
  59.9 6.6 dynamic-update-slice.44
  67.9 6.4 dynamic-update-slice.46
  76.4 137.7 %all-gather.21.cloned.1.call-done = bf16[32,1,221472]{2,1,0:T(2,128)(2,1)} async-done(((bf16[1,1,221472]{2,1,0:T(2,128)(2,1)}), bf16[32,1,221472]{2,1,0:T(2,128)(2,1)}) %all-gather.21.cloned.1.call-update) | async-done | bytes 14174224 | tf_op jit(solution)/shard_map/all_gather | solution.py:161
  214.1 15.4 copy.89
  266.8 10.0 fusion.111
  296.5 88.6 %all-gather.23.cloned.1.call-done = bf16[32,1,221472]{2,1,0:T(2,128)(2,1)} async-done(((bf16[1,1,221472]{2,1,0:T(2,128)(2,1)}), bf16[32,1,221472]{2,1,0:T(2,128)(2,1)}) %all-gather.23.cloned.1.call-update) | async-done | bytes 14174224 | tf_op jit(solution)/shard_map/all_gather | solution.py:161
  385.1 15.4 copy.88
  414.4 26.9 %all-gather.15.cloned.1.call-done = bf16[1,1024,768]{2,1,0:T(8,128)(2,1)} async-done(((bf16[1,512,768]{2,1,0:T(8,128)(2,1)}), bf16[1,1024,768]{2,1,0:T(8,128)(2,1)}) %all-gather.15.cloned.1.call-update) | async-done | bytes 1572880 | tf_op jit(solution)/shard_map/all_gather | solution.py:196
  444.9 40.7 %while.52 = (s32[]{:T(128)}, bf16[6,1,512,128]{2,3,1,0:T(8,128)(2,1)}, f32[6,1,2,512]{3,2,1,0:T(2,128)S(1)}, s32[6]{0:T(128)S(1)}, bf16[1,1024,768]{1,2,0:T(8,12...) while((s32[]{:T(128)}, ...), condition=%wide.region_5.6_spmd, body=%wide.region_2.5_spmd.sunk | while | flops 277871616 | bytes 14975167 | solution.py:104
  489.8 19.6 multiply_convert_fusion.3
  535.4 78.7 %all-gather.25.cloned.1.call-done = bf16[32,1,221232]{2,1,0:T(2,128)(2,1)} async-done(((bf16[1,1,221232]{2,1,0:T(2,128)(2,1)}), bf16[32,1,221232]{2,1,0:T(2,128)(2,1)}) %all-gather.25.cloned.1.call-update) | async-done | bytes 14158864 | tf_op jit(solution)/shard_map/all_gather | solution.py:167
  614.1 13.6 copy.91
  633.1 9.8 fusion.113
  659.0 9.9 fusion.110
  682.4 35.7 %while.53 = (s32[]{:T(128)}, bf16[6,1,512,128]{2,3,1,0:T(8,128)(2,1)}, f32[6,1,2,512]{3,2,1,0:T(2,128)S(1)}, s32[6]{0:T(128)S(1)}, bf16[1,1024,768]{1,2,0:T(8,12...) while((s32[]{:T(128)}, ...), condition=%wide.region_13.14_spmd, body=%wide.region_10.13_spmd.sunk | while | flops 277871616 | bytes 14975167 | solution.py:104
  721.5 20.2 multiply_convert_fusion.2
  741.7 7.5 convert_reduce_fusion
  760.2 88.3 %while.54 = (s32[]{:T(128)}, bf16[6,1,512,128]{2,3,1,0:T(8,128)(2,1)}, bf16[6,1,1024,128]{2,3,1,0:T(8,128)(2,1)}, bf16[6,1,1024,128]{2,3,1,0:T(8,128)(2,1)}, s32...) while((s32[]{:T(128)}, ...), condition=%wide.region_20.21_spmd, body=%wide.region_18.20_spmd.sunk | while | flops 684063744 | bytes 53375232 | solution.py:151
  848.6 18.6 copy.90
  867.3 9.9 fusion.112
  896.9 6.2 reshape.1327
  912.1 9.0 convert_reduce_fusion.1
  933.5 102.7 %while.55 = (s32[]{:T(128)}, bf16[6,1,512,128]{2,3,1,0:T(8,128)(2,1)}, bf16[6,1,1024,128]{2,3,1,0:T(8,128)(2,1)}, bf16[6,1,1024,128]{2,3,1,0:T(8,128)(2,1)}, s32...) while((s32[]{:T(128)}, ...), condition=%wide.region_29.30_spmd, body=%wide.region_27.29_spmd.sunk | while | flops 684063744 | bytes 53375232 | solution.py:151
  1046.6 9.0 fusion.88
  1064.1 8.2 reshape.1350
  1072.4 8.6 fusion.71
  1081.0 8.1 reshape.1352
  1090.9 7.0 fusion.53
  1097.9 6.7 reshape.1345
  1114.6 8.9 fusion.94
  1123.4 8.4 reshape.1339
  1131.9 8.2 fusion.62
  1140.0 8.1 reshape.1341
  1151.1 20.5 dynamic-update-slice.2
  1173.1 9.3 dynamic-update-slice.4
  1186.9 28.8 %dynamic-update-slice.8 = f32[32,221472]{1,0:T(8,128)} dynamic-update-slice(f32[32,221472]{1,0:T(8,128)} %dynamic-update-slice.7, f32[32,73728]{1,0:T(8,128)} %reshape.1350, s32[]{} %constant.220, s32[]{} %constant.229) | dynamic-update-slice | bytes 18874372
  1217.2 28.3 %dynamic-update-slice.10 = f32[32,221472]{1,0:T(8,128)} dynamic-update-slice(f32[32,221472]{1,0:T(8,128)} %dynamic-update-slice.9, f32[32,73728]{1,0:T(8,128)} %reshape.1352, s32[]{} %constant.220, s32[]{} %constant.231) | dynamic-update-slice | bytes 18874372
  1246.9 6.3 fusion.44
  1255.0 7.0 fusion.51
  1262.0 6.7 reshape.1334
  1271.9 20.5 dynamic-update-slice.14
  1293.9 9.3 dynamic-update-slice.16
  1307.8 28.7 %dynamic-update-slice.20 = f32[32,221472]{1,0:T(8,128)} dynamic-update-slice(f32[32,221472]{1,0:T(8,128)} %dynamic-update-slice.19, f32[32,73728]{1,0:T(8,128)} %reshape.1339, s32[]{} %constant.220, s32[]{} %constant.229) | dynamic-update-slice | bytes 18874372
  1338.1 28.4 %dynamic-update-slice.22 = f32[32,221472]{1,0:T(8,128)} dynamic-update-slice(f32[32,221472]{1,0:T(8,128)} %dynamic-update-slice.21, f32[32,73728]{1,0:T(8,128)} %reshape.1341, s32[]{} %constant.220, s32[]{} %constant.231) | dynamic-update-slice | bytes 18874372
  1367.9 6.5 reshape.1317
  1374.5 7.8 bitcast_add_fusion
  1385.2 789.1 %all-reduce.5.cloned.1.call-done = (f32[32,221472]{1,0:T(8,128)}, f32[32,221472]{1,0:T(8,128)}) async-done(((f32[32,221472]{1,0:T(8,128)}, f32[32,221472]{1,0:T(8,128)}), (f32[32,221472]{1,0:T(8,128)}, f32[32,221472]{1,0:T(8,128)})) %all-reduce.5.cloned.1.call-update) | async-done | bytes 56696848
  2182.6 7.4 dynamic-slice_reduce_fusion
  (844 shorter events, 576.0 us)
Async XLA Ops:
  7.2 206.9 %all-gather.21.cloned.1.call-start = ((), (), s32[]{:S(2)}) async-start(), calls=%async_computation.12 | async-start | bytes 29246976 | tf_op jit(solution)/shard_map/all_gather | solution.py:161
  8.0 33.2 %copy-start.90 = (bf16[1,24]{1,0:T(2,128)(2,1)}, bf16[1,24]{1,0:T(2,128)(2,1)S(1)}, u32[]{:S(2)}) copy-start(bf16[1,24]{1,0:T(2,128)(2,1)S(1)} %get-tuple-element.494) | copy-start | bytes 148
  11.1 31.4 %copy-start.41 = (bf16[1,1,24,2304]{3,1,2,0:T(2,128)(2,1)}, bf16[1,1,24,2304]{3,1,2,0:T(2,128)(2,1)S(1)}, u32[]{:S(2)}) copy-start(bf16[1,1,24,2304]{3,1,2,0:T(2,128)(2,1)S(1)} %copy.76) | copy-start | bytes 331780
  13.3 38.3 %copy-start.51 = (bf16[1,1,24,768]{3,1,2,0:T(2,128)(2,1)}, bf16[1,1,24,768]{3,1,2,0:T(2,128)(2,1)S(1)}, u32[]{:S(2)}) copy-start(bf16[1,1,24,768]{3,1,2,0:T(2,128)(2,1)S(1)} %copy.77) | copy-start | bytes 110596
  15.2 36.3 %copy-start.92 = (bf16[1,24]{1,0:T(2,128)(2,1)}, bf16[1,24]{1,0:T(2,128)(2,1)S(1)}, u32[]{:S(2)}) copy-start(bf16[1,24]{1,0:T(2,128)(2,1)S(1)} %get-tuple-element.486) | copy-start | bytes 148
  17.8 57.8 %copy-start.33 = (bf16[1,1,24,3072]{3,1,2,0:T(2,128)(2,1)}, bf16[1,1,24,3072]{3,1,2,0:T(2,128)(2,1)S(1)}, u32[]{:S(2)}) copy-start(bf16[1,1,24,3072]{3,1,2,0:T(2,128)(2,1)S(1)} %copy.78) | copy-start | bytes 442372
  19.1 56.7 %copy-start.7 = (f32[1,512,768]{2,1,0:T(8,128)S(1)}, f32[1,512,768]{2,1,0:T(8,128)}, u32[]{:S(2)}) copy-start(f32[1,512,768]{2,1,0:T(8,128)} %param.22) | copy-start | bytes 4718596
  20.0 56.0 %copy-start.35 = (bf16[1,1,96,768]{3,1,2,0:T(2,128)(2,1)}, bf16[1,1,96,768]{3,1,2,0:T(2,128)(2,1)S(1)}, u32[]{:S(2)}) copy-start(bf16[1,1,96,768]{3,1,2,0:T(2,128)(2,1)S(1)} %copy.79) | copy-start | bytes 442372
  41.2 343.9 %all-gather.23.cloned.1.call-start = ((), (), s32[]{:S(2)}) async-start(), calls=%async_computation.13 | async-start | bytes 29246976 | tf_op jit(solution)/shard_map/all_gather | solution.py:161
  42.4 187.1 %copy-start.43 = (bf16[1,1,24,2304]{3,1,2,0:T(2,128)(2,1)}, bf16[1,1,24,2304]{3,1,2,0:T(2,128)(2,1)S(1)}, u32[]{:S(2)}) copy-start(bf16[1,1,24,2304]{3,1,2,0:T(2,128)(2,1)S(1)} %copy.80) | copy-start | bytes 331780
  42.5 187.0 %copy-start.53 = (bf16[1,1,24,768]{3,1,2,0:T(2,128)(2,1)}, bf16[1,1,24,768]{3,1,2,0:T(2,128)(2,1)S(1)}, u32[]{:S(2)}) copy-start(bf16[1,1,24,768]{3,1,2,0:T(2,128)(2,1)S(1)} %copy.81) | copy-start | bytes 110596
  42.7 186.8 %copy-start.37 = (bf16[1,1,24,3072]{3,1,2,0:T(2,128)(2,1)}, bf16[1,1,24,3072]{3,1,2,0:T(2,128)(2,1)S(1)}, u32[]{:S(2)}) copy-start(bf16[1,1,24,3072]{3,1,2,0:T(2,128)(2,1)S(1)} %copy.82) | copy-start | bytes 442372
  44.0 185.5 %copy-start.39 = (bf16[1,1,96,768]{3,1,2,0:T(2,128)(2,1)}, bf16[1,1,96,768]{3,1,2,0:T(2,128)(2,1)S(1)}, u32[]{:S(2)}) copy-start(bf16[1,1,96,768]{3,1,2,0:T(2,128)(2,1)S(1)} %copy.83) | copy-start | bytes 442372
  75.6 337.1 %all-gather.13.cloned.1.call-start = ((), (), s32[]{:S(2)}) async-start(), calls=%async_computation.4 | async-start | bytes 2359296 | tf_op jit(solution)/shard_map/all_gather | solution.py:197
  76.0 164.6 %copy-start.59 = (f32[512]{0:T(512)}, f32[512]{0:T(512)S(1)}, u32[]{:S(2)}) copy-start(f32[512]{0:T(512)S(1)} %broadcast_multiply_fusion.3) | copy-start | bytes 6148
  76.3 153.2 %copy-start.71 = (f32[512]{0:T(512)}, f32[512]{0:T(512)S(1)}, u32[]{:S(2)}) copy-start(f32[512]{0:T(512)S(1)} %multiply_reduce_fusion.7) | copy-start | bytes 6148
  76.3 164.3 %copy-start.82 = (f32[512]{0:T(512)}, f32[512]{0:T(512)S(1)}, u32[]{:S(2)}) copy-start(f32[512]{0:T(512)S(1)} %fusion.76) | copy-start | bytes 6148
  248.6 192.7 %all-gather.15.cloned.1.call-start = ((), (), s32[]{:S(2)}) async-start(), calls=%async_computation.5 | async-start | bytes 2359296 | tf_op jit(solution)/shard_map/all_gather | solution.py:196
  251.2 363.0 %all-gather.25.cloned.1.call-start = ((), (), s32[]{:S(2)}) async-start(), calls=%async_computation.14 | async-start | bytes 29213184 | tf_op jit(solution)/shard_map/all_gather | solution.py:167
  266.7 410.3 %all-gather.17.cloned.1.call-start = ((), (), s32[]{:S(2)}) async-start(), calls=%async_computation.6 | async-start | bytes 2359296 | tf_op jit(solution)/shard_map/all_gather | solution.py:197
  283.6 206.2 %copy-start.79 = (f32[3072]{0:T(1024)}, f32[3072]{0:T(1024)S(1)}, u32[]{:S(2)}) copy-start(f32[3072]{0:T(1024)S(1)} %reshape.1359) | copy-start | bytes 36868
  289.7 200.0 %copy-start.98 = (f32[768]{0:T(1024)}, f32[768]{0:T(1024)S(1)}, u32[]{:S(2)}) copy-start(f32[768]{0:T(1024)S(1)} %reshape.1358) | copy-start | bytes 9220
  411.3 101.3 %copy-start.102 = (f32[768]{0:T(1024)}, f32[768]{0:T(1024)S(1)}, u32[]{:S(2)}) copy-start(f32[768]{0:T(1024)S(1)} %reshape.1362) | copy-start | bytes 9220
  411.4 101.2 %copy-start.104 = (f32[768]{0:T(1024)}, f32[768]{0:T(1024)S(1)}, u32[]{:S(2)}) copy-start(f32[768]{0:T(1024)S(1)} %reshape.1361) | copy-start | bytes 9220
  444.9 40.8 %copy-start.8 = (f32[1,512,768]{2,1,0:T(8,128)S(1)}, f32[1,512,768]{2,1,0:T(8,128)}, u32[]{:S(2)}) copy-start(f32[1,512,768]{2,1,0:T(8,128)} %param.22) | copy-start | bytes 4718596
  444.9 40.8 %copy-start.112 = (f32[768]{0:T(1024)S(1)}, f32[768]{0:T(1024)}, u32[]{:S(2)}) copy-start(f32[768]{0:T(1024)} %reshape.1356) | copy-start | bytes 9220
  485.6 23.8 %copy-start.14 = (bf16[1,1024,768]{1,2,0:T(8,128)(2,1)}, bf16[1,1024,768]{1,2,0:T(8,128)(2,1)S(1)}, u32[]{:S(2)}) copy-start(bf16[1,1024,768]{1,2,0:T(8,128)(2,1)S(1)} %get-tuple-element.936) | copy-start | bytes 4718596
  485.6 23.8 %copy-start.56 = (f32[6,1,2,512]{3,2,1,0:T(2,128)}, f32[6,1,2,512]{3,2,1,0:T(2,128)S(1)}, u32[]{:S(2)}) copy-start(f32[6,1,2,512]{3,2,1,0:T(2,128)S(1)} %get-tuple-element.878) | copy-start | bytes 73732
  485.7 23.8 %slice-start = ((s8[4718592]{0:T(1024)(128)(4,1)}), s8[4194304]{0:T(1024)(128)(4,1)S(1)}, s32[]{:S(2)}) async-start(s8[4718592]{0:T(1024)(128)(4,1)} %bitcast.477), calls=%async_computation.17 | async-start | bytes 8388608
  488.7 20.8 copy-start.15
  488.7 20.7 copy-start.61
  517.3 161.5 %all-gather.19.cloned.1.call-start = ((), (), s32[]{:S(2)}) async-start(), calls=%async_computation.7 | async-start | bytes 2359296 | tf_op jit(solution)/shard_map/all_gather | solution.py:196
  519.7 328.9 %all-gather.27.cloned.1.call-start = ((), (), s32[]{:S(2)}) async-start(), calls=%async_computation.15 | async-start | bytes 29213184 | tf_op jit(solution)/shard_map/all_gather | solution.py:167
  535.3 367.7 %reduce-scatter.7.cloned.1.call-start = ((), (), s32[]{:S(2)}) async-start(), calls=%async_computation.9 | async-start | bytes 2359296 | tf_op jit(solution)/shard_map/reduce_scatter | solution.py:241
  676.6 44.9 %copy-start.106 = (f32[768]{0:T(1024)}, f32[768]{0:T(1024)S(1)}, u32[]{:S(2)}) copy-start(f32[768]{0:T(1024)S(1)} %reshape.1365) | copy-start | bytes 9220
  676.6 44.8 %copy-start.108 = (f32[768]{0:T(1024)}, f32[768]{0:T(1024)S(1)}, u32[]{:S(2)}) copy-start(f32[768]{0:T(1024)S(1)} %reshape.1364) | copy-start | bytes 9220
  718.1 23.7 %slice-start.4 = ((s8[4718592]{0:T(1024)(128)(4,1)}), s8[4194304]{0:T(1024)(128)(4,1)S(1)}, s32[]{:S(2)}) async-start(s8[4718592]{0:T(1024)(128)(4,1)} %bitcast.481), calls=%async_computation.21 | async-start | bytes 8388608
  718.1 31.2 %slice-start.2 = ((s8[4718592]{0:T(1024)(128)(4,1)}), s8[4194304]{0:T(1024)(128)(4,1)S(1)}, s32[]{:S(2)}) async-start(s8[4718592]{0:T(1024)(128)(4,1)} %bitcast.479), calls=%async_computation.19 | async-start | bytes 8388608
  721.1 31.5 %copy-start.17 = (f32[1,512,768]{2,1,0:T(8,128)}, f32[1,512,768]{2,1,0:T(8,128)S(1)}, u32[]{:S(2)}) copy-start(f32[1,512,768]{2,1,0:T(8,128)S(1)} %get-tuple-element.501) | copy-start | bytes 4718596
  721.2 31.5 %copy-start.67 = (f32[512]{0:T(512)}, f32[512]{0:T(512)S(1)}, u32[]{:S(2)}) copy-start(f32[512]{0:T(512)S(1)} %broadcast_multiply_fusion) | copy-start | bytes 6148
  721.5 31.2 %copy-start.88 = (f32[512]{0:T(512)}, f32[512]{0:T(512)S(1)}, u32[]{:S(2)}) copy-start(f32[512]{0:T(512)S(1)} %fusion.79) | copy-start | bytes 6148
  721.5 27.7 %slice-start.3 = ((s8[4718592]{0:T(1024)(128)(4,1)}), s8[524288]{0:T(1024)(128)(4,1)S(1)}, s32[]{:S(2)}) async-start(s8[4718592]{0:T(1024)(128)(4,1)} %bitcast.479), calls=%async_computation.20 | async-start | bytes 1048576
  848.6 54.5 %reduce-scatter.5.cloned.1.call-start = ((), (), s32[]{:S(2)}) async-start(), calls=%async_computation.8 | async-start | bytes 2359296 | tf_op jit(solution)/shard_map/reduce_scatter | solution.py:238
  867.3 379.6 %reduce-scatter.11.cloned.1.call-start = ((), (), s32[]{:S(2)}) async-start(), calls=%async_computation.11 | async-start | bytes 2359296 | tf_op jit(solution)/shard_map/reduce_scatter | solution.py:241
  1036.3 210.6 %reduce-scatter.9.cloned.1.call-start = ((), (), s32[]{:S(2)}) async-start(), calls=%async_computation.10 | async-start | bytes 2359296 | tf_op jit(solution)/shard_map/reduce_scatter | solution.py:238
  1055.6 1118.7 %all-reduce.5.cloned.1.call-start = ((), (), s32[]{:S(2)}) async-start(), calls=%async_computation.16 | async-start | bytes 113442816
  1217.2 29.7 %copy-start.60 = (f32[512]{0:T(512)S(1)}, f32[512]{0:T(512)}, u32[]{:S(2)}) copy-start(f32[512]{0:T(512)} %copy-done.59) | copy-start | bytes 6148
  1217.2 29.7 %copy-start.83 = (f32[512]{0:T(512)S(1)}, f32[512]{0:T(512)}, u32[]{:S(2)}) copy-start(f32[512]{0:T(512)} %copy-done.82) | copy-start | bytes 6148
  (98 other events, 600.9 us)
Sparse Core Ops, SparseCore 0:
  41.4 172.6 all-gather.20
  216.9 168.1 all-gather.22
  387.2 25.3 all-gather.12
  414.1 27.2 all-gather.14
  444.2 169.8 all-gather.24
  615.5 25.3 all-gather.16
  642.5 27.2 all-gather.18
  672.8 169.8 all-gather.26
  848.7 24.3 reduce-scatter.6
  875.2 26.0 reduce-scatter.4
  1036.4 24.3 reduce-scatter.10
  1062.9 26.0 reduce-scatter.8
  1368.0 806.2 all-reduce.4
where the time goes:
time: 2220 us; the launch traced here: 2210 us
  waiting for transfers between devices  1120 us (50%)
  local copies, waits for them, and re-layouts  699 us (31%)
  matrix products  286 us (13%)
  other arithmetic  64.8 us (3%)
    unnamed x14, waiting for transfers between devices  789 us
    unnamed x312, local copies, waits for them, and re-layouts  358 us
    all_gather x2, waiting for transfers between devices, fetch_forward(): lax.all_gather(pack_own(shards), ('clip', 'seq'), axis=0, tiled=True)  226 us
    all_gather x2, waiting for transfers between devices, fetch_backward(): lax.all_gather(pack_own(shards), ('clip', 'seq'), axis=0, tiled=True)  78.8 us
    reshape x16, local copies, waits for them, and re-layouts, unpack_whole(): pieces.append(part.reshape((owners * layout[0],) + tuple(layout[1:])))  70.8 us
    dot_general x8, matrix products, project(): jnp.einsum('cfk,kn->cfn', left, right, preferred_element_type=jnp.float32)  63.1 us
    slice x12, local copies, waits for them, and re-layouts, unpack_whole(): part = packed[:, offset:offset + amount]  56.2 us
    dot_general x8, matrix products, outer_total(): jnp.einsum('cfk,cfn->kn', left, right, preferred_element_type=jnp.float32)  55.7 us
  transfers between devices with their start and end apart: 13, of which 6 were waited for; matrix products, arithmetic and copies ran while one was open for 33% of the time, Pallas kernels for 0%

commit v1 on v0

v1 whole, which is shorter than its diff:
```python
import functools
import math

import jax
import jax.numpy as jnp
from jax import lax
from jax.experimental import pallas as pl
from jax.experimental.pallas import tpu as pltpu
from jax.sharding import PartitionSpec as P

HEAD_DIM = 64
LAYERS = 2
EPSILON = 1e-05
AXES = ("clip", "seq")
LOG2_SCALE = HEAD_DIM ** (-0.5) * math.log2(math.e)
VMEM_BYTES = 56 * 1024 * 1024


class Grid:
    def __init__(self):
        clips, self.seq_size = lax.axis_size("clip"), lax.axis_size("seq")
        self.outer_size = clips // 4
        self.owners = clips * self.seq_size
        self.sizes = (self.outer_size, 2, 2, self.seq_size)
        self.strides = (4 * self.seq_size, 2 * self.seq_size, self.seq_size, 1)

    def digits(self):
        clip, seq = lax.axis_index("clip"), lax.axis_index("seq")
        return (clip // 4, (clip // 2) % 2, clip % 2, seq)

    def shift(self, array, axis, amount):
        size, stride = self.sizes[axis], self.strides[axis]
        pairs = []
        for place in range(self.owners):
            digit = (place // stride) % size
            pairs.append((place, place + ((digit + amount) % size - digit) * stride))
        return lax.ppermute(array, AXES, pairs)


OUTER, CROSS, CORE, SEQ = 0, 1, 2, 3


def place_kernel(grid, steps, splits, *refs):
    count = len(steps)
    pieces, outs, sem = refs[:count], refs[count : count + len(splits)], refs[-1]
    outer, cross, core, seq = grid.digits()
    copies = []
    for piece, step in zip(pieces, steps):
        for back in range(grid.outer_size):
            place = (lax.rem(outer + grid.outer_size - back, grid.outer_size)) * 2
            place = (place + lax.rem(cross + 2 - step[CROSS], 2)) * 2
            place = (place + lax.rem(core + 2 - step[CORE], 2)) * grid.seq_size
            place = place + lax.rem(seq + grid.seq_size - step[SEQ], grid.seq_size)
            for out, (start, stop) in zip(outs, splits):
                source = piece.at[back, :, pl.ds(start, stop - start)]
                copies.append((source, out.at[place]))
    for index, (source, target) in enumerate(copies):
        pltpu.make_async_copy(source, target, sem.at[index]).start()
    for index, (source, target) in enumerate(copies):
        pltpu.make_async_copy(source, target, sem.at[index]).wait()


def gather_rows(grid, shard, order, splits):
    rows, columns = shard.shape
    rounds = [shard] + [grid.shift(shard, OUTER, k) for k in range(1, grid.outer_size)]
    pieces = [((0, 0, 0, 0), jnp.stack(rounds))]
    for axis in order:
        more = []
        for amount in range(1, grid.sizes[axis]):
            for step, piece in pieces:
                moved = list(step)
                moved[axis] = amount
                more.append((tuple(moved), grid.shift(piece, axis, amount)))
        pieces = pieces + more
    outs = pl.pallas_call(
        functools.partial(place_kernel, grid, [step for step, _ in pieces], splits),
        out_shape=[
            jax.ShapeDtypeStruct((grid.owners, rows, stop - start), shard.dtype)
            for start, stop in splits
        ],
        in_specs=[pl.BlockSpec(memory_space=pl.ANY)] * len(pieces),
        out_specs=[pl.BlockSpec(memory_space=pl.ANY)] * len(splits),
        scratch_shapes=[pltpu.SemaphoreType.DMA((grid.owners * len(splits),))],
        cost_estimate=pl.CostEstimate(
            flops=0, transcendentals=0, bytes_accessed=4 * grid.owners * rows * columns
        ),
        name="place_rows",
    )(*[piece for _, piece in pieces])
    return [out.reshape(grid.owners * rows, out.shape[2]) for out in outs]


def scatter_rows(grid, total, order):
    columns = total.shape[1]
    rows = total.shape[0] // grid.owners
    digits = grid.digits()
    part = total.astype(jnp.bfloat16).reshape(grid.sizes + (rows, columns))
    for axis in tuple(order) + (OUTER,):
        size, digit = grid.sizes[axis], digits[axis]
        own = lax.dynamic_slice_in_dim(part, digit, 1, axis).astype(jnp.float32)
        for amount in range(1, size):
            sent = lax.dynamic_slice_in_dim(part, (digit + amount) % size, 1, axis)
            own = own + grid.shift(sent, axis, amount).astype(jnp.float32)
        part = own if axis == OUTER else own.astype(jnp.bfloat16)
    return part.reshape(rows, columns)


def head_of(array, head):
    lane = lax.broadcasted_iota(jnp.int32, array.shape, 1)
    inside = lane < HEAD_DIM if head == 0 else lane >= HEAD_DIM
    return jnp.where(inside, array, jnp.zeros_like(array))


def times_transposed(left, right):
    return lax.dot_general(
        left, right, (((1,), (1,)), ((), ())), preferred_element_type=jnp.float32
    )


def times(left, right):
    return lax.dot_general(
        left, right, (((1,), (0,)), ((), ())), preferred_element_type=jnp.float32
    )


def attend_kernel(q_ref, k_ref, v_ref, k_far_ref, v_far_ref, o_ref, log_ref):
    keys = (k_ref[...], k_far_ref[...])
    values = (v_ref[...].T, v_far_ref[...].T)
    query = q_ref[...]
    mixed, logs = [], []
    for head in range(2):
        rows = slice(head * HEAD_DIM, (head + 1) * HEAD_DIM)
        part = head_of(query, head)
        scores = [times_transposed(key, part) for key in keys]
        highest = functools.reduce(
            jnp.maximum, [jnp.max(score, axis=0, keepdims=True) for score in scores]
        )
        weights = [jnp.exp2((score - highest) * LOG2_SCALE) for score in scores]
        total = sum(jnp.sum(weight, axis=0, keepdims=True) for weight in weights)
        inverse = 1.0 / total
        probs = [(weight * inverse).astype(jnp.bfloat16) for weight in weights]
        mixed.append(sum(times(value[rows], prob) for value, prob in zip(values, probs)))
        logs.append(highest * LOG2_SCALE + jnp.log2(total))
    o_ref[...] = jnp.concatenate(mixed, axis=0).T.astype(o_ref.dtype)
    log_ref[0] = jnp.concatenate(logs, axis=0)


def attend_back_kernel(
    q_ref, k_ref, v_ref, k_far_ref, v_far_ref, log_ref, g_ref,
    dq_ref, d_ref, d_far_ref,
):
    width = q_ref.shape[1] * pl.num_programs(0)
    column = pl.multiple_of(pl.program_id(0) * 128, 128)
    second = pl.multiple_of(d_ref.shape[1] // 2 + pl.program_id(0) * 128, 128)
    keys = (k_ref[...], k_far_ref[...])
    keys_turned = [key.T for key in keys]
    values = (v_ref[...], v_far_ref[...])
    query, grad = q_ref[...], g_ref[...]
    scale = HEAD_DIM ** (-0.5)
    grad_query = []
    grad_keys, grad_values = [None, None], [None, None]
    for head in range(2):
        rows = slice(head * HEAD_DIM, (head + 1) * HEAD_DIM)
        part, grad_part = head_of(query, head), head_of(grad, head)
        log = log_ref[0, head : head + 1, :]
        probs = [
            jnp.exp2(times_transposed(key, part) * LOG2_SCALE - log) for key in keys
        ]
        pulls = [times_transposed(value, grad_part) for value in values]
        inner = sum(
            jnp.sum(prob * pull, axis=0, keepdims=True) for prob, pull in zip(probs, pulls)
        )
        scores = [
            (prob * (pull - inner)).astype(jnp.bfloat16) for prob, pull in zip(probs, pulls)
        ]
        grad_query.append(
            sum(times(key[rows], score) for key, score in zip(keys_turned, scores))
        )
        for side in range(2):
            more = times(scores[side], part)
            grad_keys[side] = more if head == 0 else grad_keys[side] + more
            more = times(probs[side].astype(jnp.bfloat16), grad_part)
            grad_values[side] = more if head == 0 else grad_values[side] + more
    dq_ref[...] = (jnp.concatenate(grad_query, axis=0).T * scale).astype(dq_ref.dtype)
    for side, out in enumerate((d_ref, d_far_ref)):
        out[:, pl.ds(column, 128)] = (grad_keys[side] * scale).astype(out.dtype)
        out[:, pl.ds(second, 128)] = grad_values[side].astype(out.dtype)


def block_specs(frames, far, blocks):
    return [
        pl.BlockSpec((frames, 128), lambda i: (0, i)),
        pl.BlockSpec((frames, 128), lambda i: (0, i)),
        pl.BlockSpec((frames, 128), lambda i: (0, i + blocks)),
        pl.BlockSpec((far, 128), lambda i: (0, i)),
        pl.BlockSpec((far, 128), lambda i: (0, i + blocks)),
    ]


def attend(query, pair, pair_far):
    frames, width = query.shape
    far, blocks = pair_far.shape[0], width // 128
    work = frames * (frames + far) * width
    return pl.pallas_call(
        attend_kernel,
        grid=(blocks,),
        in_specs=block_specs(frames, far, blocks),
        out_specs=[
            pl.BlockSpec((frames, 128), lambda i: (0, i)),
            pl.BlockSpec((1, 2, frames), lambda i: (i, 0, 0)),
        ],
        out_shape=[
            jax.ShapeDtypeStruct((frames, width), jnp.bfloat16),
            jax.ShapeDtypeStruct((blocks, 2, frames), jnp.float32),
        ],
        compiler_params=pltpu.CompilerParams(vmem_limit_bytes=VMEM_BYTES),
        cost_estimate=pl.CostEstimate(
            flops=16 * work, transcendentals=work // HEAD_DIM, bytes_accessed=8 * frames * width
        ),
        name="attend",
    )(query, pair, pair, pair_far, pair_far)


def attend_back(query, pair, pair_far, logs, grad):
    frames, width = query.shape
    far, blocks = pair_far.shape[0], width // 128
    work = frames * (frames + far) * width
    return pl.pallas_call(
        attend_back_kernel,
        grid=(blocks,),
        in_specs=block_specs(frames, far, blocks)
        + [
            pl.BlockSpec((1, 2, frames), lambda i: (i, 0, 0)),
            pl.BlockSpec((frames, 128), lambda i: (0, i)),
        ],
        out_specs=[
            pl.BlockSpec((frames, 128), lambda i: (0, i)),
            pl.BlockSpec((frames, 2 * width), lambda i: (0, 0)),
            pl.BlockSpec((far, 2 * width), lambda i: (0, 0)),
        ],
        out_shape=[
            jax.ShapeDtypeStruct((frames, width), jnp.bfloat16),
            jax.ShapeDtypeStruct((frames, 2 * width), jnp.bfloat16),
            jax.ShapeDtypeStruct((far, 2 * width), jnp.bfloat16),
        ],
        compiler_params=pltpu.CompilerParams(vmem_limit_bytes=VMEM_BYTES),
        cost_estimate=pl.CostEstimate(
            flops=40 * work, transcendentals=work // HEAD_DIM, bytes_accessed=16 * frames * width
        ),
        name="attend_back",
    )(query, pair, pair, pair_far, pair_far, logs, grad)


def normal_parts(rows):
    center = jnp.mean(rows, axis=-1, keepdims=True)
    spread = rows - center
    variance = jnp.mean(spread * spread, axis=-1, keepdims=True)
    rate = lax.rsqrt(variance + EPSILON)
    return spread * rate, rate


def normal_back(grad, rows, gain):
    unit, rate = normal_parts(rows)
    scaled = grad * gain
    pulled = rate * (
        scaled
        - jnp.mean(scaled, axis=-1, keepdims=True)
        - unit * jnp.mean(scaled * unit, axis=-1, keepdims=True)
    )
    return pulled, jnp.sum(grad * unit, axis=0), jnp.sum(grad, axis=0)


def gelu_exact(values):
    return jax.nn.gelu(values, approximate=False)


def outer_total(left, right):
    return lax.dot_general(
        left, right, (((0,), (0,)), ((), ())), preferred_element_type=jnp.float32
    )


def column_total(values):
    return jnp.sum(values.astype(jnp.float32), axis=0)


SMALL = (0, 1, 3, 5, 6, 7, 9, 11)


def gather_small(grid, params):
    shards = [params[slot].astype(jnp.bfloat16) for slot in SMALL]
    packed = jnp.concatenate([shard.reshape(1, -1) for shard in shards], axis=1)
    whole = lax.all_gather(packed, AXES, axis=0, tiled=True)
    found, offset = {}, 0
    for slot, shard in zip(SMALL, shards):
        amount = shard.size
        part = whole[:, offset : offset + amount].reshape((grid.owners,) + shard.shape)
        found[slot] = jnp.moveaxis(part, 0, 1).reshape(LAYERS, -1).astype(jnp.float32)
        offset += amount
    return found


def scatter_small(grid, totals):
    packed = jnp.concatenate(
        [
            jnp.moveaxis(total.reshape(LAYERS, grid.owners, -1), 1, 0).reshape(grid.owners, -1)
            for total in totals
        ],
        axis=1,
    )
    own = lax.psum_scatter(packed, AXES, scatter_dimension=0, tiled=True)
    pieces, offset = [], 0
    for total in totals:
        amount = total.size // grid.owners
        pieces.append(own[0, offset : offset + amount].reshape(LAYERS, -1))
        offset += amount
    return pieces


def layer_forward(grid, hidden, small, matrices):
    g1, s1, bm, bo, g2, s2, bu, bd = small
    w_query, w_pair, w_out, w_up, w_down = matrices
    width = hidden.shape[1]
    normed = (normal_parts(hidden)[0] * g1 + s1).astype(jnp.bfloat16)
    normed_far = jnp.concatenate(
        [grid.shift(normed, SEQ, amount) for amount in range(1, grid.seq_size)], axis=0
    )
    pair_bias = jnp.concatenate([jnp.zeros((width,), jnp.float32), bm[width:]])
    query = (times(normed, w_query) + bm[:width]).astype(jnp.bfloat16)
    pair = (times(normed, w_pair) + pair_bias).astype(jnp.bfloat16)
    pair_far = (times(normed_far, w_pair) + pair_bias).astype(jnp.bfloat16)
    attended, logs = attend(query, pair, pair_far)
    middle = hidden + (times(attended, w_out) + bo)
    normed_two = (normal_parts(middle)[0] * g2 + s2).astype(jnp.bfloat16)
    before = times(normed_two, w_up) + bu
    active = gelu_exact(before).astype(jnp.bfloat16)
    output = middle + (times(active, w_down) + bd)
    return output, (
        hidden, normed, normed_far, query, pair, pair_far, logs, attended, middle,
        normed_two, before, active,
    )


def layer_backward(grid, grad_hidden, kept, small, matrices):
    (
        hidden, normed, normed_far, query, pair, pair_far, logs, attended, middle,
        normed_two, before, active,
    ) = kept
    g1, s1, bm, bo, g2, s2, bu, bd = small
    w_query, w_pair, w_out, w_up, w_down = matrices
    frames, width = hidden.shape
    grad_down = grad_hidden.astype(jnp.bfloat16)
    down = scatter_rows(grid, outer_total(active, grad_down), (CORE, SEQ, CROSS))
    down_bias = column_total(grad_down)
    grad_active = times_transposed(grad_down, w_down)
    grad_before = jax.vjp(gelu_exact, before)[1](grad_active)[0].astype(jnp.bfloat16)
    up = scatter_rows(grid, outer_total(normed_two, grad_before), (CORE, CROSS, SEQ))
    up_bias = column_total(grad_before)
    grad_two = times_transposed(grad_before, w_up)
    pulled, gain_two, shift_two = normal_back(grad_two, middle, g2)
    grad_middle = grad_hidden + pulled
    grad_branch = grad_middle.astype(jnp.bfloat16)
    out = scatter_rows(grid, outer_total(attended, grad_branch), (CORE, SEQ, CROSS))
    out_bias = column_total(grad_branch)
    grad_attended = times_transposed(grad_branch, w_out).astype(jnp.bfloat16)
    grad_query, grad_pair, grad_far = attend_back(query, pair, pair_far, logs, grad_attended)
    far = times_transposed(grad_far, w_pair).astype(jnp.bfloat16)
    arrived = sum(
        grid.shift(
            far[(amount - 1) * frames : amount * frames], SEQ, grid.seq_size - amount
        ).astype(jnp.float32)
        for amount in range(1, grid.seq_size)
    )
    mixing = jnp.concatenate(
        [
            outer_total(normed, grad_query).astype(jnp.bfloat16),
            (outer_total(normed, grad_pair) + outer_total(normed_far, grad_far)).astype(
                jnp.bfloat16
            ),
        ],
        axis=1,
    )
    mixing = scatter_rows(grid, mixing, (CORE, CROSS, SEQ))
    mixing_bias = jnp.concatenate(
        [
            column_total(grad_query),
            column_total(grad_pair[:, width:]) + column_total(grad_far[:, width:]),
        ]
    )
    grad_normed = (
        times_transposed(grad_query, w_query) + times_transposed(grad_pair, w_pair) + arrived
    )
    pulled, gain_one, shift_one = normal_back(grad_normed, hidden, g1)
    return grad_middle + pulled, (
        gain_one, shift_one, mixing, mixing_bias, out, out_bias, gain_two, shift_two,
        up, up_bias, down, down_bias,
    )


def body(frames, cotangent, *params):
    grid = Grid()
    width = frames.shape[2]
    small = gather_small(grid, params)
    small = [[small[slot][layer] for slot in SMALL] for layer in range(LAYERS)]
    matrices = []
    for layer in range(LAYERS):
        mixing, out, up, down = [
            params[slot][layer].astype(jnp.bfloat16) for slot in (2, 4, 8, 10)
        ]
        first = gather_rows(
            grid,
            jnp.concatenate([mixing, out], axis=1),
            (CROSS, SEQ, CORE),
            ((0, width), (width, 3 * width), (3 * width, 4 * width)),
        )
        second = gather_rows(grid, up, (SEQ, CROSS, CORE), ((0, up.shape[1]),))
        third = gather_rows(grid, down, (CROSS, SEQ, CORE), ((0, width),))
        matrices.append(first + second + third)
    hidden = frames.reshape(-1, width)
    records = []
    for layer in range(LAYERS):
        hidden, kept = layer_forward(grid, hidden, small[layer], matrices[layer])
        records.append(kept)
    grad_hidden = cotangent.reshape(-1, width)
    shares = [None] * LAYERS
    for layer in reversed(range(LAYERS)):
        grad_hidden, shares[layer] = layer_backward(
            grid, grad_hidden, records[layer], small[layer], matrices[layer]
        )
    stacked = [jnp.stack([share[slot] for share in shares]) for slot in range(12)]
    for slot, piece in zip(SMALL, scatter_small(grid, [stacked[slot] for slot in SMALL])):
        stacked[slot] = piece
    return tuple([hidden.reshape(frames.shape), grad_hidden.reshape(frames.shape)] + stacked)


def solution(mesh):
    vector, matrix = P(None, AXES), P(None, AXES, None)
    whole = P("clip", "seq", None)
    params = tuple(matrix if slot in (2, 4, 8, 10) else vector for slot in range(12))
    return jax.shard_map(
        body,
        mesh=mesh,
        in_specs=(whole, whole) + params,
        out_specs=(whole, whole) + params,
        check_vma=False,
    )
```

time: 2220 us -> 1740 us (0.78)
  Pallas kernels: 0 us -> 942 us
  waiting for transfers between devices: 1120 us -> 288 us
  local copies, waits for them, and re-layouts: 699 us -> 74.2 us
  matrix products: 286 us -> 160 us
  starting transfers between devices: 0.75 us -> 126 us
  blocking collectives: 0 us -> 71.5 us
    pallas_call x0 -> x10, Pallas kernels: none -> 942 us  [the longest x6 867 us: gather_rows(): pl.pallas_call(functools.partial(place_kernel, grid, [step for step, _ in...]
    unnamed x14 -> x2, waiting for transfers between devices: 789 us -> 115 us
    unnamed x312 -> x329, local copies, waits for them, and re-layouts: 358 us -> 8.28 us
    all_gather x8 -> x0, waiting for transfers between devices: 332 us -> none  [the longest x2 226 us: fetch_forward(): lax.all_gather(pack_own(shards), ('clip', 'seq'), axis=0, tiled=True)]
    ppermute x0 -> x112, waiting for transfers between devices: none -> 173 us  [shift(): return lax.ppermute(array, AXES, pairs)]
    dot_general x108 -> x36, matrix products: 286 us -> 160 us  [the longest x12 73.3 us: times(): lax.dot_general(left, right, (((1,), (0,)), ((), ())), preferred_element_...]
    ppermute x0 -> x112, starting transfers between devices: none -> 126 us  [shift(): return lax.ppermute(array, AXES, pairs)]
    reshape x38 -> x16, local copies, waits for them, and re-layouts: 124 us -> 6.98 us  [the longest x8 6.29 us: scatter_small(): jnp.moveaxis(total.reshape(LAYERS, grid.owners, -1), 1, 0)]
  transfers between devices with their start and end apart: 13 -> 113, of which waited for: 6 -> 36; matrix products, arithmetic and copies ran while one was open for 33% -> 12% of each run, Pallas kernels for 0% -> 52%
where the time goes in v1:
time: 1740 us; the launch traced here: 1730 us
  Pallas kernels  942 us (54%)
  waiting for transfers between devices  288 us (17%)
  matrix products  160 us (9%)
  starting transfers between devices  126 us (7%)
  local copies, waits for them, and re-layouts  74.2 us (4%)
  blocking collectives  71.5 us (4%)
  other arithmetic  47.8 us (3%)
    pallas_call x6, Pallas kernels, gather_rows(): pl.pallas_call(functools.partial(place_kernel, grid, [step for step, _ in...  867 us
    ppermute x112, waiting for transfers between devices, shift(): return lax.ppermute(array, AXES, pairs)  173 us
    ppermute x112, starting transfers between devices, shift(): return lax.ppermute(array, AXES, pairs)  126 us
    unnamed x2, waiting for transfers between devices  115 us
    dot_general x12, matrix products, times(): lax.dot_general(left, right, (((1,), (0,)), ((), ())), preferred_element_...  73.3 us
    all_gather x1, blocking collectives, gather_small(): whole = lax.all_gather(packed, AXES, axis=0, tiled=True)  71.5 us
    pallas_call x2, Pallas kernels, attend_back(): pl.pallas_call(attend_back_kernel, grid=(blocks,), in_specs=block_specs(f...  45.9 us
    dot_general x12, matrix products, times_transposed(): lax.dot_general(left, right, (((1,), (1,)), ((), ())), preferred_element_...  44.9 us
  transfers between devices with their start and end apart: 113, of which 36 were waited for; matrix products, arithmetic and copies ran while one was open for 12% of the time, Pallas kernels for 52%

profile of v1, /device:TPU:0, one launch (start us, length us, event | category | flops | bytes accessed | tf_op | source)
XLA Modules:
  0.0 1726.4 jit_solution(18247695495062895062)
XLA Ops:
  10.2 4.0 collective-permute-start.32
  20.9 71.5 %all-gather = bf16[32,1,576]{2,1,0:T(2,128)(2,1)S(1)} all-gather(bf16[1,1,576]{2,1,0:T(2,128)(2,1)S(1)} %bitcast.338), channel_id=1, replica_groups=mesh['clip'=16,'seq'=2] {'clip','seq'}, dimensions={0}, use_global_device_ids=true | all-gather | bytes 38016 | tf_op jit(solution)/shard_map/all_gather | solution.py:292
  111.8 3.8 collective-permute-start.43
  116.2 6.2 collective-permute-done.12
  122.4 3.8 collective-permute-start.23
  126.5 6.3 collective-permute-start.4
  147.7 8.0 collective-permute-done.53
  181.3 144.9 %place_rows.6 = (bf16[32,24,768]{2,1,0:T(8,128)(2,1)}, bf16[32,24,1536]{2,1,0:T(8,128)(2,1)}, bf16[32,24,768]{2,1,0:T(8,128)(2,1)}) custom-call(bf16[4,24,3072]{2,1,0:T(8,128)(2,1)} %copy-done.23, bf16[4,24,3072]{2,1,0:T(8,128)(2,1)} %collective-permute-done.3.refs_1_, bf16[4,24,3072]{2,1,0:T(8,128)(2,1)} %collective-permute-done.4.refs_2_, ...), custom_call_target="tpu_custom_call" | custom-call | bytes 9437184 | tf_op jit(solution)/shard_map/place_rows/pallas_call | solution.py:75
  326.4 4.5 fusion.20.k_far_ref.v_far_ref
  336.6 10.4 collective-permute-done.24.refs_1_
  349.6 14.6 attend.2
  364.2 144.4 %place_rows.7 = bf16[32,24,3072]{2,1,0:T(8,128)(2,1)} custom-call(bf16[4,24,3072]{2,1,0:T(8,128)(2,1)} %copy-done.22, bf16[4,24,3072]{2,1,0:T(8,128)(2,1)} %collective-permute-done.14.refs_1_, bf16[4,24,3072]{2,1,0:T(8,128)(2,1)} %collective-permute-done.15.refs_2_, bf16[4,24,3072]{2,1,0:T(8,128)(2,1)} %collective-permute-done.16.refs_3_, ...), custom_call_target="tpu_custom_call" | custom-call | bytes 9437184 | tf_op jit(solution)/shard_map/place_rows/pallas_call | solution.py:75
  515.6 11.2 collective-permute-done.46.refs_2_
  532.2 21.5 %multiply_convert_fusion.1 = (bf16[512,3072]{1,0:T(8,128)(2,1)}, f32[512,3072]{1,0:T(8,128)}, f32[512,3072]{1,0:T(8,128)}) fusion(f32[3072]{0:T(1024)S(1)} %copy-done.110, bf16[768,3072]{1,0:T(8,128)(2,1)S(1)} %bitcast.269, f32[512,768]{1,0:T(8,128)S(1)} %get-tuple-element.140, f32[768]{0:T(1024)S(1)} %copy-done.116, f32[768]{0:T(1024)S(1)} %copy-done.102, ...), kind=kOutput, calls=%fused_computation.29 | convolution fusion | flops 2521694208 | bytes 22042624 | tf_op jit(solution)/shard_map/dot_general | solution.py:120
  553.7 144.4 %place_rows.8 = bf16[32,96,768]{2,1,0:T(8,128)(2,1)} custom-call(bf16[4,96,768]{2,1,0:T(8,128)(2,1)} %pad_maximum_fusion.4.refs_0_, bf16[4,96,768]{2,1,0:T(8,128)(2,1)} %collective-permute-done.24.refs_1_, bf16[4,96,768]{2,1,0:T(8,128)(2,1)} %collective-permute-done.25.refs_2_, bf16[4,96,768]{2,1,0:T(8,128)(2,1)} %collective-permute-done.26.refs_3_, ...), custom_call_target="tpu_custom_call" | custom-call | bytes 9437184 | tf_op jit(solution)/shard_map/place_rows/pallas_call | solution.py:75
  700.5 6.0 fusion.54
  707.2 6.9 collective-permute-done.47.refs_3_
  719.3 144.4 %place_rows.11 = bf16[32,96,768]{2,1,0:T(8,128)(2,1)} custom-call(bf16[4,96,768]{2,1,0:T(8,128)(2,1)} %pad_maximum_fusion.7.refs_0_, bf16[4,96,768]{2,1,0:T(8,128)(2,1)} %collective-permute-done.55.refs_1_, bf16[4,96,768]{2,1,0:T(8,128)(2,1)} %collective-permute-done.56.refs_2_, bf16[4,96,768]{2,1,0:T(8,128)(2,1)} %collective-permute-done.57.refs_3_, ...), custom_call_target="tpu_custom_call" | custom-call | bytes 9437184 | tf_op jit(solution)/shard_map/place_rows/pallas_call | solution.py:75
  863.6 144.4 %place_rows.10 = bf16[32,24,3072]{2,1,0:T(8,128)(2,1)} custom-call(bf16[4,24,3072]{2,1,0:T(8,128)(2,1)} %pad_maximum_fusion.6.refs_0_, bf16[4,24,3072]{2,1,0:T(8,128)(2,1)} %collective-permute-done.45.refs_1_, bf16[4,24,3072]{2,1,0:T(8,128)(2,1)} %collective-permute-done.46.refs_2_, bf16[4,24,3072]{2,1,0:T(8,128)(2,1)} %copy-done.41, ...), custom_call_target="tpu_custom_call" | custom-call | bytes 9437184 | tf_op jit(solution)/shard_map/place_rows/pallas_call | solution.py:75
  1008.1 145.0 %place_rows.9 = (bf16[32,24,768]{2,1,0:T(8,128)(2,1)}, bf16[32,24,1536]{2,1,0:T(8,128)(2,1)}, bf16[32,24,768]{2,1,0:T(8,128)(2,1)}) custom-call(bf16[4,24,3072]{2,1,0:T(8,128)(2,1)} %pad_maximum_fusion.5.refs_0_, bf16[4,24,3072]{2,1,0:T(8,128)(2,1)} %collective-permute-done.34.refs_1_, bf16[4,24,3072]{2,1,0:T(8,128)(2,1)} %collective-permute-done.35.refs_2_, ...), custom_call_target="tpu_custom_call" | custom-call | bytes 9437184 | tf_op jit(solution)/shard_map/place_rows/pallas_call | solution.py:75
  1161.2 14.5 attend.3
  1178.3 20.1 %multiply_convert_fusion = (bf16[512,3072]{1,0:T(8,128)(2,1)}, f32[512,3072]{1,0:T(8,128)}, f32[512,3072]{1,0:T(8,128)}) fusion(f32[3072]{0:T(1024)S(1)} %add.676, bf16[768,3072]{1,0:T(8,128)(2,1)} %bitcast.283, f32[512,768]{1,0:T(8,128)S(1)} %get-tuple-element.145, f32[768]{0:T(1024)S(1)} %add.673, f32[768]{0:T(1024)S(1)} %mul.306, ...), kind=kOutput, calls=%fused_computation.16 | convolution fusion | flops 2521694208 | bytes 22042624 | tf_op jit(solution)/shard_map/dot_general | solution.py:120
  1198.4 7.6 convert_reduce_fusion
  1209.0 5.0 convolution_convert_fusion.2
  1218.8 22.7 %attend_back.2 = (bf16[512,768]{1,0:T(8,128)(2,1)}, bf16[512,1536]{1,0:T(8,128)(2,1)}, bf16[512,1536]{1,0:T(8,128)(2,1)}) custom-call(bf16[512,768]{1,0:T(8,128)(2,1)} %add_convert_fusion.16.q_ref, bf16[512,1536]{1,0:T(8,128)(2,1)} %fusion.21.k_ref.v_ref, bf16[512,1536]{1,0:T(8,128)(2,1)} %fusion.21.k_ref.v_ref, ...), custom_call_target="tpu_custom_call" | custom-call | flops 16106127360 | bytes 6291456 | tf_op jit(solution)/shard_map/attend_back/pallas_call | solution.py:227
  1242.8 4.6 convolution_convert_fusion.11
  1249.6 3.6 fusion.62
  1253.2 4.4 fusion.56
  1257.6 3.8 add_bitcast_fusion.1
  1268.8 4.6 add_convert_fusion.5
  1290.2 7.7 convert_reduce_fusion.1
  1301.1 4.8 convolution_convert_fusion.3
  1305.9 4.5 convolution_convert_fusion.1
  1314.3 23.2 %attend_back.3 = (bf16[512,768]{1,0:T(8,128)(2,1)}, bf16[512,1536]{1,0:T(8,128)(2,1)}, bf16[512,1536]{1,0:T(8,128)(2,1)}) custom-call(bf16[512,768]{1,0:T(8,128)(2,1)} %add_convert_fusion.20.q_ref, bf16[512,1536]{1,0:T(8,128)(2,1)} %fusion.19.k_ref.v_ref, bf16[512,1536]{1,0:T(8,128)(2,1)} %fusion.19.k_ref.v_ref, ...), custom_call_target="tpu_custom_call" | custom-call | flops 16106127360 | bytes 6291456 | tf_op jit(solution)/shard_map/attend_back/pallas_call | solution.py:227
  1338.8 3.8 convolution_convert_fusion.10
  1355.2 4.6 add_convert_fusion.6
  1371.9 3.8 collective-permute-start.87
  1386.3 4.6 multiply_reduce_fusion.3
  1408.1 115.1 %all-reduce.5.cloned.1.call-done = f32[32,576]{1,0:T(8,128)} async-done(((f32[32,576]{1,0:T(8,128)}), f32[32,576]{1,0:T(8,128)}) %all-reduce.5.cloned.1.call-update) | async-done | bytes 73744
  1555.5 15.2 collective-permute-done.71
  1573.7 8.7 collective-permute-done.72
  1595.7 19.2 %collective-permute-done.65 = bf16[4,1,1,2,24,2304]{5,4,3,2,1,0:T(8,128)(2,1)S(1)} collective-permute-done((bf16[4,1,1,2,24,2304]{5,4,3,2,1,0:T(8,128)(2,1)S(1)}, bf16[4,1,1,2,24,2304]{5,4,3,2,1,0:T(8,128)(2,1)S(1)}, u32[]{:S(2)}, u32[]{:S(2)}) %collective-permute-start.65) | collective-permute-done | bytes 884768 | tf_op jit(solution)/shard_map/ppermute | solution.py:37
  1619.6 29.7 %collective-permute-done.66 = bf16[4,1,1,1,24,2304]{5,4,3,2,1,0:T(8,128)(2,1)S(1)} collective-permute-done((bf16[4,1,1,1,24,2304]{5,4,3,2,1,0:T(8,128)(2,1)S(1)}, bf16[4,1,1,1,24,2304]{5,4,3,2,1,0:T(8,128)(2,1)S(1)}, u32[]{:S(2)}, u32[]{:S(2)}) %collective-permute-start.66) | collective-permute-done | bytes 442400 | tf_op jit(solution)/shard_map/ppermute | solution.py:37
  1660.4 5.6 collective-permute-done.96
  1673.5 6.3 collective-permute-start.109
  1679.8 4.9 collective-permute-done.98
  1703.0 5.1 collective-permute-start.105
  1711.1 3.9 collective-permute-done.92
  (806 shorter events, 301.8 us)
Async XLA Ops:
  7.3 1515.9 %all-reduce.5.cloned.1.call-start = ((), (), s32[]{:S(2)}) async-start(), calls=%async_computation | async-start | bytes 163840
  10.2 93.1 %collective-permute-start.32 = (bf16[24,3072]{1,0:T(8,128)(2,1)}, bf16[24,3072]{1,0:T(8,128)(2,1)S(1)}, u32[]{:S(2)}, u32[]{:S(2)}) collective-permute-start(bf16[24,3072]{1,0:T(8,128)(2,1)} %get-tuple-element.116), channel_id=1, source_target_pairs={{0,16},{1,17},{2,18},{3,19},{4,20},{5,21},{6,22},{7,23},{8,24},{9,... | collective-permute-start | bytes 442376 | tf_op jit(solution)/shard_map/ppermute | solution.py:37
  14.2 92.3 %collective-permute-start.31 = (bf16[24,3072]{1,0:T(8,128)(2,1)}, bf16[24,3072]{1,0:T(8,128)(2,1)S(1)}, u32[]{:S(2)}, u32[]{:S(2)}) collective-permute-start(bf16[24,3072]{1,0:T(8,128)(2,1)} %get-tuple-element.116), channel_id=1, source_target_pairs={{0,8},{1,9},{2,10},{3,11},{4,12},{5,13},{6,14},{7,15},{8,16},{9,17... | collective-permute-start | bytes 442376 | tf_op jit(solution)/shard_map/ppermute | solution.py:37
  15.8 84.4 %collective-permute-start.1 = (bf16[24,3072]{1,0:T(8,128)(2,1)S(1)}, bf16[24,3072]{1,0:T(8,128)(2,1)S(1)}, u32[]{:S(2)}, u32[]{:S(2)}) collective-permute-start(bf16[24,3072]{1,0:T(8,128)(2,1)S(1)} %get-tuple-element.118), channel_id=1, source_target_pairs={{0,16},{1,17},{2,18},{3,19},{4,20},{5,21},{6,22},{7,23},{8,24},{9,... | collective-permute-start | bytes 442376 | tf_op jit(solution)/shard_map/ppermute | solution.py:37
  16.2 84.1 %collective-permute-start = (bf16[24,3072]{1,0:T(8,128)(2,1)S(1)}, bf16[24,3072]{1,0:T(8,128)(2,1)S(1)}, u32[]{:S(2)}, u32[]{:S(2)}) collective-permute-start(bf16[24,3072]{1,0:T(8,128)(2,1)S(1)} %get-tuple-element.118), channel_id=1, source_target_pairs={{0,8},{1,9},{2,10},{3,11},{4,12},{5,13},{6,14},{7,15},{8,16},{9,17... | collective-permute-start | bytes 442376 | tf_op jit(solution)/shard_map/ppermute | solution.py:37
  18.7 81.7 %collective-permute-start.2 = (bf16[24,3072]{1,0:T(8,128)(2,1)S(1)}, bf16[24,3072]{1,0:T(8,128)(2,1)S(1)}, u32[]{:S(2)}, u32[]{:S(2)}) collective-permute-start(bf16[24,3072]{1,0:T(8,128)(2,1)S(1)} %get-tuple-element.118), channel_id=1, source_target_pairs={{0,24},{1,25},{2,26},{3,27},{4,28},{5,29},{6,30},{7,31},{8,0},{9,1... | collective-permute-start | bytes 442376 | tf_op jit(solution)/shard_map/ppermute | solution.py:37
  102.4 30.4 %collective-permute-start.3 = (bf16[4,24,3072]{2,1,0:T(8,128)(2,1)S(1)}, bf16[4,24,3072]{2,1,0:T(8,128)(2,1)}, u32[]{:S(2)}, u32[]{:S(2)}) collective-permute-start(bf16[4,24,3072]{2,1,0:T(8,128)(2,1)S(1)} %pad_maximum_fusion.2.refs_0_), channel_id=1, source_target_pairs={{0,4},{1,5},{2,6},{3,7},{4,0},{5,1},{6,2},{7,3},{8,12},{9,13},{10,... | collective-permute-start | bytes 1769480 | tf_op jit(solution)/shard_map/ppermute | solution.py:37
  126.5 29.7 %collective-permute-start.4 = (bf16[4,24,3072]{2,1,0:T(8,128)(2,1)S(1)}, bf16[4,24,3072]{2,1,0:T(8,128)(2,1)}, u32[]{:S(2)}, u32[]{:S(2)}) collective-permute-start(bf16[4,24,3072]{2,1,0:T(8,128)(2,1)S(1)} %pad_maximum_fusion.2.refs_0_), channel_id=1, source_target_pairs={{0,1},{1,0},{2,3},{3,2},{4,5},{5,4},{6,7},{7,6},{8,9},{9,8},{10,11... | collective-permute-start | bytes 1769480 | tf_op jit(solution)/shard_map/ppermute | solution.py:37
  132.8 27.0 %collective-permute-start.5 = (bf16[4,24,3072]{2,1,0:T(8,128)(2,1)}, bf16[4,24,3072]{2,1,0:T(8,128)(2,1)}, u32[]{:S(2)}, u32[]{:S(2)}) collective-permute-start(bf16[4,24,3072]{2,1,0:T(8,128)(2,1)} %collective-permute-done.3.refs_1_), channel_id=1, source_target_pairs={{0,1},{1,0},{2,3},{3,2},{4,5},{5,4},{6,7},{7,6},{8,9},{9,8},{10,11... | collective-permute-start | bytes 1769480 | tf_op jit(solution)/shard_map/ppermute | solution.py:37
  140.0 32.9 %collective-permute-start.14 = (bf16[4,24,3072]{2,1,0:T(8,128)(2,1)S(1)}, bf16[4,24,3072]{2,1,0:T(8,128)(2,1)}, u32[]{:S(2)}, u32[]{:S(2)}) collective-permute-start(bf16[4,24,3072]{2,1,0:T(8,128)(2,1)S(1)} %pad_maximum_fusion.3.refs_0_), channel_id=1, source_target_pairs={{0,1},{1,0},{2,3},{3,2},{4,5},{5,4},{6,7},{7,6},{8,9},{9,8},{10,11... | collective-permute-start | bytes 1769480 | tf_op jit(solution)/shard_map/ppermute | solution.py:37
  155.7 21.8 %collective-permute-start.7 = (bf16[4,24,3072]{2,1,0:T(8,128)(2,1)}, bf16[4,24,3072]{2,1,0:T(8,128)(2,1)}, u32[]{:S(2)}, u32[]{:S(2)}) collective-permute-start(bf16[4,24,3072]{2,1,0:T(8,128)(2,1)} %collective-permute-done.3.refs_1_), channel_id=1, source_target_pairs={{0,2},{1,3},{2,0},{3,1},{4,6},{5,7},{6,4},{7,5},{8,10},{9,11},{10,... | collective-permute-start | bytes 1769480 | tf_op jit(solution)/shard_map/ppermute | solution.py:37
  172.9 153.4 %collective-permute-start.10 = (bf16[512,768]{1,0:T(8,128)(2,1)S(1)}, bf16[512,768]{1,0:T(8,128)(2,1)}, u32[]{:S(2)}, u32[]{:S(2)}) collective-permute-start(bf16[512,768]{1,0:T(8,128)(2,1)S(1)} %add_convert_fusion.19), channel_id=1, source_target_pairs={{0,1},{1,0},{2,3},{3,2},{4,5},{5,4},{6,7},{7,6},{8,9},{9,8},{10,11... | collective-permute-start | bytes 2359304 | tf_op jit(solution)/shard_map/ppermute | solution.py:37
  176.9 154.0 %collective-permute-start.58 = (bf16[4,96,768]{2,1,0:T(8,128)(2,1)}, bf16[4,96,768]{2,1,0:T(8,128)(2,1)S(1)}, u32[]{:S(2)}, u32[]{:S(2)}) collective-permute-start(bf16[4,96,768]{2,1,0:T(8,128)(2,1)} %pad_maximum_fusion.7.refs_0_), channel_id=1, source_target_pairs={{0,2},{1,3},{2,0},{3,1},{4,6},{5,7},{6,4},{7,5},{8,10},{9,11},{10,... | collective-permute-start | bytes 1769480 | tf_op jit(solution)/shard_map/ppermute | solution.py:37
  177.1 153.9 %collective-permute-start.56 = (bf16[4,96,768]{2,1,0:T(8,128)(2,1)}, bf16[4,96,768]{2,1,0:T(8,128)(2,1)}, u32[]{:S(2)}, u32[]{:S(2)}) collective-permute-start(bf16[4,96,768]{2,1,0:T(8,128)(2,1)} %pad_maximum_fusion.7.refs_0_), channel_id=1, source_target_pairs={{0,1},{1,0},{2,3},{3,2},{4,5},{5,4},{6,7},{7,6},{8,9},{9,8},{10,11... | collective-permute-start | bytes 1769480 | tf_op jit(solution)/shard_map/ppermute | solution.py:37
  177.4 154.1 %collective-permute-start.15 = (bf16[4,24,3072]{2,1,0:T(8,128)(2,1)S(1)}, bf16[4,24,3072]{2,1,0:T(8,128)(2,1)}, u32[]{:S(2)}, u32[]{:S(2)}) collective-permute-start(bf16[4,24,3072]{2,1,0:T(8,128)(2,1)S(1)} %pad_maximum_fusion.3.refs_0_), channel_id=1, source_target_pairs={{0,4},{1,5},{2,6},{3,7},{4,0},{5,1},{6,2},{7,3},{8,12},{9,13},{10,... | collective-permute-start | bytes 1769480 | tf_op jit(solution)/shard_map/ppermute | solution.py:37
  177.5 154.1 %collective-permute-start.16 = (bf16[4,24,3072]{2,1,0:T(8,128)(2,1)}, bf16[4,24,3072]{2,1,0:T(8,128)(2,1)}, u32[]{:S(2)}, u32[]{:S(2)}) collective-permute-start(bf16[4,24,3072]{2,1,0:T(8,128)(2,1)} %collective-permute-done.14.refs_1_), channel_id=1, source_target_pairs={{0,4},{1,5},{2,6},{3,7},{4,0},{5,1},{6,2},{7,3},{8,12},{9,13},{10,... | collective-permute-start | bytes 1769480 | tf_op jit(solution)/shard_map/ppermute | solution.py:37
  347.0 164.2 %collective-permute-start.55 = (bf16[4,96,768]{2,1,0:T(8,128)(2,1)}, bf16[4,96,768]{2,1,0:T(8,128)(2,1)}, u32[]{:S(2)}, u32[]{:S(2)}) collective-permute-start(bf16[4,96,768]{2,1,0:T(8,128)(2,1)} %pad_maximum_fusion.7.refs_0_), channel_id=1, source_target_pairs={{0,4},{1,5},{2,6},{3,7},{4,0},{5,1},{6,2},{7,3},{8,12},{9,13},{10,... | collective-permute-start | bytes 1769480 | tf_op jit(solution)/shard_map/ppermute | solution.py:37
  347.3 165.7 %collective-permute-start.27 = (bf16[4,96,768]{2,1,0:T(8,128)(2,1)}, bf16[4,96,768]{2,1,0:T(8,128)(2,1)}, u32[]{:S(2)}, u32[]{:S(2)}) collective-permute-start(bf16[4,96,768]{2,1,0:T(8,128)(2,1)} %pad_maximum_fusion.4.refs_0_), channel_id=1, source_target_pairs={{0,2},{1,3},{2,0},{3,1},{4,6},{5,7},{6,4},{7,5},{8,10},{9,11},{10,... | collective-permute-start | bytes 1769480 | tf_op jit(solution)/shard_map/ppermute | solution.py:37
  347.3 167.4 %collective-permute-start.25 = (bf16[4,96,768]{2,1,0:T(8,128)(2,1)}, bf16[4,96,768]{2,1,0:T(8,128)(2,1)}, u32[]{:S(2)}, u32[]{:S(2)}) collective-permute-start(bf16[4,96,768]{2,1,0:T(8,128)(2,1)} %pad_maximum_fusion.4.refs_0_), channel_id=1, source_target_pairs={{0,1},{1,0},{2,3},{3,2},{4,5},{5,4},{6,7},{7,6},{8,9},{9,8},{10,11... | collective-permute-start | bytes 1769480 | tf_op jit(solution)/shard_map/ppermute | solution.py:37
  349.1 165.6 %collective-permute-start.48 = (bf16[4,24,3072]{2,1,0:T(8,128)(2,1)}, bf16[4,24,3072]{2,1,0:T(8,128)(2,1)}, u32[]{:S(2)}, u32[]{:S(2)}) collective-permute-start(bf16[4,24,3072]{2,1,0:T(8,128)(2,1)} %pad_maximum_fusion.6.refs_0_), channel_id=1, source_target_pairs={{0,2},{1,3},{2,0},{3,1},{4,6},{5,7},{6,4},{7,5},{8,10},{9,11},{10,... | collective-permute-start | bytes 1769480 | tf_op jit(solution)/shard_map/ppermute | solution.py:37
  349.3 166.0 %collective-permute-start.26 = (bf16[4,96,768]{2,1,0:T(8,128)(2,1)}, bf16[4,96,768]{2,1,0:T(8,128)(2,1)}, u32[]{:S(2)}, u32[]{:S(2)}) collective-permute-start(bf16[4,96,768]{2,1,0:T(8,128)(2,1)} %collective-permute-done.24.refs_1_), channel_id=1, source_target_pairs={{0,1},{1,0},{2,3},{3,2},{4,5},{5,4},{6,7},{7,6},{8,9},{9,8},{10,11... | collective-permute-start | bytes 1769480 | tf_op jit(solution)/shard_map/ppermute | solution.py:37
  526.8 171.2 %collective-permute-start.35 = (bf16[4,24,3072]{2,1,0:T(8,128)(2,1)}, bf16[4,24,3072]{2,1,0:T(8,128)(2,1)}, u32[]{:S(2)}, u32[]{:S(2)}) collective-permute-start(bf16[4,24,3072]{2,1,0:T(8,128)(2,1)} %pad_maximum_fusion.5.refs_0_), channel_id=1, source_target_pairs={{0,1},{1,0},{2,3},{3,2},{4,5},{5,4},{6,7},{7,6},{8,9},{9,8},{10,11... | collective-permute-start | bytes 1769480 | tf_op jit(solution)/shard_map/ppermute | solution.py:37
  528.6 169.9 %collective-permute-start.34 = (bf16[4,24,3072]{2,1,0:T(8,128)(2,1)}, bf16[4,24,3072]{2,1,0:T(8,128)(2,1)}, u32[]{:S(2)}, u32[]{:S(2)}) collective-permute-start(bf16[4,24,3072]{2,1,0:T(8,128)(2,1)} %pad_maximum_fusion.5.refs_0_), channel_id=1, source_target_pairs={{0,4},{1,5},{2,6},{3,7},{4,0},{5,1},{6,2},{7,3},{8,12},{9,13},{10,... | collective-permute-start | bytes 1769480 | tf_op jit(solution)/shard_map/ppermute | solution.py:37
  530.3 168.9 %collective-permute-start.59 = (bf16[4,96,768]{2,1,0:T(8,128)(2,1)}, bf16[4,96,768]{2,1,0:T(8,128)(2,1)S(1)}, u32[]{:S(2)}, u32[]{:S(2)}) collective-permute-start(bf16[4,96,768]{2,1,0:T(8,128)(2,1)} %collective-permute-done.55.refs_1_), channel_id=1, source_target_pairs={{0,2},{1,3},{2,0},{3,1},{4,6},{5,7},{6,4},{7,5},{8,10},{9,11},{10,... | collective-permute-start | bytes 1769480 | tf_op jit(solution)/shard_map/ppermute | solution.py:37
  530.3 170.0 %collective-permute-start.57 = (bf16[4,96,768]{2,1,0:T(8,128)(2,1)}, bf16[4,96,768]{2,1,0:T(8,128)(2,1)}, u32[]{:S(2)}, u32[]{:S(2)}) collective-permute-start(bf16[4,96,768]{2,1,0:T(8,128)(2,1)} %collective-permute-done.55.refs_1_), channel_id=1, source_target_pairs={{0,1},{1,0},{2,3},{3,2},{4,5},{5,4},{6,7},{7,6},{8,9},{9,8},{10,11... | collective-permute-start | bytes 1769480 | tf_op jit(solution)/shard_map/ppermute | solution.py:37
  531.3 167.8 %collective-permute-start.60 = (bf16[4,96,768]{2,1,0:T(8,128)(2,1)}, bf16[4,96,768]{2,1,0:T(8,128)(2,1)S(1)}, u32[]{:S(2)}, u32[]{:S(2)}) collective-permute-start(bf16[4,96,768]{2,1,0:T(8,128)(2,1)} %collective-permute-done.56.refs_2_), channel_id=1, source_target_pairs={{0,2},{1,3},{2,0},{3,1},{4,6},{5,7},{6,4},{7,5},{8,10},{9,11},{10,... | collective-permute-start | bytes 1769480 | tf_op jit(solution)/shard_map/ppermute | solution.py:37
  706.6 301.4 %collective-permute-start.37 = (bf16[4,24,3072]{2,1,0:T(8,128)(2,1)}, bf16[4,24,3072]{2,1,0:T(8,128)(2,1)}, u32[]{:S(2)}, u32[]{:S(2)}) collective-permute-start(bf16[4,24,3072]{2,1,0:T(8,128)(2,1)} %pad_maximum_fusion.5.refs_0_), channel_id=1, source_target_pairs={{0,2},{1,3},{2,0},{3,1},{4,6},{5,7},{6,4},{7,5},{8,10},{9,11},{10,... | collective-permute-start | bytes 1769480 | tf_op jit(solution)/shard_map/ppermute | solution.py:37
  707.0 301.0 %collective-permute-start.38 = (bf16[4,24,3072]{2,1,0:T(8,128)(2,1)}, bf16[4,24,3072]{2,1,0:T(8,128)(2,1)}, u32[]{:S(2)}, u32[]{:S(2)}) collective-permute-start(bf16[4,24,3072]{2,1,0:T(8,128)(2,1)} %collective-permute-done.34.refs_1_), channel_id=1, source_target_pairs={{0,2},{1,3},{2,0},{3,1},{4,6},{5,7},{6,4},{7,5},{8,10},{9,11},{10,... | collective-permute-start | bytes 1769480 | tf_op jit(solution)/shard_map/ppermute | solution.py:37
  714.1 293.9 %collective-permute-start.39 = (bf16[4,24,3072]{2,1,0:T(8,128)(2,1)}, bf16[4,24,3072]{2,1,0:T(8,128)(2,1)}, u32[]{:S(2)}, u32[]{:S(2)}) collective-permute-start(bf16[4,24,3072]{2,1,0:T(8,128)(2,1)} %collective-permute-done.35.refs_2_), channel_id=1, source_target_pairs={{0,2},{1,3},{2,0},{3,1},{4,6},{5,7},{6,4},{7,5},{8,10},{9,11},{10,... | collective-permute-start | bytes 1769480 | tf_op jit(solution)/shard_map/ppermute | solution.py:37
  715.3 292.8 %collective-permute-start.40 = (bf16[4,24,3072]{2,1,0:T(8,128)(2,1)}, bf16[4,24,3072]{2,1,0:T(8,128)(2,1)}, u32[]{:S(2)}, u32[]{:S(2)}) collective-permute-start(bf16[4,24,3072]{2,1,0:T(8,128)(2,1)} %collective-permute-done.36.refs_3_), channel_id=1, source_target_pairs={{0,2},{1,3},{2,0},{3,1},{4,6},{5,7},{6,4},{7,5},{8,10},{9,11},{10,... | collective-permute-start | bytes 1769480 | tf_op jit(solution)/shard_map/ppermute | solution.py:37
  717.3 441.4 %collective-permute-start.41 = (bf16[512,768]{1,0:T(8,128)(2,1)S(1)}, bf16[512,768]{1,0:T(8,128)(2,1)S(1)}, u32[]{:S(2)}, u32[]{:S(2)}) collective-permute-start(bf16[512,768]{1,0:T(8,128)(2,1)S(1)} %add_convert_fusion.17), channel_id=1, source_target_pairs={{0,1},{1,0},{2,3},{3,2},{4,5},{5,4},{6,7},{7,6},{8,9},{9,8},{10,11... | collective-permute-start | bytes 2359304 | tf_op jit(solution)/shard_map/ppermute | solution.py:37
  1285.3 79.7 %collective-permute-start.83 = (bf16[4,2,1,1,24,768]{5,4,3,2,1,0:T(8,128)(2,1)}, bf16[4,2,1,1,24,768]{5,4,3,2,1,0:T(8,128)(2,1)S(1)}, u32[]{:S(2)}, u32[]{:S(2)}) collective-permute-start(bf16[4,2,1,1,24,768]{5,4,3,2,1,0:T(8,128)(2,1)} %constant_dynamic-slice_fusion.28), channel_id=1, source_target_pairs={{0,1},{1,0},{2,3},{3,2},{4,5},{5,4},{6,7},{7,6},{8,9},{9,8},{10,11... | collective-permute-start | bytes 884744 | tf_op jit(solution)/shard_map/ppermute | solution.py:37
  1352.4 29.9 %collective-permute-start.76 = (bf16[4,2,1,2,24,768]{5,4,3,2,1,0:T(8,128)(2,1)}, bf16[4,2,1,2,24,768]{5,4,3,2,1,0:T(8,128)(2,1)}, u32[]{:S(2)}, u32[]{:S(2)}) collective-permute-start(bf16[4,2,1,2,24,768]{5,4,3,2,1,0:T(8,128)(2,1)} %constant_dynamic-slice_fusion.35), channel_id=1, source_target_pairs={{0,2},{1,3},{2,0},{3,1},{4,6},{5,7},{6,4},{7,5},{8,10},{9,11},{10,... | collective-permute-start | bytes 1769480 | tf_op jit(solution)/shard_map/ppermute | solution.py:37
  1352.4 33.9 %collective-permute-start.63 = (bf16[512,768]{1,0:T(8,128)(2,1)}, bf16[512,768]{1,0:T(8,128)(2,1)}, u32[]{:S(2)}, u32[]{:S(2)}) collective-permute-start(bf16[512,768]{1,0:T(8,128)(2,1)} %convolution_convert_fusion.10), channel_id=1, source_target_pairs={{0,1},{1,0},{2,3},{3,2},{4,5},{5,4},{6,7},{7,6},{8,9},{9,8},{10,11... | collective-permute-start | bytes 2359304 | tf_op jit(solution)/shard_map/ppermute | solution.py:37
  1380.9 152.8 %collective-permute-start.70 = (bf16[4,2,1,2,24,2304]{5,4,3,2,1,0:T(8,128)(2,1)}, bf16[4,2,1,2,24,2304]{5,4,3,2,1,0:T(8,128)(2,1)}, u32[]{:S(2)}, u32[]{:S(2)}) collective-permute-start(bf16[4,2,1,2,24,2304]{5,4,3,2,1,0:T(8,128)(2,1)} %constant_dynamic-slice_fusion.41), channel_id=1, source_target_pairs={{0,2},{1,3},{2,0},{3,1},{4,6},{5,7},{6,4},{7,5},{8,10},{9,11},{10,... | collective-permute-start | bytes 5308424 | tf_op jit(solution)/shard_map/ppermute | solution.py:37
  1380.9 167.4 %collective-permute-start.94 = (bf16[4,2,1,2,24,3072]{5,4,3,2,1,0:T(8,128)(2,1)}, bf16[4,2,1,2,24,3072]{5,4,3,2,1,0:T(8,128)(2,1)}, u32[]{:S(2)}, u32[]{:S(2)}) collective-permute-start(bf16[4,2,1,2,24,3072]{5,4,3,2,1,0:T(8,128)(2,1)} %constant_dynamic-slice_fusion.17), channel_id=1, source_target_pairs={{0,2},{1,3},{2,0},{3,1},{4,6},{5,7},{6,4},{7,5},{8,10},{9,11},{10,... | collective-permute-start | bytes 7077896 | tf_op jit(solution)/shard_map/ppermute | solution.py:37
  1381.4 171.1 %collective-permute-start.106 = (bf16[4,2,1,2,96,768]{5,4,3,2,1,0:T(8,128)(2,1)}, bf16[4,2,1,2,96,768]{5,4,3,2,1,0:T(8,128)(2,1)}, u32[]{:S(2)}, u32[]{:S(2)}) collective-permute-start(bf16[4,2,1,2,96,768]{5,4,3,2,1,0:T(8,128)(2,1)} %constant_dynamic-slice_fusion.5), channel_id=1, source_target_pairs={{0,2},{1,3},{2,0},{3,1},{4,6},{5,7},{6,4},{7,5},{8,10},{9,11},{10,... | collective-permute-start | bytes 7077896 | tf_op jit(solution)/shard_map/ppermute | solution.py:37
  1385.2 145.6 %collective-permute-start.77 = (bf16[4,2,1,1,24,768]{5,4,3,2,1,0:T(8,128)(2,1)}, bf16[4,2,1,1,24,768]{5,4,3,2,1,0:T(8,128)(2,1)S(1)}, u32[]{:S(2)}, u32[]{:S(2)}) collective-permute-start(bf16[4,2,1,1,24,768]{5,4,3,2,1,0:T(8,128)(2,1)} %constant_dynamic-slice_fusion.34), channel_id=1, source_target_pairs={{0,1},{1,0},{2,3},{3,2},{4,5},{5,4},{6,7},{7,6},{8,9},{9,8},{10,11... | collective-permute-start | bytes 884744 | tf_op jit(solution)/shard_map/ppermute | solution.py:37
  1544.6 28.0 %collective-permute-start.64 = (bf16[4,2,1,2,24,2304]{5,4,3,2,1,0:T(8,128)(2,1)}, bf16[4,2,1,2,24,2304]{5,4,3,2,1,0:T(8,128)(2,1)S(1)}, u32[]{:S(2)}, u32[]{:S(2)}) collective-permute-start(bf16[4,2,1,2,24,2304]{5,4,3,2,1,0:T(8,128)(2,1)} %constant_dynamic-slice_fusion.47), channel_id=1, source_target_pairs={{0,2},{1,3},{2,0},{3,1},{4,6},{5,7},{6,4},{7,5},{8,10},{9,11},{10,... | collective-permute-start | bytes 5308424 | tf_op jit(solution)/shard_map/ppermute | solution.py:37
  1546.0 37.7 %collective-permute-start.88 = (bf16[4,2,1,2,24,3072]{5,4,3,2,1,0:T(8,128)(2,1)S(1)}, bf16[4,2,1,2,24,3072]{5,4,3,2,1,0:T(8,128)(2,1)S(1)}, u32[]{:S(2)}, u32[]{:S(2)}) collective-permute-start(bf16[4,2,1,2,24,3072]{5,4,3,2,1,0:T(8,128)(2,1)S(1)} %copy-done.24), channel_id=1, source_target_pairs={{0,2},{1,3},{2,0},{3,1},{4,6},{5,7},{6,4},{7,5},{8,10},{9,11},{10,... | collective-permute-start | bytes 7077896 | tf_op jit(solution)/shard_map/ppermute | solution.py:37
  1547.5 40.2 %collective-permute-start.100 = (bf16[4,2,1,2,96,768]{5,4,3,2,1,0:T(8,128)(2,1)S(1)}, bf16[4,2,1,2,96,768]{5,4,3,2,1,0:T(8,128)(2,1)S(1)}, u32[]{:S(2)}, u32[]{:S(2)}) collective-permute-start(bf16[4,2,1,2,96,768]{5,4,3,2,1,0:T(8,128)(2,1)S(1)} %copy-done.25), channel_id=1, source_target_pairs={{0,2},{1,3},{2,0},{3,1},{4,6},{5,7},{6,4},{7,5},{8,10},{9,11},{10,... | collective-permute-start | bytes 7077896 | tf_op jit(solution)/shard_map/ppermute | solution.py:37
  1548.3 22.4 %collective-permute-start.71 = (bf16[4,1,1,2,24,2304]{5,4,3,2,1,0:T(8,128)(2,1)S(1)}, bf16[4,1,1,2,24,2304]{5,4,3,2,1,0:T(8,128)(2,1)S(1)}, u32[]{:S(2)}, u32[]{:S(2)}) collective-permute-start(bf16[4,1,1,2,24,2304]{5,4,3,2,1,0:T(8,128)(2,1)S(1)} %constant_dynamic-slice_fusion.40), channel_id=1, source_target_pairs={{0,4},{1,5},{2,6},{3,7},{4,0},{5,1},{6,2},{7,3},{8,12},{9,13},{10,... | collective-permute-start | bytes 2654216 | tf_op jit(solution)/shard_map/ppermute | solution.py:37
  1552.4 64.3 %collective-permute-start.95 = (bf16[4,1,1,2,24,3072]{5,4,3,2,1,0:T(8,128)(2,1)S(1)}, bf16[4,1,1,2,24,3072]{5,4,3,2,1,0:T(8,128)(2,1)S(1)}, u32[]{:S(2)}, u32[]{:S(2)}) collective-permute-start(bf16[4,1,1,2,24,3072]{5,4,3,2,1,0:T(8,128)(2,1)S(1)} %constant_dynamic-slice_fusion.16), channel_id=1, source_target_pairs={{0,4},{1,5},{2,6},{3,7},{4,0},{5,1},{6,2},{7,3},{8,12},{9,13},{10,... | collective-permute-start | bytes 3538952 | tf_op jit(solution)/shard_map/ppermute | solution.py:37
  1573.1 41.8 %collective-permute-start.65 = (bf16[4,1,1,2,24,2304]{5,4,3,2,1,0:T(8,128)(2,1)S(1)}, bf16[4,1,1,2,24,2304]{5,4,3,2,1,0:T(8,128)(2,1)S(1)}, u32[]{:S(2)}, u32[]{:S(2)}) collective-permute-start(bf16[4,1,1,2,24,2304]{5,4,3,2,1,0:T(8,128)(2,1)S(1)} %constant_dynamic-slice_fusion.46), channel_id=1, source_target_pairs={{0,4},{1,5},{2,6},{3,7},{4,0},{5,1},{6,2},{7,3},{8,12},{9,13},{10,... | collective-permute-start | bytes 2654216 | tf_op jit(solution)/shard_map/ppermute | solution.py:37
  1590.4 28.9 %collective-permute-start.107 = (bf16[4,2,1,1,96,768]{5,4,3,2,1,0:T(8,128)(2,1)S(1)}, bf16[4,2,1,1,96,768]{5,4,3,2,1,0:T(8,128)(2,1)S(1)}, u32[]{:S(2)}, u32[]{:S(2)}) collective-permute-start(bf16[4,2,1,1,96,768]{5,4,3,2,1,0:T(8,128)(2,1)S(1)} %constant_dynamic-slice_fusion.4), channel_id=1, source_target_pairs={{0,1},{1,0},{2,3},{3,2},{4,5},{5,4},{6,7},{7,6},{8,9},{9,8},{10,11... | collective-permute-start | bytes 3538952 | tf_op jit(solution)/shard_map/ppermute | solution.py:37
  1591.9 92.9 %collective-permute-start.89 = (bf16[4,1,1,2,24,3072]{5,4,3,2,1,0:T(8,128)(2,1)S(1)}, bf16[4,1,1,2,24,3072]{5,4,3,2,1,0:T(8,128)(2,1)S(1)}, u32[]{:S(2)}, u32[]{:S(2)}) collective-permute-start(bf16[4,1,1,2,24,3072]{5,4,3,2,1,0:T(8,128)(2,1)S(1)} %constant_dynamic-slice_fusion.22), channel_id=1, source_target_pairs={{0,4},{1,5},{2,6},{3,7},{4,0},{5,1},{6,2},{7,3},{8,12},{9,13},{10,... | collective-permute-start | bytes 3538952 | tf_op jit(solution)/shard_map/ppermute | solution.py:37
  1594.2 96.6 %collective-permute-start.101 = (bf16[4,2,1,1,96,768]{5,4,3,2,1,0:T(8,128)(2,1)S(1)}, bf16[4,2,1,1,96,768]{5,4,3,2,1,0:T(8,128)(2,1)S(1)}, u32[]{:S(2)}, u32[]{:S(2)}) collective-permute-start(bf16[4,2,1,1,96,768]{5,4,3,2,1,0:T(8,128)(2,1)S(1)} %constant_dynamic-slice_fusion.10), channel_id=1, source_target_pairs={{0,1},{1,0},{2,3},{3,2},{4,5},{5,4},{6,7},{7,6},{8,9},{9,8},{10,11... | collective-permute-start | bytes 3538952 | tf_op jit(solution)/shard_map/ppermute | solution.py:37
  1615.2 34.1 %collective-permute-start.66 = (bf16[4,1,1,1,24,2304]{5,4,3,2,1,0:T(8,128)(2,1)S(1)}, bf16[4,1,1,1,24,2304]{5,4,3,2,1,0:T(8,128)(2,1)S(1)}, u32[]{:S(2)}, u32[]{:S(2)}) collective-permute-start(bf16[4,1,1,1,24,2304]{5,4,3,2,1,0:T(8,128)(2,1)S(1)} %constant_dynamic-slice_fusion.45), channel_id=1, source_target_pairs={{0,1},{1,0},{2,3},{3,2},{4,5},{5,4},{6,7},{7,6},{8,9},{9,8},{10,11... | collective-permute-start | bytes 1327112 | tf_op jit(solution)/shard_map/ppermute | solution.py:37
  (229 other events, 4284.2 us)
Sparse Core Ops, SparseCore 0:
  1403.8 119.3 all-reduce.4

commit v2 on v1

v2 whole, which is shorter than its diff:
```python
import functools
import math

import jax
import jax.numpy as jnp
from jax import lax
from jax.experimental import pallas as pl
from jax.experimental.pallas import tpu as pltpu
from jax.sharding import PartitionSpec as P

HEAD_DIM = 64
LAYERS = 2
EPSILON = 1e-05
AXES = ("clip", "seq")
LOG2_SCALE = HEAD_DIM ** (-0.5) * math.log2(math.e)
VMEM_BYTES = 56 * 1024 * 1024
QUICK = pl.CostEstimate(flops=1000, transcendentals=0, bytes_accessed=1000)


class Grid:
    def __init__(self):
        clips, self.seq_size = lax.axis_size("clip"), lax.axis_size("seq")
        self.outer_size = clips // 4
        self.owners = clips * self.seq_size
        self.sizes = (self.outer_size, 2, 2, self.seq_size)
        self.strides = (4 * self.seq_size, 2 * self.seq_size, self.seq_size, 1)

    def digits(self):
        clip, seq = lax.axis_index("clip"), lax.axis_index("seq")
        return (clip // 4, (clip // 2) % 2, clip % 2, seq)

    def shift(self, array, axis, amount):
        size, stride = self.sizes[axis], self.strides[axis]
        pairs = []
        for place in range(self.owners):
            digit = (place // stride) % size
            pairs.append((place, place + ((digit + amount) % size - digit) * stride))
        return lax.ppermute(array, AXES, pairs)


OUTER, CROSS, CORE, SEQ = 0, 1, 2, 3


class Traffic:
    def __init__(self):
        self.active = []

    def add(self, stages):
        found = {}
        self.active.append([stages, next(stages), found])
        return found

    def tick(self, *state):
        flying = [entry[1] for entry in self.active]
        state, flying = lax.optimization_barrier((list(state), flying))
        going = []
        for (stages, _, found), arrays in zip(self.active, flying):
            try:
                going.append([stages, stages.send(arrays), found])
            except StopIteration as end:
                found["value"] = end.value
        self.active = going
        return state[0] if len(state) == 1 else state


def around(grid, array, axis):
    return [grid.shift(array, axis, amount) for amount in range(1, grid.sizes[axis])]


def join(pieces):
    return jnp.concatenate(pieces, axis=0)


def spread(steps, axis, size):
    return [
        step[:axis] + (amount,) + step[axis + 1 :] for amount in range(size) for step in steps
    ]


def place_kernel(grid, steps, splits, *refs):
    count = len(steps)
    pieces, outs, sem = refs[:count], refs[count : count + len(splits)], refs[-1]
    digits = grid.digits()
    copies = []
    for piece, found in zip(pieces, steps):
        for index, step in enumerate(found):
            place = 0
            for axis in range(4):
                size = grid.sizes[axis]
                place = place * size + lax.rem(digits[axis] + size - step[axis], size)
            for out, (start, stop, blocks) in zip(outs, splits):
                size = (stop - start) // blocks
                for block in range(blocks):
                    source = piece.at[index, :, pl.ds(start + block * size, size)]
                    target = out.at[place * blocks + block]
                    copies.append(pltpu.make_async_copy(source, target, sem.at[len(copies)]))
    for copy in copies:
        copy.start()
    for copy in copies:
        copy.wait()


def gather_rows(grid, shard, splits):
    rows, columns = shard.shape
    own = shard[None]
    own, *rounds = yield [own] + around(grid, own, OUTER)
    half = max(grid.outer_size // 2, 1)
    line = [(back, 0, 0, 0) for back in range(grid.outer_size)]
    groups = [[own] + rounds[: half - 1], rounds[half - 1 :]]
    steps = [line[:half], line[half:]]
    orders = [(CROSS, SEQ), (SEQ, CROSS)]
    pieces = [join(group) for group in groups]
    for turn in range(2):
        moved = [around(grid, piece, order[turn]) for piece, order in zip(pieces, orders)]
        pieces, moved = yield pieces, moved
        if turn == 0:
            pieces = [join([piece] + more) for piece, more in zip(pieces, moved)]
            steps = [
                spread(step, order[turn], grid.sizes[order[turn]])
                for step, order in zip(steps, orders)
            ]
    steps = [
        spread(step, order[1], grid.sizes[order[1]]) for step, order in zip(steps, orders)
    ]
    steps = [
        part[start : start + piece.shape[0]]
        for part, piece in zip(steps, pieces)
        for start in range(0, len(part), piece.shape[0])
    ]
    pieces = [part for piece, more in zip(pieces, moved) for part in [piece] + more]
    far = [grid.shift(piece, CORE, 1) for piece in pieces]
    pieces, far = yield pieces, far
    steps = steps + [[step[:CORE] + (1,) + step[CORE + 1 :] for step in found] for found in steps]
    outs = pl.pallas_call(
        functools.partial(place_kernel, grid, steps, splits),
        out_shape=[
            jax.ShapeDtypeStruct(
                (grid.owners * blocks, rows, (stop - start) // blocks), shard.dtype
            )
            for start, stop, blocks in splits
        ],
        in_specs=[pl.BlockSpec(memory_space=pl.ANY)] * len(steps),
        out_specs=[pl.BlockSpec(memory_space=pltpu.VMEM)] * len(splits),
        scratch_shapes=[pltpu.SemaphoreType.DMA((grid.owners * sum(split[2] for split in splits),))],
        compiler_params=pltpu.CompilerParams(vmem_limit_bytes=VMEM_BYTES),
        cost_estimate=QUICK,
        name="place_rows",
    )(*pieces, *far)
    return [out.reshape(-1, out.shape[2]) for out in outs]


def exchange(grid, part, axis):
    size, digit = grid.sizes[axis], grid.digits()[axis]
    kept = lax.dynamic_slice_in_dim(part, digit, 1, axis)
    arrived = [
        grid.shift(lax.dynamic_slice_in_dim(part, (digit + amount) % size, 1, axis), axis, amount)
        for amount in range(1, size)
    ]
    return kept, arrived


def total_of(kept, arrived):
    return sum((piece.astype(jnp.float32) for piece in arrived), kept.astype(jnp.float32))


def by_core(grid, total):
    rows, columns = total.shape
    shape = grid.sizes + (rows // grid.owners, columns)
    core = grid.digits()[CORE]
    total = total.astype(jnp.bfloat16).reshape(shape)
    return [lax.dynamic_slice_in_dim(total, place, 1, CORE) for place in (core, 1 - core)]


def scatter_rows(grid, kept, sent):
    kept, arrived = yield kept, [grid.shift(sent, CORE, 1)]
    part = total_of(kept, arrived).astype(jnp.bfloat16)
    half = grid.outer_size // 2
    parts = [part[:half], part[half:]]
    orders = [(CROSS, SEQ), (SEQ, CROSS)]
    for turn in range(2):
        flying = yield [exchange(grid, part, order[turn]) for part, order in zip(parts, orders)]
        parts = [total_of(*entry).astype(jnp.bfloat16) for entry in flying]
    kept, arrived = yield exchange(grid, join(parts), OUTER)
    return total_of(kept, arrived).reshape(kept.shape[-2:])


def split_columns(rows_first, blocks):
    owners, rows, columns = rows_first.shape
    turned = rows_first.reshape(owners, blocks, rows // blocks, columns)
    return jnp.moveaxis(turned, 1, 2).reshape(owners * (rows // blocks), blocks * columns)


def turned_product(left, right):
    return lax.dot_general(
        left, right, (((0,), (0,)), ((), ())), preferred_element_type=jnp.float32
    )


def feed_shares_kernel(
    grid, normed_ref, before_ref, mixed_ref, branch_ref, active_ref, down_ref, kept_ref, sent_ref
):
    step = pl.program_id(0)
    first = lax.axis_index("clip") % 2 == 0
    outer, _, _, seq = grid.sizes
    width = normed_ref.shape[1]
    ups = pl.num_programs(0) - 1 - outer
    rows = width // grid.owners

    def store(total, low, column):
        for ref, here in ((kept_ref, True), (sent_ref, False)):
            part = jnp.where(first == here, total[:, :, 0], total[:, :, 1])
            part = part.reshape(-1, width).astype(ref.dtype)
            ref[pl.ds(low, part.shape[0]), pl.ds(column, width)] = part

    def by_owner(total):
        return total.reshape(outer, 2, 2, seq * rows, width)

    @pl.when(step < ups)
    def _():
        column = pl.multiple_of(step * width, 128)
        store(by_owner(turned_product(normed_ref[...], before_ref[...])), 0, column)

    @pl.when(step == ups)
    def _():
        total = turned_product(mixed_ref[...], branch_ref[...])
        store(by_owner(total), 0, pl.multiple_of(step * width, 128))

    @pl.when(step > ups)
    def _():
        total = turned_product(active_ref[...], down_ref[...])
        blocks = total.shape[0] // (4 * seq * rows)
        total = total.reshape(1, 2, 2, seq, blocks, rows, width)
        line = pl.multiple_of((step - ups - 1) * (2 * seq * rows), 2 * seq * rows)
        for block in range(blocks):
            store(
                total[:, :, :, :, block].reshape(1, 2, 2, seq * rows, width),
                line,
                pl.multiple_of((ups + 1 + block) * width, 128),
            )


def feed_shares(grid, normed, before, mixed, branch, active, down):
    frames, width = normed.shape
    units = before.shape[1]
    blocks, rows = units // width, width // grid.owners
    columns = 2 * units + width
    if rows % 8 or grid.outer_size != blocks:
        up = outer_total(normed, before)
        out = outer_total(mixed, branch)
        low = split_columns(outer_total(active, down).reshape(grid.owners, -1, width), blocks)
        return by_core(grid, jnp.concatenate([up, out, low], axis=1))
    whole = pl.BlockSpec((frames, width), lambda i: (0, 0))
    half = pl.BlockSpec((width // 2, columns), lambda i: (0, 0))
    pair = pl.pallas_call(
        functools.partial(feed_shares_kernel, grid),
        grid=(2 * blocks + 1,),
        in_specs=[
            whole,
            pl.BlockSpec((frames, width), lambda i: (0, jnp.minimum(i, blocks - 1))),
            whole,
            whole,
            pl.BlockSpec((frames, width), lambda i: (0, jnp.maximum(i - blocks - 1, 0))),
            whole,
        ],
        out_specs=[half, half],
        out_shape=[jax.ShapeDtypeStruct((width // 2, columns), jnp.bfloat16)] * 2,
        compiler_params=pltpu.CompilerParams(vmem_limit_bytes=VMEM_BYTES),
        cost_estimate=QUICK,
        name="feed_shares",
    )(normed, before, mixed, branch, active, down)
    shape = (grid.outer_size, 2, 1, grid.seq_size, rows, columns)
    return [part.reshape(shape) for part in pair]


def mixing_shares_kernel(grid, near_ref, far_ref, query_ref, pair_ref, pair_far_ref, *outs):
    step = pl.program_id(0)
    first = lax.axis_index("clip") % 2 == 0
    outer, _, _, seq = grid.sizes
    width = near_ref.shape[1]
    rows = width // grid.owners

    def store(total):
        total = total.reshape(outer, 2, 2, seq * rows, width)
        for ref, here in zip(outs, (True, False)):
            part = jnp.where(first == here, total[:, :, 0], total[:, :, 1])
            ref[...] = part.reshape(-1, width).astype(ref.dtype)

    @pl.when(step == 0)
    def _():
        store(turned_product(near_ref[...], query_ref[...]))

    @pl.when(step > 0)
    def _():
        store(
            turned_product(near_ref[...], pair_ref[...])
            + turned_product(far_ref[...], pair_far_ref[...])
        )


def mixing_shares(grid, near, far, query, pair, pair_far):
    frames, width = near.shape
    rows = width // grid.owners
    if rows % 8:
        total = jnp.concatenate(
            [
                outer_total(near, query),
                outer_total(near, pair) + outer_total(far, pair_far),
            ],
            axis=1,
        )
        return by_core(grid, total)
    near_spec = pl.BlockSpec((frames, width), lambda i: (0, 0))
    half = pl.BlockSpec((width // 2, width), lambda i: (0, i))
    parts = pl.pallas_call(
        functools.partial(mixing_shares_kernel, grid),
        grid=(3,),
        in_specs=[
            near_spec,
            pl.BlockSpec(far.shape, lambda i: (0, 0)),
            near_spec,
            pl.BlockSpec((frames, width), lambda i: (0, jnp.maximum(i - 1, 0))),
            pl.BlockSpec((far.shape[0], width), lambda i: (0, jnp.maximum(i - 1, 0))),
        ],
        out_specs=[half, half],
        out_shape=[jax.ShapeDtypeStruct((width // 2, 3 * width), jnp.bfloat16)] * 2,
        compiler_params=pltpu.CompilerParams(vmem_limit_bytes=VMEM_BYTES),
        cost_estimate=QUICK,
        name="mixing_shares",
    )(near, far, query, pair, pair_far)
    shape = (grid.outer_size, 2, 1, grid.seq_size, rows, 3 * width)
    return [part.reshape(shape) for part in parts]


def head_of(array, head):
    lane = lax.broadcasted_iota(jnp.int32, array.shape, 1)
    inside = lane < HEAD_DIM if head == 0 else lane >= HEAD_DIM
    return jnp.where(inside, array, jnp.zeros_like(array))


def times_transposed(left, right):
    return lax.dot_general(
        left, right, (((1,), (1,)), ((), ())), preferred_element_type=jnp.float32
    )


def times(left, right):
    return lax.dot_general(
        left, right, (((1,), (0,)), ((), ())), preferred_element_type=jnp.float32
    )


def attend_kernel(q_ref, k_ref, v_ref, k_far_ref, v_far_ref, o_ref, log_ref):
    keys = (k_ref[...], k_far_ref[...])
    values = (v_ref[...].T, v_far_ref[...].T)
    query = q_ref[...]
    mixed, logs = [], []
    for head in range(2):
        rows = slice(head * HEAD_DIM, (head + 1) * HEAD_DIM)
        part = head_of(query, head)
        scores = [times_transposed(key, part) for key in keys]
        highest = functools.reduce(
            jnp.maximum, [jnp.max(score, axis=0, keepdims=True) for score in scores]
        )
        weights = [jnp.exp2((score - highest) * LOG2_SCALE) for score in scores]
        total = sum(jnp.sum(weight, axis=0, keepdims=True) for weight in weights)
        inverse = 1.0 / total
        probs = [(weight * inverse).astype(jnp.bfloat16) for weight in weights]
        mixed.append(sum(times(value[rows], prob) for value, prob in zip(values, probs)))
        logs.append(highest * LOG2_SCALE + jnp.log2(total))
    o_ref[...] = jnp.concatenate(mixed, axis=0).T.astype(o_ref.dtype)
    log_ref[0] = jnp.concatenate(logs, axis=0)


def attend_back_kernel(
    q_ref, k_ref, v_ref, k_far_ref, v_far_ref, log_ref, g_ref,
    dq_ref, d_ref, d_far_ref,
):
    width = q_ref.shape[1] * pl.num_programs(0)
    column = pl.multiple_of(pl.program_id(0) * 128, 128)
    second = pl.multiple_of(d_ref.shape[1] // 2 + pl.program_id(0) * 128, 128)
    keys = (k_ref[...], k_far_ref[...])
    keys_turned = [key.T for key in keys]
    values = (v_ref[...], v_far_ref[...])
    query, grad = q_ref[...], g_ref[...]
    scale = HEAD_DIM ** (-0.5)
    grad_query = []
    grad_keys, grad_values = [None, None], [None, None]
    for head in range(2):
        rows = slice(head * HEAD_DIM, (head + 1) * HEAD_DIM)
        part, grad_part = head_of(query, head), head_of(grad, head)
        log = log_ref[0, head : head + 1, :]
        probs = [
            jnp.exp2(times_transposed(key, part) * LOG2_SCALE - log) for key in keys
        ]
        pulls = [times_transposed(value, grad_part) for value in values]
        inner = sum(
            jnp.sum(prob * pull, axis=0, keepdims=True) for prob, pull in zip(probs, pulls)
        )
        scores = [
            (prob * (pull - inner)).astype(jnp.bfloat16) for prob, pull in zip(probs, pulls)
        ]
        grad_query.append(
            sum(times(key[rows], score) for key, score in zip(keys_turned, scores))
        )
        for side in range(2):
            more = times(scores[side], part)
            grad_keys[side] = more if head == 0 else grad_keys[side] + more
            more = times(probs[side].astype(jnp.bfloat16), grad_part)
            grad_values[side] = more if head == 0 else grad_values[side] + more
    dq_ref[...] = (jnp.concatenate(grad_query, axis=0).T * scale).astype(dq_ref.dtype)
    for side, out in enumerate((d_ref, d_far_ref)):
        out[:, pl.ds(column, 128)] = (grad_keys[side] * scale).astype(out.dtype)
        out[:, pl.ds(second, 128)] = grad_values[side].astype(out.dtype)


def block_specs(frames, far, blocks):
    return [
        pl.BlockSpec((frames, 128), lambda i: (0, i)),
        pl.BlockSpec((frames, 128), lambda i: (0, i)),
        pl.BlockSpec((frames, 128), lambda i: (0, i + blocks)),
        pl.BlockSpec((far, 128), lambda i: (0, i)),
        pl.BlockSpec((far, 128), lambda i: (0, i + blocks)),
    ]


def attend(query, pair, pair_far):
    frames, width = query.shape
    far, blocks = pair_far.shape[0], width // 128
    return pl.pallas_call(
        attend_kernel,
        grid=(blocks,),
        in_specs=block_specs(frames, far, blocks),
        out_specs=[
            pl.BlockSpec((frames, 128), lambda i: (0, i)),
            pl.BlockSpec((1, 2, frames), lambda i: (i, 0, 0)),
        ],
        out_shape=[
            jax.ShapeDtypeStruct((frames, width), jnp.bfloat16),
            jax.ShapeDtypeStruct((blocks, 2, frames), jnp.float32),
        ],
        compiler_params=pltpu.CompilerParams(vmem_limit_bytes=VMEM_BYTES),
        cost_estimate=QUICK,
        name="attend",
    )(query, pair, pair, pair_far, pair_far)


def attend_back(query, pair, pair_far, logs, grad):
    frames, width = query.shape
    far, blocks = pair_far.shape[0], width // 128
    return pl.pallas_call(
        attend_back_kernel,
        grid=(blocks,),
        in_specs=block_specs(frames, far, blocks)
        + [
            pl.BlockSpec((1, 2, frames), lambda i: (i, 0, 0)),
            pl.BlockSpec((frames, 128), lambda i: (0, i)),
        ],
        out_specs=[
            pl.BlockSpec((frames, 128), lambda i: (0, i)),
            pl.BlockSpec((frames, 2 * width), lambda i: (0, 0)),
            pl.BlockSpec((far, 2 * width), lambda i: (0, 0)),
        ],
        out_shape=[
            jax.ShapeDtypeStruct((frames, width), jnp.bfloat16),
            jax.ShapeDtypeStruct((frames, 2 * width), jnp.bfloat16),
            jax.ShapeDtypeStruct((far, 2 * width), jnp.bfloat16),
        ],
        compiler_params=pltpu.CompilerParams(vmem_limit_bytes=VMEM_BYTES),
        cost_estimate=QUICK,
        name="attend_back",
    )(query, pair, pair, pair_far, pair_far, logs, grad)


def normal_parts(rows):
    center = jnp.mean(rows, axis=-1, keepdims=True)
    spread = rows - center
    variance = jnp.mean(spread * spread, axis=-1, keepdims=True)
    rate = lax.rsqrt(variance + EPSILON)
    return spread * rate, rate


def normal_back(grad, rows, gain):
    unit, rate = normal_parts(rows)
    scaled = grad * gain
    pulled = rate * (
        scaled
        - jnp.mean(scaled, axis=-1, keepdims=True)
        - unit * jnp.mean(scaled * unit, axis=-1, keepdims=True)
    )
    return pulled, jnp.sum(grad * unit, axis=0), jnp.sum(grad, axis=0)


def raise_kernel(left_ref, right_ref, bias_ref, active_ref, slope_ref):
    values = times(left_ref[...], right_ref[...]) + bias_ref[...]
    below = 0.5 + 0.5 * lax.erf(values * math.sqrt(0.5))
    density = jnp.exp(-0.5 * values * values) * (1.0 / math.sqrt(2.0 * math.pi))
    active_ref[...] = (values * below).astype(active_ref.dtype)
    slope_ref[...] = below + values * density


def raise_width(left, right, bias):
    frames, width = left.shape
    units = right.shape[1]
    tile = 512
    return pl.pallas_call(
        raise_kernel,
        grid=(units // tile,),
        in_specs=[
            pl.BlockSpec((frames, width), lambda i: (0, 0)),
            pl.BlockSpec((width, tile), lambda i: (0, i)),
            pl.BlockSpec((1, tile), lambda i: (0, i)),
        ],
        out_specs=[pl.BlockSpec((frames, tile), lambda i: (0, i))] * 2,
        out_shape=[
            jax.ShapeDtypeStruct((frames, units), jnp.bfloat16),
            jax.ShapeDtypeStruct((frames, units), jnp.float32),
        ],
        compiler_params=pltpu.CompilerParams(vmem_limit_bytes=VMEM_BYTES),
        cost_estimate=QUICK,
        name="raise_width",
    )(left, right, bias.reshape(1, -1))


def outer_total(left, right):
    return lax.dot_general(
        left, right, (((0,), (0,)), ((), ())), preferred_element_type=jnp.float32
    )


def column_total(values):
    return jnp.sum(values.astype(jnp.float32), axis=0)


SMALL = (0, 1, 3, 5, 6, 7, 9, 11)


def everywhere(grid, array):
    for axis in (OUTER, CROSS, SEQ, CORE):
        array = sum(around(grid, array, axis), array)
    return array


def gather_small(grid, params):
    place = lax.axis_index("clip") * grid.seq_size + lax.axis_index("seq")
    lanes = []
    for slot in SMALL:
        shard = params[slot].astype(jnp.bfloat16)
        empty = jnp.zeros((LAYERS, shard.shape[1] * grid.owners), jnp.bfloat16)
        lanes.append(lax.dynamic_update_slice_in_dim(empty, shard, place * shard.shape[1], 1))
    whole = everywhere(grid, jnp.concatenate(lanes, axis=1)).astype(jnp.float32)
    found, offset = [[] for _ in range(LAYERS)], 0
    for lane in lanes:
        for layer in range(LAYERS):
            found[layer].append(whole[layer, offset : offset + lane.shape[1]])
        offset += lane.shape[1]
    return found


def scatter_small(grid, totals):
    place = lax.axis_index("clip") * grid.seq_size + lax.axis_index("seq")
    whole = jnp.stack([jnp.concatenate(layer) for layer in totals])
    for axis in (CORE, SEQ, CROSS, OUTER):
        whole, moved = yield whole, around(grid, whole, axis)
        whole = sum(moved, whole)
    pieces, offset = [], 0
    for total in totals[0]:
        amount = total.shape[0] // grid.owners
        pieces.append(
            lax.dynamic_slice_in_dim(whole, offset + place * amount, amount, 1)
        )
        offset += total.shape[0]
    return pieces


def pair_of(normed, w_pair, bias):
    return (times(normed, w_pair) + bias).astype(jnp.bfloat16)


def body(frames, cotangent, *params):
    grid, traffic = Grid(), Traffic()
    width = frames.shape[2]
    rows = frames.shape[0] * frames.shape[1]
    units = params[8].shape[2]
    blocks = units // width
    shards = []
    for layer in range(LAYERS):
        mixing, out, up, down = [
            params[slot][layer].astype(jnp.bfloat16) for slot in (2, 4, 8, 10)
        ]
        shards.append((mixing, jnp.concatenate([out, up, split_columns(down[None], blocks)], 1)))
    edges = [width, 3 * width, 4 * width, 4 * width + units, 4 * width + 2 * units]
    starts = [0] + edges[:-1]
    splits = [(start, stop, 1) for start, stop in zip(starts, edges)]
    splits[-1] = splits[-1][:2] + (blocks,)
    behind = [(start - edges[1], stop - edges[1], count) for start, stop, count in splits[2:]]

    def normal(hidden, gain, shift):
        normed = (normal_parts(hidden)[0] * gain + shift).astype(jnp.bfloat16)
        return normed, join(around(grid, normed, SEQ))

    hidden = frames.reshape(rows, width)
    kept = [{} for _ in range(LAYERS)]

    first = shards[0][0]
    first, vectors = lax.optimization_barrier((first, [params[slot] for slot in SMALL]))
    mixing = traffic.add(gather_rows(grid, first, tuple(splits[:2])))
    small = gather_small(grid, dict(zip(SMALL, vectors)))
    hidden = traffic.tick(hidden)
    rest = traffic.add(gather_rows(grid, shards[0][1], tuple(behind)))
    normed, normed_far = normal(hidden, *small[0][:2])
    hidden, normed, normed_far = traffic.tick(hidden, normed, normed_far)
    hidden, normed, normed_far = traffic.tick(hidden, normed, normed_far)
    second = traffic.add(
        gather_rows(grid, jnp.concatenate(shards[1], axis=1), tuple(splits))
    )
    hidden, normed, normed_far = traffic.tick(hidden, normed, normed_far)
    for layer in range(LAYERS):
        g1, s1, bm, bo, g2, s2, bu, bd = small[layer]
        keep = kept[layer]
        if layer == 0:
            w_query, w_pair = mixing["value"]
        else:
            while "value" not in second:
                hidden, normed, normed_far = traffic.tick(hidden, normed, normed_far)
            w_query, w_pair, w_out, w_up, w_down = second["value"]
        query = (times(normed, w_query) + bm[:width]).astype(jnp.bfloat16)
        pair_bias = jnp.concatenate([jnp.zeros((width,), jnp.float32), bm[width:]])
        pair, pair_far = [pair_of(part, w_pair, pair_bias) for part in (normed, normed_far)]
        attended, logs = attend(query, pair, pair_far)
        keep.update(
            hidden=hidden, normed=normed, normed_far=normed_far, query=query, pair=pair,
            pair_far=pair_far, logs=logs, w_query=w_query, w_pair=w_pair,
        )
        if layer == 0:
            while "value" not in rest:
                attended = traffic.tick(attended)
            w_out, w_up, w_down = rest["value"]
        middle = hidden + (times(attended, w_out) + bo)
        normed_two = (normal_parts(middle)[0] * g2 + s2).astype(jnp.bfloat16)
        active, slope = raise_width(normed_two, w_up, bu)
        keep.update(
            attended=attended, middle=middle, normed_two=normed_two, active=active,
            slope=slope, w_out=w_out, w_up=w_up, w_down=w_down,
        )
        hidden = middle + (times(active, w_down) + bd)
        if layer + 1 < LAYERS:
            normed, normed_far = normal(hidden, *small[layer + 1][:2])

    grad_hidden = cotangent.reshape(rows, width)
    shares, totals = [None] * LAYERS, [None] * LAYERS
    for layer in reversed(range(LAYERS)):
        g1, s1, bm, bo, g2, s2, bu, bd = small[layer]
        keep = kept[layer]
        grad_down = grad_hidden.astype(jnp.bfloat16)
        grad_before = (times_transposed(grad_down, keep["w_down"]) * keep["slope"]).astype(
            jnp.bfloat16
        )
        down_bias = column_total(grad_down)
        grad_hidden, grad_down, grad_before = traffic.tick(grad_hidden, grad_down, grad_before)
        up_bias = column_total(grad_before)
        grad_two = times_transposed(grad_before, keep["w_up"])
        pulled, gain_two, shift_two = normal_back(grad_two, keep["middle"], g2)
        grad_middle = grad_hidden + pulled
        grad_branch = grad_middle.astype(jnp.bfloat16)
        out_bias = column_total(grad_branch)
        grad_attended = times_transposed(grad_branch, keep["w_out"]).astype(jnp.bfloat16)
        feed = feed_shares(
            grid, keep["normed_two"], grad_before, keep["attended"], grad_branch,
            keep["active"], grad_down,
        )
        feed, grad_middle, grad_attended = traffic.tick(feed, grad_middle, grad_attended)
        feed_share = traffic.add(scatter_rows(grid, *feed))
        grad_query, grad_pair, grad_far = attend_back(
            keep["query"], keep["pair"], keep["pair_far"], keep["logs"], grad_attended
        )
        grad_query, grad_pair, grad_far = traffic.tick(grad_query, grad_pair, grad_far)
        far = times_transposed(grad_far, keep["w_pair"]).astype(jnp.bfloat16)
        arrived = [
            grid.shift(far[(amount - 1) * rows : amount * rows], SEQ, grid.seq_size - amount)
            for amount in range(1, grid.seq_size)
        ]
        mixed = mixing_shares(
            grid, keep["normed"], keep["normed_far"], grad_query, grad_pair, grad_far
        )
        mixing_bias = jnp.concatenate(
            [
                column_total(grad_query),
                column_total(grad_pair[:, width:]) + column_total(grad_far[:, width:]),
            ]
        )
        grad_normed = times_transposed(grad_query, keep["w_query"]) + times_transposed(
            grad_pair, keep["w_pair"]
        )
        mixed, grad_normed, arrived = traffic.tick(mixed, grad_normed, arrived)
        mixed_share = traffic.add(scatter_rows(grid, *mixed))
        grad_normed = total_of(grad_normed, arrived)
        pulled, gain_one, shift_one = normal_back(grad_normed, keep["hidden"], g1)
        grad_hidden = grad_middle + pulled
        shares[layer] = (mixed_share, feed_share)
        totals[layer] = (
            gain_one, shift_one, mixing_bias, out_bias, gain_two, shift_two, up_bias, down_bias,
        )
    owned = traffic.add(scatter_small(grid, totals))
    while traffic.active:
        grad_hidden = traffic.tick(grad_hidden)
    stacked = dict(zip(SMALL, owned["value"]))
    stacked[2] = jnp.stack([layer[0]["value"] for layer in shares])
    feeds = [layer[1]["value"] for layer in shares]
    stacked[4] = jnp.stack([feed[:, units : units + width] for feed in feeds])
    stacked[8] = jnp.stack([feed[:, :units] for feed in feeds])
    lows = [feed[:, units + width :].reshape(-1, blocks, width) for feed in feeds]
    stacked[10] = jnp.stack([jnp.moveaxis(low, 1, 0).reshape(-1, width) for low in lows])
    return tuple(
        [hidden.reshape(frames.shape), grad_hidden.reshape(frames.shape)]
        + [stacked[slot] for slot in range(12)]
    )


def solution(mesh):
    vector, matrix = P(None, AXES), P(None, AXES, None)
    whole = P("clip", "seq", None)
    params = tuple(matrix if slot in (2, 4, 8, 10) else vector for slot in range(12))
    return jax.shard_map(
        body,
        mesh=mesh,
        in_specs=(whole, whole) + params,
        out_specs=(whole, whole) + params,
        check_vma=False,
    )
```

time: 1740 us -> 664 us (0.38)
  Pallas kernels: 942 us -> 167 us
  waiting for transfers between devices: 288 us -> 189 us
  matrix products: 160 us -> 72.9 us
  blocking collectives: 71.5 us -> 0 us
  local copies, waits for them, and re-layouts: 74.2 us -> 41.8 us
    pallas_call x6 -> x9, Pallas kernels: 867 us -> 92.3 us  [the longest x2 30.3 us: feed_shares(): pl.pallas_call(functools.partial(feed_shares_kernel, grid), grid=(2 * blo...]
    unnamed x2 -> x0, waiting for transfers between devices: 115 us -> none
    all_gather x1 -> x0, blocking collectives: 71.5 us -> none  [gather_small(): whole = lax.all_gather(packed, AXES, axis=0, tiled=True)]
    dot_general x12 -> x0, matrix products: 41.5 us -> none  [outer_total(): lax.dot_general(left, right, (((0,), (0,)), ((), ())), preferred_element_...]
    dot_general x12 -> x10, matrix products: 73.3 us -> 35.2 us  [times(): lax.dot_general(left, right, (((1,), (0,)), ((), ())), preferred_element_...]
    convert_element_type x37 -> x35, other arithmetic: 17.4 us -> 37 us  [the longest x4 13.2 us: scatter_rows(): part = total_of(kept, arrived).astype(jnp.bfloat16)]
    ppermute x112 -> x81, waiting for transfers between devices: 173 us -> 189 us  [shift(): return lax.ppermute(array, AXES, pairs)]
    ppermute x112 -> x81, starting transfers between devices: 126 us -> 121 us  [shift(): return lax.ppermute(array, AXES, pairs)]
  transfers between devices with their start and end apart: 113 -> 81, of which waited for: 36 -> 31; matrix products, arithmetic and copies ran while one was open for 12% -> 14% of each run, Pallas kernels for 52% -> 18%
where the time goes in v2:
time: 664 us; the launch traced here: 657 us
  waiting for transfers between devices  189 us (28%)
  Pallas kernels  167 us (25%)
  starting transfers between devices  121 us (18%)
  matrix products  72.9 us (11%)
  other arithmetic  62.9 us (9%)
  local copies, waits for them, and re-layouts  41.8 us (6%)
    ppermute x81, waiting for transfers between devices, shift(): return lax.ppermute(array, AXES, pairs)  189 us
    ppermute x81, starting transfers between devices, shift(): return lax.ppermute(array, AXES, pairs)  121 us
    pallas_call x2, Pallas kernels, attend_back(): pl.pallas_call(attend_back_kernel, grid=(blocks,), in_specs=block_specs(f...  46.1 us
    dot_general x12, matrix products, times_transposed(): lax.dot_general(left, right, (((1,), (1,)), ((), ())), preferred_element_...  37.8 us
    dot_general x10, matrix products, times(): lax.dot_general(left, right, (((1,), (0,)), ((), ())), preferred_element_...  35.2 us
    pallas_call x2, Pallas kernels, feed_shares(): pl.pallas_call(functools.partial(feed_shares_kernel, grid), grid=(2 * blo...  30.3 us
    pallas_call x2, Pallas kernels, attend(): pl.pallas_call(attend_kernel, grid=(blocks,), in_specs=block_specs(frames...  28.9 us
    pallas_call x3, Pallas kernels, gather_rows(): pl.pallas_call(functools.partial(place_kernel, grid, steps, splits), out_...  27.2 us
  transfers between devices with their start and end apart: 81, of which 31 were waited for; matrix products, arithmetic and copies ran while one was open for 14% of the time, Pallas kernels for 18%

profile of v2, /device:TPU:0, one launch (start us, length us, event | category | flops | bytes accessed | tf_op | source)
XLA Modules:
  0.0 657.1 jit_solution(14101037207467066108)
XLA Ops:
  8.8 3.6 collective-permute-start.3
  39.2 11.9 %collective-permute-done.13 = bf16[1,24,6912]{2,1,0:T(8,128)(2,1)} collective-permute-done((bf16[1,24,6912]{2,1,0:T(8,128)(2,1)S(1)}, bf16[1,24,6912]{2,1,0:T(8,128)(2,1)}, u32[]{:S(2)}, u32[]{:S(2)}) %collective-permute-start.13) | collective-permute-done | bytes 331808 | tf_op jit(solution)/shard_map/ppermute | solution.py:38
  51.1 8.3 %collective-permute-done.11 = bf16[2,24,2304]{2,1,0:T(8,128)(2,1)S(1)} collective-permute-done((bf16[2,24,2304]{2,1,0:T(8,128)(2,1)S(1)}, bf16[2,24,2304]{2,1,0:T(8,128)(2,1)S(1)}, u32[]{:S(2)}, u32[]{:S(2)}) %collective-permute-start.11) | collective-permute-done | bytes 221216 | tf_op jit(solution)/shard_map/ppermute | solution.py:38
  66.9 8.0 %collective-permute-start.25 = (bf16[1,24,9216]{2,1,0:T(8,128)(2,1)S(1)}, bf16[1,24,9216]{2,1,0:T(8,128)(2,1)S(1)}, u32[]{:S(2)}, u32[]{:S(2)}) collective-permute-start(bf16[1,24,9216]{2,1,0:T(8,128)(2,1)S(1)} %maximum_bitcast_fusion), channel_id=1, source_target_pairs={{0,8},{1,9},{2,10},{3,11},{4,12},{5,13},{6,14},{7,15},{8,16},{9,17... | collective-permute-start | bytes 1327112 | tf_op jit(solution)/shard_map/ppermute | solution.py:38
  74.9 14.7 %collective-permute-done.16.refs_3_ = bf16[4,24,2304]{2,1,0:T(8,128)(2,1)S(1)} collective-permute-done((bf16[4,24,2304]{2,1,0:T(8,128)(2,1)S(1)}, bf16[4,24,2304]{2,1,0:T(8,128)(2,1)S(1)}, u32[]{:S(2)}, u32[]{:S(2)}) %collective-permute-start.16) | collective-permute-done | bytes 442400 | tf_op jit(solution)/shard_map/ppermute | solution.py:38
  90.9 5.8 collective-permute-start.26
  96.7 4.4 collective-permute-start.27
  101.1 12.2 %collective-permute-done.26 = bf16[1,24,9216]{2,1,0:T(8,128)(2,1)S(1)} collective-permute-done((bf16[1,24,9216]{2,1,0:T(8,128)(2,1)S(1)}, bf16[1,24,9216]{2,1,0:T(8,128)(2,1)S(1)}, u32[]{:S(2)}, u32[]{:S(2)}) %collective-permute-start.26) | collective-permute-done | bytes 442400 | tf_op jit(solution)/shard_map/ppermute | solution.py:38
  121.2 4.8 place_rows.3
  126.0 4.6 fusion.2.k_far_ref.v_far_ref
  133.2 5.9 collective-permute-done.33
  142.3 14.4 %attend.2 = (bf16[512,768]{1,0:T(8,128)(2,1)}, f32[6,2,512]{2,1,0:T(2,128)}) custom-call(bf16[512,768]{1,0:T(8,128)(2,1)} %add_convert_fusion.12.q_ref, bf16[512,1536]{1,0:T(8,128)(2,1)} %fusion.1.k_ref.v_ref, bf16[512,1536]{1,0:T(8,128)(2,1)} %fusion.1.k_ref.v_ref, bf16[512,1536]{1,0:T(8,128)(2,1)} %fusion.2.k_far_ref.v_far_ref, ...), custom_call_target="tpu_custom_call" | custom-call | flops 1000 | bytes 1000 | tf_op jit(solution)/shard_map/attend/pallas_call | solution.py:429
  165.6 9.9 %place_rows.4 = (bf16[32,24,768]{2,1,0:T(8,128)(2,1)}, bf16[32,24,3072]{2,1,0:T(8,128)(2,1)}, bf16[128,24,768]{2,1,0:T(8,128)(2,1)}) custom-call(bf16[4,24,6912]{2,1,0:T(8,128)(2,1)} %copy-done.28, bf16[4,24,6912]{2,1,0:T(8,128)(2,1)} %collective-permute-done.23.refs_1_, bf16[4,24,6912]{2,1,0:T(8,128)(2,1)} %copy-done.27, ...), custom_call_target="tpu_custom_call" | custom-call | flops 1000 | bytes 1000 | tf_op jit(solution)/shard_map/place_rows/pallas_call | solution.py:134
  179.6 9.9 %raise_width.2 = (bf16[512,3072]{1,0:T(8,128)(2,1)}, f32[512,3072]{1,0:T(8,128)}) custom-call(bf16[512,768]{1,0:T(8,128)(2,1)} %add_convert_fusion.11.left_ref.normed_ref, bf16[768,3072]{1,0:T(8,128)(2,1)} %bitcast.159, f32[1,3072]{1,0:T(1,128)} %get-tuple-element.568.bias_ref), custom_call_target="tpu_custom_call" | custom-call | flops 1000 | bytes 1000 | tf_op jit(solution)/shard_map/raise_width/pallas_call | solution.py:505
  189.5 6.0 fusion.27
  196.7 21.1 %collective-permute-done.34.far_ref = bf16[512,768]{1,0:T(8,128)(2,1)S(1)} collective-permute-done((bf16[512,768]{1,0:T(8,128)(2,1)S(1)}, bf16[512,768]{1,0:T(8,128)(2,1)S(1)}, u32[]{:S(2)}, u32[]{:S(2)}) %collective-permute-start.34) | collective-permute-done | bytes 786464 | tf_op jit(solution)/shard_map/ppermute | solution.py:38
  221.8 7.6 %collective-permute-done.38.refs_5_ = bf16[4,24,9216]{2,1,0:T(8,128)(2,1)S(1)} collective-permute-done((bf16[4,24,9216]{2,1,0:T(8,128)(2,1)}, bf16[4,24,9216]{2,1,0:T(8,128)(2,1)S(1)}, u32[]{:S(2)}, u32[]{:S(2)}) %collective-permute-start.38) | collective-permute-done | bytes 1769504 | tf_op jit(solution)/shard_map/ppermute | solution.py:38
  231.8 12.5 %place_rows.5 = (bf16[32,24,768]{2,1,0:T(8,128)(2,1)}, bf16[32,24,1536]{2,1,0:T(8,128)(2,1)}, bf16[32,24,768]{2,1,0:T(8,128)(2,1)}, bf16[32,24,3072]{2,1,0:T(8,128)(2,1)}, bf16[128,24,768]{2,1,0:T(8,128)(2,1)}) custom-call(bf16[4,24,9216]{2,1,0:T(8,128)(2,1)} %constant_dynamic-update-slice_fusion.28.refs_0_, ...), custom_call_target="tpu_custom_call" | custom-call | flops 1000 | bytes 1000 | tf_op jit(solution)/shard_map/place_rows/pallas_call | solution.py:134
  244.4 4.3 fusion.4.k_far_ref.v_far_ref
  252.0 3.2 add_convert_fusion.9.q_ref
  255.2 14.5 %attend.3 = (bf16[512,768]{1,0:T(8,128)(2,1)}, f32[6,2,512]{2,1,0:T(2,128)}) custom-call(bf16[512,768]{1,0:T(8,128)(2,1)} %add_convert_fusion.9.q_ref, bf16[512,1536]{1,0:T(8,128)(2,1)} %fusion.3.k_ref.v_ref, bf16[512,1536]{1,0:T(8,128)(2,1)} %fusion.3.k_ref.v_ref, bf16[512,1536]{1,0:T(8,128)(2,1)} %fusion.4.k_far_ref.v_far_ref, ...), custom_call_target="tpu_custom_call" | custom-call | flops 1000 | bytes 1000 | tf_op jit(solution)/shard_map/attend/pallas_call | solution.py:429
  273.2 6.9 %fusion.5 = f32[3072,512]{0,1:T(8,128)} fusion(bf16[3072,768]{1,0:T(8,128)(2,1)} %bitcast.193, f32[1,512,768]{2,1,0:T(8,128)S(1)} %copy-done.11), kind=kOutput, calls=%fused_computation.99 | convolution fusion | flops 2416312320 | bytes 12582912 | tf_op jit(solution)/shard_map/dot_general | solution.py:341
  281.4 10.0 %raise_width.3 = (bf16[512,3072]{1,0:T(8,128)(2,1)}, f32[512,3072]{1,0:T(8,128)}) custom-call(bf16[512,768]{1,0:T(8,128)(2,1)} %add_convert_fusion.8.left_ref.normed_ref, bf16[768,3072]{1,0:T(8,128)(2,1)} %bitcast.163, f32[1,3072]{1,0:T(1,128)} %get-tuple-element.567.bias_ref), custom_call_target="tpu_custom_call" | custom-call | flops 1000 | bytes 1000 | tf_op jit(solution)/shard_map/raise_width/pallas_call | solution.py:505
  291.3 6.0 fusion.37
  297.4 3.6 fusion.before_ref
  301.0 7.1 %multiply_reduce_fusion = (f32[768]{0:T(1024)}, f32[512]{0:T(512)S(1)}, f32[512]{0:T(512)S(1)}, f32[768]{0:T(1024)}, f32[512,768]{1,0:T(8,128)S(1)}) fusion(f32[512,768]{1,0:T(8,128)S(1)} %get-tuple-element.490, f32[512]{0:T(512)S(1)} %add_rsqrt_fusion.2, f32[512]{0:T(512)S(1)} %get-tuple-element.576, f32[768]{0:T(1024)S(1)} %get-tuple-element.464, ...), kind=kOutput, calls=%fused_computation.38 | convolution fusion | flops 2419455488 | bytes 11027456 | tf_op jit(solution)/shard_map/dot_general | solution.py:341
  312.3 15.0 %feed_shares.2 = (bf16[384,6912]{1,0:T(8,128)(2,1)}, bf16[384,6912]{1,0:T(8,128)(2,1)}) custom-call(bf16[512,768]{1,0:T(8,128)(2,1)} %add_convert_fusion.8.left_ref.normed_ref, bf16[512,3072]{1,0:T(8,128)(2,1)} %copy-done.1, bf16[512,768]{1,0:T(8,128)(2,1)} %get-tuple-element.325.mixed_ref, bf16[512,768]{1,0:T(8,128)(2,1)} %copy-done.22, ...), custom_call_target="tpu_custom_call" | custom-call | flops 1000 | bytes 1000 | tf_op jit(solution)/shard_map/feed_shares/pallas_call | solution.py:254
  327.9 23.3 %attend_back.2 = (bf16[512,768]{1,0:T(8,128)(2,1)}, bf16[512,1536]{1,0:T(8,128)(2,1)}, bf16[512,1536]{1,0:T(8,128)(2,1)}) custom-call(bf16[512,768]{1,0:T(8,128)(2,1)} %add_convert_fusion.9.q_ref, bf16[512,1536]{1,0:T(8,128)(2,1)} %fusion.3.k_ref.v_ref, bf16[512,1536]{1,0:T(8,128)(2,1)} %fusion.3.k_ref.v_ref, bf16[512,1536]{1,0:T(8,128)(2,1)} %fusion.4.k_far_ref.v_far_ref, ...), custom_call_target="tpu_custom_call" | custom-call | flops 1000 | bytes 1000 | tf_op jit(solution)/shard_map/attend_back/pallas_call | solution.py:450
  351.9 5.3 add_convert_fusion.1
  367.0 7.4 %mixing_shares.2 = (bf16[384,2304]{1,0:T(8,128)(2,1)}, bf16[384,2304]{1,0:T(8,128)(2,1)}) custom-call(bf16[512,768]{1,0:T(8,128)(2,1)} %copy-done.25, bf16[512,768]{1,0:T(8,128)(2,1)} %copy-done.49, bf16[512,768]{1,0:T(8,128)(2,1)} %get-tuple-element.344.query_ref, bf16[512,1536]{1,0:T(8,128)(2,1)} %get-tuple-element.345.pair_ref, ...), custom_call_target="tpu_custom_call" | custom-call | flops 1000 | bytes 1000 | tf_op jit(solution)/shard_map/mixing_shares/pallas_call | solution.py:314
  374.4 3.7 fusion.38
  379.0 28.3 %collective-permute-done.42 = bf16[512,768]{1,0:T(8,128)(2,1)S(1)} collective-permute-done((bf16[512,768]{1,0:T(8,128)(2,1)}, bf16[512,768]{1,0:T(8,128)(2,1)S(1)}, u32[]{:S(2)}, u32[]{:S(2)}) %collective-permute-start.42) | collective-permute-done | bytes 786464 | tf_op jit(solution)/shard_map/ppermute | solution.py:38
  438.8 12.1 %collective-permute-start.48 = (bf16[1,1,1,1,24,6912]{5,4,3,2,1,0:T(8,128)(2,1)S(1)}, bf16[1,1,1,1,24,6912]{5,4,3,2,1,0:T(8,128)(2,1)S(1)}, u32[]{:S(2)}, u32[]{:S(2)}) collective-permute-start(bf16[1,1,1,1,24,6912]{5,4,3,2,1,0:T(8,128)(2,1)S(1)} %get-tuple-element.521), channel_id=1, source_target_pairs={{0,8},{1,9},{2,10},{3,11},{4,12},{5,13},{6,14},{7,15},{8,16},{9,17... | collective-permute-start | bytes 995336 | tf_op jit(solution)/shard_map/ppermute | solution.py:38
  458.0 15.4 %feed_shares.3 = (bf16[384,6912]{1,0:T(8,128)(2,1)}, bf16[384,6912]{1,0:T(8,128)(2,1)}) custom-call(bf16[512,768]{1,0:T(8,128)(2,1)} %add_convert_fusion.11.left_ref.normed_ref, bf16[512,3072]{1,0:T(8,128)(2,1)} %copy-done.3, bf16[512,768]{1,0:T(8,128)(2,1)} %get-tuple-element.288.mixed_ref, bf16[512,768]{1,0:T(8,128)(2,1)} %get-tuple-element.482.branch_ref, ...), custom_call_target="tpu_custom_call" | custom-call | flops 1000 | bytes 1000 | tf_op jit(solution)/shard_map/feed_shares/pallas_call | solution.py:254
  483.9 22.8 %attend_back.3 = (bf16[512,768]{1,0:T(8,128)(2,1)}, bf16[512,1536]{1,0:T(8,128)(2,1)}, bf16[512,1536]{1,0:T(8,128)(2,1)}) custom-call(bf16[512,768]{1,0:T(8,128)(2,1)} %add_convert_fusion.12.q_ref, bf16[512,1536]{1,0:T(8,128)(2,1)} %fusion.1.k_ref.v_ref, bf16[512,1536]{1,0:T(8,128)(2,1)} %fusion.1.k_ref.v_ref, bf16[512,1536]{1,0:T(8,128)(2,1)} %fusion.2.k_far_ref.v_far_ref, ...), custom_call_target="tpu_custom_call" | custom-call | flops 1000 | bytes 1000 | tf_op jit(solution)/shard_map/attend_back/pallas_call | solution.py:450
  510.1 5.4 add_convert_fusion
  522.6 3.8 collective-permute-start.57
  531.6 7.5 %mixing_shares.3 = (bf16[384,2304]{1,0:T(8,128)(2,1)}, bf16[384,2304]{1,0:T(8,128)(2,1)}) custom-call(bf16[512,768]{1,0:T(8,128)(2,1)} %copy-done.24, bf16[512,768]{1,0:T(8,128)(2,1)} %collective-permute-done.9.far_ref, bf16[512,768]{1,0:T(8,128)(2,1)} %get-tuple-element.383.query_ref, bf16[512,1536]{1,0:T(8,128)(2,1)} %get-tuple-element.384.pair_ref, ...), custom_call_target="tpu_custom_call" | custom-call | flops 1000 | bytes 1000 | tf_op jit(solution)/shard_map/mixing_shares/pallas_call | solution.py:314
  545.4 3.4 collective-permute-done.59
  548.9 16.4 %collective-permute-done.56 = bf16[512,768]{1,0:T(8,128)(2,1)S(1)} collective-permute-done((bf16[512,768]{1,0:T(8,128)(2,1)}, bf16[512,768]{1,0:T(8,128)(2,1)S(1)}, u32[]{:S(2)}, u32[]{:S(2)}) %collective-permute-start.56) | collective-permute-done | bytes 786464 | tf_op jit(solution)/shard_map/ppermute | solution.py:38
  576.1 10.2 %collective-permute-done.63 = bf16[2,1,1,1,24,6912]{5,4,3,2,1,0:T(8,128)(2,1)S(1)} collective-permute-done((bf16[2,1,1,1,24,6912]{5,4,3,2,1,0:T(8,128)(2,1)S(1)}, bf16[2,1,1,1,24,6912]{5,4,3,2,1,0:T(8,128)(2,1)S(1)}, u32[]{:S(2)}, u32[]{:S(2)}) %collective-permute-start.63) | collective-permute-done | bytes 663584 | tf_op jit(solution)/shard_map/ppermute | solution.py:38
  586.3 3.3 collective-permute-done.62
  594.6 5.2 collective-permute-start.66
  603.3 6.0 collective-permute-done.66
  609.3 11.8 %collective-permute-done.67 = bf16[1,1,1,1,24,6912]{5,4,3,2,1,0:T(8,128)(2,1)S(1)} collective-permute-done((bf16[1,1,1,1,24,6912]{5,4,3,2,1,0:T(8,128)(2,1)S(1)}, bf16[1,1,1,1,24,6912]{5,4,3,2,1,0:T(8,128)(2,1)S(1)}, u32[]{:S(2)}, u32[]{:S(2)}) %collective-permute-start.67) | collective-permute-done | bytes 331808 | tf_op jit(solution)/shard_map/ppermute | solution.py:38
  626.6 3.7 collective-permute-done.73
  630.7 7.7 %collective-permute-start.78 = (f32[2,9216]{1,0:T(2,128)S(1)}, f32[2,9216]{1,0:T(2,128)S(1)}, u32[]{:S(2)}, u32[]{:S(2)}) collective-permute-start(f32[2,9216]{1,0:T(2,128)S(1)} %add.677), channel_id=1, source_target_pairs={{0,8},{1,9},{2,10},{3,11},{4,12},{5,13},{6,14},{7,15},{8,16},{9,17... | collective-permute-start | bytes 221192 | tf_op jit(solution)/shard_map/ppermute | solution.py:38
  649.0 4.8 collective-permute-done.76
  (548 shorter events, 210.5 us)
Async XLA Ops:
  28.3 22.7 %collective-permute-start.13 = (bf16[1,24,6912]{2,1,0:T(8,128)(2,1)S(1)}, bf16[1,24,6912]{2,1,0:T(8,128)(2,1)}, u32[]{:S(2)}, u32[]{:S(2)}) collective-permute-start(bf16[1,24,6912]{2,1,0:T(8,128)(2,1)S(1)} %maximum_bitcast_fusion.1), channel_id=1, source_target_pairs={{0,16},{1,17},{2,18},{3,19},{4,20},{5,21},{6,22},{7,23},{8,24},{9,... | collective-permute-start | bytes 995336 | tf_op jit(solution)/shard_map/ppermute | solution.py:38
  30.4 20.7 %collective-permute-start.14 = (bf16[1,24,6912]{2,1,0:T(8,128)(2,1)S(1)}, bf16[1,24,6912]{2,1,0:T(8,128)(2,1)}, u32[]{:S(2)}, u32[]{:S(2)}) collective-permute-start(bf16[1,24,6912]{2,1,0:T(8,128)(2,1)S(1)} %maximum_bitcast_fusion.1), channel_id=1, source_target_pairs={{0,24},{1,25},{2,26},{3,27},{4,28},{5,29},{6,30},{7,31},{8,0},{9,1... | collective-permute-start | bytes 995336 | tf_op jit(solution)/shard_map/ppermute | solution.py:38
  32.0 19.0 %collective-permute-start.10 = (bf16[2,24,2304]{2,1,0:T(8,128)(2,1)S(1)}, bf16[2,24,2304]{2,1,0:T(8,128)(2,1)S(1)}, u32[]{:S(2)}, u32[]{:S(2)}) collective-permute-start(bf16[2,24,2304]{2,1,0:T(8,128)(2,1)S(1)} %constant_dynamic-update-slice_fusion.8), channel_id=1, source_target_pairs={{0,4},{1,5},{2,6},{3,7},{4,0},{5,1},{6,2},{7,3},{8,12},{9,13},{10,... | collective-permute-start | bytes 663560 | tf_op jit(solution)/shard_map/ppermute | solution.py:38
  34.9 24.5 %collective-permute-start.9 = (bf16[512,768]{1,0:T(8,128)(2,1)S(1)}, bf16[512,768]{1,0:T(8,128)(2,1)}, u32[]{:S(2)}, u32[]{:S(2)}) collective-permute-start(bf16[512,768]{1,0:T(8,128)(2,1)S(1)} %add_convert_fusion.13.near_ref), channel_id=1, source_target_pairs={{0,1},{1,0},{2,3},{3,2},{4,5},{5,4},{6,7},{7,6},{8,9},{9,8},{10,11... | collective-permute-start | bytes 2359304 | tf_op jit(solution)/shard_map/ppermute | solution.py:38
  39.0 20.4 %collective-permute-start.11 = (bf16[2,24,2304]{2,1,0:T(8,128)(2,1)S(1)}, bf16[2,24,2304]{2,1,0:T(8,128)(2,1)S(1)}, u32[]{:S(2)}, u32[]{:S(2)}) collective-permute-start(bf16[2,24,2304]{2,1,0:T(8,128)(2,1)S(1)} %constant_dynamic-update-slice_fusion.10), channel_id=1, source_target_pairs={{0,1},{1,0},{2,3},{3,2},{4,5},{5,4},{6,7},{7,6},{8,9},{9,8},{10,11... | collective-permute-start | bytes 663560 | tf_op jit(solution)/shard_map/ppermute | solution.py:38
  61.4 28.2 %collective-permute-start.18 = (bf16[2,24,6912]{2,1,0:T(8,128)(2,1)S(1)}, bf16[2,24,6912]{2,1,0:T(8,128)(2,1)S(1)}, u32[]{:S(2)}, u32[]{:S(2)}) collective-permute-start(bf16[2,24,6912]{2,1,0:T(8,128)(2,1)S(1)} %constant_dynamic-update-slice_fusion.18), channel_id=1, source_target_pairs={{0,1},{1,0},{2,3},{3,2},{4,5},{5,4},{6,7},{7,6},{8,9},{9,8},{10,11... | collective-permute-start | bytes 1990664 | tf_op jit(solution)/shard_map/ppermute | solution.py:38
  64.1 25.5 %collective-permute-start.17 = (bf16[2,24,6912]{2,1,0:T(8,128)(2,1)S(1)}, bf16[2,24,6912]{2,1,0:T(8,128)(2,1)S(1)}, u32[]{:S(2)}, u32[]{:S(2)}) collective-permute-start(bf16[2,24,6912]{2,1,0:T(8,128)(2,1)S(1)} %constant_dynamic-update-slice_fusion.16), channel_id=1, source_target_pairs={{0,4},{1,5},{2,6},{3,7},{4,0},{5,1},{6,2},{7,3},{8,12},{9,13},{10,... | collective-permute-start | bytes 1990664 | tf_op jit(solution)/shard_map/ppermute | solution.py:38
  64.8 24.8 %collective-permute-start.16 = (bf16[4,24,2304]{2,1,0:T(8,128)(2,1)S(1)}, bf16[4,24,2304]{2,1,0:T(8,128)(2,1)S(1)}, u32[]{:S(2)}, u32[]{:S(2)}) collective-permute-start(bf16[4,24,2304]{2,1,0:T(8,128)(2,1)S(1)} %constant_dynamic-update-slice_fusion.14.refs_2_), channel_id=1, source_target_pairs={{0,4},{1,5},{2,6},{3,7},{4,0},{5,1},{6,2},{7,3},{8,12},{9,13},{10,... | collective-permute-start | bytes 1327112 | tf_op jit(solution)/shard_map/ppermute | solution.py:38
  66.4 23.2 %collective-permute-start.15 = (bf16[4,24,2304]{2,1,0:T(8,128)(2,1)S(1)}, bf16[4,24,2304]{2,1,0:T(8,128)(2,1)S(1)}, u32[]{:S(2)}, u32[]{:S(2)}) collective-permute-start(bf16[4,24,2304]{2,1,0:T(8,128)(2,1)S(1)} %constant_dynamic-update-slice_fusion.12.refs_0_), channel_id=1, source_target_pairs={{0,1},{1,0},{2,3},{3,2},{4,5},{5,4},{6,7},{7,6},{8,9},{9,8},{10,11... | collective-permute-start | bytes 1327112 | tf_op jit(solution)/shard_map/ppermute | solution.py:38
  66.9 34.2 %collective-permute-start.25 = (bf16[1,24,9216]{2,1,0:T(8,128)(2,1)S(1)}, bf16[1,24,9216]{2,1,0:T(8,128)(2,1)S(1)}, u32[]{:S(2)}, u32[]{:S(2)}) collective-permute-start(bf16[1,24,9216]{2,1,0:T(8,128)(2,1)S(1)} %maximum_bitcast_fusion), channel_id=1, source_target_pairs={{0,8},{1,9},{2,10},{3,11},{4,12},{5,13},{6,14},{7,15},{8,16},{9,17... | collective-permute-start | bytes 1327112 | tf_op jit(solution)/shard_map/ppermute | solution.py:38
  89.7 29.4 %collective-permute-start.24 = (bf16[4,24,6912]{2,1,0:T(8,128)(2,1)S(1)}, bf16[4,24,6912]{2,1,0:T(8,128)(2,1)}, u32[]{:S(2)}, u32[]{:S(2)}) collective-permute-start(bf16[4,24,6912]{2,1,0:T(8,128)(2,1)S(1)} %constant_dynamic-update-slice_fusion.22.refs_2_), channel_id=1, source_target_pairs={{0,4},{1,5},{2,6},{3,7},{4,0},{5,1},{6,2},{7,3},{8,12},{9,13},{10,... | collective-permute-start | bytes 3981320 | tf_op jit(solution)/shard_map/ppermute | solution.py:38
  90.4 29.1 %collective-permute-start.23 = (bf16[4,24,6912]{2,1,0:T(8,128)(2,1)S(1)}, bf16[4,24,6912]{2,1,0:T(8,128)(2,1)}, u32[]{:S(2)}, u32[]{:S(2)}) collective-permute-start(bf16[4,24,6912]{2,1,0:T(8,128)(2,1)S(1)} %constant_dynamic-update-slice_fusion.20.refs_0_), channel_id=1, source_target_pairs={{0,1},{1,0},{2,3},{3,2},{4,5},{5,4},{6,7},{7,6},{8,9},{9,8},{10,11... | collective-permute-start | bytes 3981320 | tf_op jit(solution)/shard_map/ppermute | solution.py:38
  90.9 22.4 %collective-permute-start.26 = (bf16[1,24,9216]{2,1,0:T(8,128)(2,1)S(1)}, bf16[1,24,9216]{2,1,0:T(8,128)(2,1)S(1)}, u32[]{:S(2)}, u32[]{:S(2)}) collective-permute-start(bf16[1,24,9216]{2,1,0:T(8,128)(2,1)S(1)} %maximum_bitcast_fusion), channel_id=1, source_target_pairs={{0,16},{1,17},{2,18},{3,19},{4,20},{5,21},{6,22},{7,23},{8,24},{9,... | collective-permute-start | bytes 1327112 | tf_op jit(solution)/shard_map/ppermute | solution.py:38
  96.7 16.6 %collective-permute-start.27 = (bf16[1,24,9216]{2,1,0:T(8,128)(2,1)S(1)}, bf16[1,24,9216]{2,1,0:T(8,128)(2,1)S(1)}, u32[]{:S(2)}, u32[]{:S(2)}) collective-permute-start(bf16[1,24,9216]{2,1,0:T(8,128)(2,1)S(1)} %maximum_bitcast_fusion), channel_id=1, source_target_pairs={{0,24},{1,25},{2,26},{3,27},{4,28},{5,29},{6,30},{7,31},{8,0},{9,1... | collective-permute-start | bytes 1327112 | tf_op jit(solution)/shard_map/ppermute | solution.py:38
  119.6 19.5 %collective-permute-start.33 = (bf16[2,24,9216]{2,1,0:T(8,128)(2,1)S(1)}, bf16[2,24,9216]{2,1,0:T(8,128)(2,1)}, u32[]{:S(2)}, u32[]{:S(2)}) collective-permute-start(bf16[2,24,9216]{2,1,0:T(8,128)(2,1)S(1)} %constant_dynamic-update-slice_fusion.26), channel_id=1, source_target_pairs={{0,1},{1,0},{2,3},{3,2},{4,5},{5,4},{6,7},{7,6},{8,9},{9,8},{10,11... | collective-permute-start | bytes 2654216 | tf_op jit(solution)/shard_map/ppermute | solution.py:38
  120.1 37.4 %collective-permute-start.28 = (bf16[4,24,6912]{2,1,0:T(8,128)(2,1)S(1)}, bf16[4,24,6912]{2,1,0:T(8,128)(2,1)}, u32[]{:S(2)}, u32[]{:S(2)}) collective-permute-start(bf16[4,24,6912]{2,1,0:T(8,128)(2,1)S(1)} %constant_dynamic-update-slice_fusion.20.refs_0_), channel_id=1, source_target_pairs={{0,2},{1,3},{2,0},{3,1},{4,6},{5,7},{6,4},{7,5},{8,10},{9,11},{10,... | collective-permute-start | bytes 3981320 | tf_op jit(solution)/shard_map/ppermute | solution.py:38
  120.2 37.3 %collective-permute-start.29 = (bf16[4,24,6912]{2,1,0:T(8,128)(2,1)}, bf16[4,24,6912]{2,1,0:T(8,128)(2,1)}, u32[]{:S(2)}, u32[]{:S(2)}) collective-permute-start(bf16[4,24,6912]{2,1,0:T(8,128)(2,1)} %collective-permute-done.23.refs_1_), channel_id=1, source_target_pairs={{0,2},{1,3},{2,0},{3,1},{4,6},{5,7},{6,4},{7,5},{8,10},{9,11},{10,... | collective-permute-start | bytes 3981320 | tf_op jit(solution)/shard_map/ppermute | solution.py:38
  120.7 36.8 %collective-permute-start.30 = (bf16[4,24,6912]{2,1,0:T(8,128)(2,1)S(1)}, bf16[4,24,6912]{2,1,0:T(8,128)(2,1)}, u32[]{:S(2)}, u32[]{:S(2)}) collective-permute-start(bf16[4,24,6912]{2,1,0:T(8,128)(2,1)S(1)} %constant_dynamic-update-slice_fusion.22.refs_2_), channel_id=1, source_target_pairs={{0,2},{1,3},{2,0},{3,1},{4,6},{5,7},{6,4},{7,5},{8,10},{9,11},{10,... | collective-permute-start | bytes 3981320 | tf_op jit(solution)/shard_map/ppermute | solution.py:38
  120.7 36.8 %collective-permute-start.31 = (bf16[4,24,6912]{2,1,0:T(8,128)(2,1)}, bf16[4,24,6912]{2,1,0:T(8,128)(2,1)}, u32[]{:S(2)}, u32[]{:S(2)}) collective-permute-start(bf16[4,24,6912]{2,1,0:T(8,128)(2,1)} %collective-permute-done.24.refs_3_), channel_id=1, source_target_pairs={{0,2},{1,3},{2,0},{3,1},{4,6},{5,7},{6,4},{7,5},{8,10},{9,11},{10,... | collective-permute-start | bytes 3981320 | tf_op jit(solution)/shard_map/ppermute | solution.py:38
  139.1 18.4 %collective-permute-start.32 = (bf16[2,24,9216]{2,1,0:T(8,128)(2,1)S(1)}, bf16[2,24,9216]{2,1,0:T(8,128)(2,1)S(1)}, u32[]{:S(2)}, u32[]{:S(2)}) collective-permute-start(bf16[2,24,9216]{2,1,0:T(8,128)(2,1)S(1)} %constant_dynamic-update-slice_fusion.24), channel_id=1, source_target_pairs={{0,4},{1,5},{2,6},{3,7},{4,0},{5,1},{6,2},{7,3},{8,12},{9,13},{10,... | collective-permute-start | bytes 2654216 | tf_op jit(solution)/shard_map/ppermute | solution.py:38
  161.1 56.7 %collective-permute-start.36 = (bf16[4,24,9216]{2,1,0:T(8,128)(2,1)S(1)}, bf16[4,24,9216]{2,1,0:T(8,128)(2,1)}, u32[]{:S(2)}, u32[]{:S(2)}) collective-permute-start(bf16[4,24,9216]{2,1,0:T(8,128)(2,1)S(1)} %constant_dynamic-update-slice_fusion.30.refs_2_), channel_id=1, source_target_pairs={{0,4},{1,5},{2,6},{3,7},{4,0},{5,1},{6,2},{7,3},{8,12},{9,13},{10,... | collective-permute-start | bytes 5308424 | tf_op jit(solution)/shard_map/ppermute | solution.py:38
  163.6 54.2 %collective-permute-start.35 = (bf16[4,24,9216]{2,1,0:T(8,128)(2,1)}, bf16[4,24,9216]{2,1,0:T(8,128)(2,1)}, u32[]{:S(2)}, u32[]{:S(2)}) collective-permute-start(bf16[4,24,9216]{2,1,0:T(8,128)(2,1)} %constant_dynamic-update-slice_fusion.28.refs_0_), channel_id=1, source_target_pairs={{0,1},{1,0},{2,3},{3,2},{4,5},{5,4},{6,7},{7,6},{8,9},{9,8},{10,11... | collective-permute-start | bytes 5308424 | tf_op jit(solution)/shard_map/ppermute | solution.py:38
  196.5 21.3 %collective-permute-start.34 = (bf16[512,768]{1,0:T(8,128)(2,1)S(1)}, bf16[512,768]{1,0:T(8,128)(2,1)S(1)}, u32[]{:S(2)}, u32[]{:S(2)}) collective-permute-start(bf16[512,768]{1,0:T(8,128)(2,1)S(1)} %add_convert_fusion.10.near_ref), channel_id=1, source_target_pairs={{0,1},{1,0},{2,3},{3,2},{4,5},{5,4},{6,7},{7,6},{8,9},{9,8},{10,11... | collective-permute-start | bytes 2359304 | tf_op jit(solution)/shard_map/ppermute | solution.py:38
  327.2 24.6 %collective-permute-start.41 = (bf16[4,2,1,2,24,6912]{5,4,3,2,1,0:T(8,128)(2,1)}, bf16[4,2,1,2,24,6912]{5,4,3,2,1,0:T(8,128)(2,1)}, u32[]{:S(2)}, u32[]{:S(2)}) collective-permute-start(bf16[4,2,1,2,24,6912]{5,4,3,2,1,0:T(8,128)(2,1)} %bitcast.187), channel_id=1, source_target_pairs={{0,2},{1,3},{2,0},{3,1},{4,6},{5,7},{6,4},{7,5},{8,10},{9,11},{10,... | collective-permute-start | bytes 15925256 | tf_op jit(solution)/shard_map/ppermute | solution.py:38
  358.8 48.5 %collective-permute-start.44 = (bf16[2,2,1,1,24,6912]{5,4,3,2,1,0:T(8,128)(2,1)}, bf16[2,2,1,1,24,6912]{5,4,3,2,1,0:T(8,128)(2,1)}, u32[]{:S(2)}, u32[]{:S(2)}) collective-permute-start(bf16[2,2,1,1,24,6912]{5,4,3,2,1,0:T(8,128)(2,1)} %get-tuple-element.501), channel_id=1, source_target_pairs={{0,1},{1,0},{2,3},{3,2},{4,5},{5,4},{6,7},{7,6},{8,9},{9,8},{10,11... | collective-permute-start | bytes 3981320 | tf_op jit(solution)/shard_map/ppermute | solution.py:38
  361.9 45.4 %collective-permute-start.43 = (bf16[2,1,1,2,24,6912]{5,4,3,2,1,0:T(8,128)(2,1)}, bf16[2,1,1,2,24,6912]{5,4,3,2,1,0:T(8,128)(2,1)}, u32[]{:S(2)}, u32[]{:S(2)}) collective-permute-start(bf16[2,1,1,2,24,6912]{5,4,3,2,1,0:T(8,128)(2,1)} %get-tuple-element.503), channel_id=1, source_target_pairs={{0,4},{1,5},{2,6},{3,7},{4,0},{5,1},{6,2},{7,3},{8,12},{9,13},{10,... | collective-permute-start | bytes 3981320 | tf_op jit(solution)/shard_map/ppermute | solution.py:38
  365.8 41.5 %collective-permute-start.42 = (bf16[512,768]{1,0:T(8,128)(2,1)}, bf16[512,768]{1,0:T(8,128)(2,1)S(1)}, u32[]{:S(2)}, u32[]{:S(2)}) collective-permute-start(bf16[512,768]{1,0:T(8,128)(2,1)} %convolution_convert_fusion.3), channel_id=1, source_target_pairs={{0,1},{1,0},{2,3},{3,2},{4,5},{5,4},{6,7},{7,6},{8,9},{9,8},{10,11... | collective-permute-start | bytes 2359304 | tf_op jit(solution)/shard_map/ppermute | solution.py:38
  410.1 19.8 %collective-permute-start.46 = (bf16[2,1,1,1,24,6912]{5,4,3,2,1,0:T(8,128)(2,1)}, bf16[2,1,1,1,24,6912]{5,4,3,2,1,0:T(8,128)(2,1)}, u32[]{:S(2)}, u32[]{:S(2)}) collective-permute-start(bf16[2,1,1,1,24,6912]{5,4,3,2,1,0:T(8,128)(2,1)} %get-tuple-element.523), channel_id=1, source_target_pairs={{0,4},{1,5},{2,6},{3,7},{4,0},{5,1},{6,2},{7,3},{8,12},{9,13},{10,... | collective-permute-start | bytes 1990664 | tf_op jit(solution)/shard_map/ppermute | solution.py:38
  433.5 43.1 %collective-permute-start.52 = (bf16[2,2,1,1,24,2304]{5,4,3,2,1,0:T(8,128)(2,1)S(1)}, bf16[2,2,1,1,24,2304]{5,4,3,2,1,0:T(8,128)(2,1)S(1)}, u32[]{:S(2)}, u32[]{:S(2)}) collective-permute-start(bf16[2,2,1,1,24,2304]{5,4,3,2,1,0:T(8,128)(2,1)S(1)} %get-tuple-element.531), channel_id=1, source_target_pairs={{0,1},{1,0},{2,3},{3,2},{4,5},{5,4},{6,7},{7,6},{8,9},{9,8},{10,11... | collective-permute-start | bytes 1327112 | tf_op jit(solution)/shard_map/ppermute | solution.py:38
  435.3 41.3 %collective-permute-start.51 = (bf16[2,1,1,2,24,2304]{5,4,3,2,1,0:T(8,128)(2,1)S(1)}, bf16[2,1,1,2,24,2304]{5,4,3,2,1,0:T(8,128)(2,1)S(1)}, u32[]{:S(2)}, u32[]{:S(2)}) collective-permute-start(bf16[2,1,1,2,24,2304]{5,4,3,2,1,0:T(8,128)(2,1)S(1)} %get-tuple-element.533), channel_id=1, source_target_pairs={{0,4},{1,5},{2,6},{3,7},{4,0},{5,1},{6,2},{7,3},{8,12},{9,13},{10,... | collective-permute-start | bytes 1327112 | tf_op jit(solution)/shard_map/ppermute | solution.py:38
  438.8 37.7 %collective-permute-start.48 = (bf16[1,1,1,1,24,6912]{5,4,3,2,1,0:T(8,128)(2,1)S(1)}, bf16[1,1,1,1,24,6912]{5,4,3,2,1,0:T(8,128)(2,1)S(1)}, u32[]{:S(2)}, u32[]{:S(2)}) collective-permute-start(bf16[1,1,1,1,24,6912]{5,4,3,2,1,0:T(8,128)(2,1)S(1)} %get-tuple-element.521), channel_id=1, source_target_pairs={{0,8},{1,9},{2,10},{3,11},{4,12},{5,13},{6,14},{7,15},{8,16},{9,17... | collective-permute-start | bytes 995336 | tf_op jit(solution)/shard_map/ppermute | solution.py:38
  450.9 25.7 %collective-permute-start.49 = (bf16[1,1,1,1,24,6912]{5,4,3,2,1,0:T(8,128)(2,1)S(1)}, bf16[1,1,1,1,24,6912]{5,4,3,2,1,0:T(8,128)(2,1)}, u32[]{:S(2)}, u32[]{:S(2)}) collective-permute-start(bf16[1,1,1,1,24,6912]{5,4,3,2,1,0:T(8,128)(2,1)S(1)} %get-tuple-element.522), channel_id=1, source_target_pairs={{0,16},{1,17},{2,18},{3,19},{4,20},{5,21},{6,22},{7,23},{8,24},{9,... | collective-permute-start | bytes 995336 | tf_op jit(solution)/shard_map/ppermute | solution.py:38
  452.7 23.9 %collective-permute-start.50 = (bf16[1,1,1,1,24,6912]{5,4,3,2,1,0:T(8,128)(2,1)S(1)}, bf16[1,1,1,1,24,6912]{5,4,3,2,1,0:T(8,128)(2,1)}, u32[]{:S(2)}, u32[]{:S(2)}) collective-permute-start(bf16[1,1,1,1,24,6912]{5,4,3,2,1,0:T(8,128)(2,1)S(1)} %get-tuple-element.519), channel_id=1, source_target_pairs={{0,24},{1,25},{2,26},{3,27},{4,28},{5,29},{6,30},{7,31},{8,0},{9,1... | collective-permute-start | bytes 995336 | tf_op jit(solution)/shard_map/ppermute | solution.py:38
  476.6 33.5 %collective-permute-start.55 = (bf16[4,2,1,2,24,6912]{5,4,3,2,1,0:T(8,128)(2,1)}, bf16[4,2,1,2,24,6912]{5,4,3,2,1,0:T(8,128)(2,1)}, u32[]{:S(2)}, u32[]{:S(2)}) collective-permute-start(bf16[4,2,1,2,24,6912]{5,4,3,2,1,0:T(8,128)(2,1)} %bitcast.188), channel_id=1, source_target_pairs={{0,2},{1,3},{2,0},{3,1},{4,6},{5,7},{6,4},{7,5},{8,10},{9,11},{10,... | collective-permute-start | bytes 15925256 | tf_op jit(solution)/shard_map/ppermute | solution.py:38
  482.7 27.4 %collective-permute-start.54 = (bf16[2,1,1,1,24,2304]{5,4,3,2,1,0:T(8,128)(2,1)S(1)}, bf16[2,1,1,1,24,2304]{5,4,3,2,1,0:T(8,128)(2,1)S(1)}, u32[]{:S(2)}, u32[]{:S(2)}) collective-permute-start(bf16[2,1,1,1,24,2304]{5,4,3,2,1,0:T(8,128)(2,1)S(1)} %get-tuple-element.551), channel_id=1, source_target_pairs={{0,4},{1,5},{2,6},{3,7},{4,0},{5,1},{6,2},{7,3},{8,12},{9,13},{10,... | collective-permute-start | bytes 663560 | tf_op jit(solution)/shard_map/ppermute | solution.py:38
  483.6 26.5 %collective-permute-start.53 = (bf16[2,1,1,1,24,2304]{5,4,3,2,1,0:T(8,128)(2,1)S(1)}, bf16[2,1,1,1,24,2304]{5,4,3,2,1,0:T(8,128)(2,1)S(1)}, u32[]{:S(2)}, u32[]{:S(2)}) collective-permute-start(bf16[2,1,1,1,24,2304]{5,4,3,2,1,0:T(8,128)(2,1)S(1)} %get-tuple-element.553), channel_id=1, source_target_pairs={{0,1},{1,0},{2,3},{3,2},{4,5},{5,4},{6,7},{7,6},{8,9},{9,8},{10,11... | collective-permute-start | bytes 663560 | tf_op jit(solution)/shard_map/ppermute | solution.py:38
  517.2 48.0 %collective-permute-start.61 = (bf16[2,2,1,1,24,6912]{5,4,3,2,1,0:T(8,128)(2,1)}, bf16[2,2,1,1,24,6912]{5,4,3,2,1,0:T(8,128)(2,1)}, u32[]{:S(2)}, u32[]{:S(2)}) collective-permute-start(bf16[2,2,1,1,24,6912]{5,4,3,2,1,0:T(8,128)(2,1)} %get-tuple-element.497), channel_id=1, source_target_pairs={{0,1},{1,0},{2,3},{3,2},{4,5},{5,4},{6,7},{7,6},{8,9},{9,8},{10,11... | collective-permute-start | bytes 3981320 | tf_op jit(solution)/shard_map/ppermute | solution.py:38
  520.3 45.0 %collective-permute-start.60 = (bf16[2,1,1,2,24,6912]{5,4,3,2,1,0:T(8,128)(2,1)}, bf16[2,1,1,2,24,6912]{5,4,3,2,1,0:T(8,128)(2,1)}, u32[]{:S(2)}, u32[]{:S(2)}) collective-permute-start(bf16[2,1,1,2,24,6912]{5,4,3,2,1,0:T(8,128)(2,1)} %get-tuple-element.499), channel_id=1, source_target_pairs={{0,4},{1,5},{2,6},{3,7},{4,0},{5,1},{6,2},{7,3},{8,12},{9,13},{10,... | collective-permute-start | bytes 3981320 | tf_op jit(solution)/shard_map/ppermute | solution.py:38
  522.6 21.4 %collective-permute-start.57 = (bf16[1,1,1,1,24,2304]{5,4,3,2,1,0:T(8,128)(2,1)}, bf16[1,1,1,1,24,2304]{5,4,3,2,1,0:T(8,128)(2,1)}, u32[]{:S(2)}, u32[]{:S(2)}) collective-permute-start(bf16[1,1,1,1,24,2304]{5,4,3,2,1,0:T(8,128)(2,1)} %get-tuple-element.549), channel_id=1, source_target_pairs={{0,8},{1,9},{2,10},{3,11},{4,12},{5,13},{6,14},{7,15},{8,16},{9,17... | collective-permute-start | bytes 331784 | tf_op jit(solution)/shard_map/ppermute | solution.py:38
  526.4 19.0 %collective-permute-start.58 = (bf16[1,1,1,1,24,2304]{5,4,3,2,1,0:T(8,128)(2,1)}, bf16[1,1,1,1,24,2304]{5,4,3,2,1,0:T(8,128)(2,1)}, u32[]{:S(2)}, u32[]{:S(2)}) collective-permute-start(bf16[1,1,1,1,24,2304]{5,4,3,2,1,0:T(8,128)(2,1)} %get-tuple-element.550), channel_id=1, source_target_pairs={{0,16},{1,17},{2,18},{3,19},{4,20},{5,21},{6,22},{7,23},{8,24},{9,... | collective-permute-start | bytes 331784 | tf_op jit(solution)/shard_map/ppermute | solution.py:38
  529.9 35.3 %collective-permute-start.56 = (bf16[512,768]{1,0:T(8,128)(2,1)}, bf16[512,768]{1,0:T(8,128)(2,1)S(1)}, u32[]{:S(2)}, u32[]{:S(2)}) collective-permute-start(bf16[512,768]{1,0:T(8,128)(2,1)} %convolution_convert_fusion.2), channel_id=1, source_target_pairs={{0,1},{1,0},{2,3},{3,2},{4,5},{5,4},{6,7},{7,6},{8,9},{9,8},{10,11... | collective-permute-start | bytes 2359304 | tf_op jit(solution)/shard_map/ppermute | solution.py:38
  568.9 17.4 %collective-permute-start.63 = (bf16[2,1,1,1,24,6912]{5,4,3,2,1,0:T(8,128)(2,1)S(1)}, bf16[2,1,1,1,24,6912]{5,4,3,2,1,0:T(8,128)(2,1)S(1)}, u32[]{:S(2)}, u32[]{:S(2)}) collective-permute-start(bf16[2,1,1,1,24,6912]{5,4,3,2,1,0:T(8,128)(2,1)S(1)} %get-tuple-element.515), channel_id=1, source_target_pairs={{0,4},{1,5},{2,6},{3,7},{4,0},{5,1},{6,2},{7,3},{8,12},{9,13},{10,... | collective-permute-start | bytes 1990664 | tf_op jit(solution)/shard_map/ppermute | solution.py:38
  570.4 19.2 %collective-permute-start.64 = (bf16[4,2,1,2,24,2304]{5,4,3,2,1,0:T(8,128)(2,1)S(1)}, bf16[4,2,1,2,24,2304]{5,4,3,2,1,0:T(8,128)(2,1)S(1)}, u32[]{:S(2)}, u32[]{:S(2)}) collective-permute-start(bf16[4,2,1,2,24,2304]{5,4,3,2,1,0:T(8,128)(2,1)S(1)} %bitcast.203), channel_id=1, source_target_pairs={{0,2},{1,3},{2,0},{3,1},{4,6},{5,7},{6,4},{7,5},{8,10},{9,11},{10,... | collective-permute-start | bytes 5308424 | tf_op jit(solution)/shard_map/ppermute | solution.py:38
  572.5 17.0 %collective-permute-start.62 = (bf16[2,1,1,1,24,6912]{5,4,3,2,1,0:T(8,128)(2,1)S(1)}, bf16[2,1,1,1,24,6912]{5,4,3,2,1,0:T(8,128)(2,1)S(1)}, u32[]{:S(2)}, u32[]{:S(2)}) collective-permute-start(bf16[2,1,1,1,24,6912]{5,4,3,2,1,0:T(8,128)(2,1)S(1)} %get-tuple-element.517), channel_id=1, source_target_pairs={{0,1},{1,0},{2,3},{3,2},{4,5},{5,4},{6,7},{7,6},{8,9},{9,8},{10,11... | collective-permute-start | bytes 1990664 | tf_op jit(solution)/shard_map/ppermute | solution.py:38
  592.0 29.1 %collective-permute-start.70 = (bf16[2,2,1,1,24,2304]{5,4,3,2,1,0:T(8,128)(2,1)S(1)}, bf16[2,2,1,1,24,2304]{5,4,3,2,1,0:T(8,128)(2,1)S(1)}, u32[]{:S(2)}, u32[]{:S(2)}) collective-permute-start(bf16[2,2,1,1,24,2304]{5,4,3,2,1,0:T(8,128)(2,1)S(1)} %get-tuple-element.527), channel_id=1, source_target_pairs={{0,1},{1,0},{2,3},{3,2},{4,5},{5,4},{6,7},{7,6},{8,9},{9,8},{10,11... | collective-permute-start | bytes 1327112 | tf_op jit(solution)/shard_map/ppermute | solution.py:38
  592.4 28.7 %collective-permute-start.69 = (bf16[2,1,1,2,24,2304]{5,4,3,2,1,0:T(8,128)(2,1)S(1)}, bf16[2,1,1,2,24,2304]{5,4,3,2,1,0:T(8,128)(2,1)S(1)}, u32[]{:S(2)}, u32[]{:S(2)}) collective-permute-start(bf16[2,1,1,2,24,2304]{5,4,3,2,1,0:T(8,128)(2,1)S(1)} %get-tuple-element.529), channel_id=1, source_target_pairs={{0,4},{1,5},{2,6},{3,7},{4,0},{5,1},{6,2},{7,3},{8,12},{9,13},{10,... | collective-permute-start | bytes 1327112 | tf_op jit(solution)/shard_map/ppermute | solution.py:38
  599.8 21.3 %collective-permute-start.67 = (bf16[1,1,1,1,24,6912]{5,4,3,2,1,0:T(8,128)(2,1)S(1)}, bf16[1,1,1,1,24,6912]{5,4,3,2,1,0:T(8,128)(2,1)S(1)}, u32[]{:S(2)}, u32[]{:S(2)}) collective-permute-start(bf16[1,1,1,1,24,6912]{5,4,3,2,1,0:T(8,128)(2,1)S(1)} %get-tuple-element.514), channel_id=1, source_target_pairs={{0,16},{1,17},{2,18},{3,19},{4,20},{5,21},{6,22},{7,23},{8,24},{9,... | collective-permute-start | bytes 995336 | tf_op jit(solution)/shard_map/ppermute | solution.py:38
  601.0 20.1 %collective-permute-start.68 = (bf16[1,1,1,1,24,6912]{5,4,3,2,1,0:T(8,128)(2,1)S(1)}, bf16[1,1,1,1,24,6912]{5,4,3,2,1,0:T(8,128)(2,1)S(1)}, u32[]{:S(2)}, u32[]{:S(2)}) collective-permute-start(bf16[1,1,1,1,24,6912]{5,4,3,2,1,0:T(8,128)(2,1)S(1)} %get-tuple-element.511), channel_id=1, source_target_pairs={{0,24},{1,25},{2,26},{3,27},{4,28},{5,29},{6,30},{7,31},{8,0},{9,1... | collective-permute-start | bytes 995336 | tf_op jit(solution)/shard_map/ppermute | solution.py:38
  (125 other events, 1377.5 us)

commit v3 on v2

--- a/solution.py
+++ b/solution.py
@@ -28,6 +28,13 @@
     def digits(self):
         clip, seq = lax.axis_index("clip"), lax.axis_index("seq")
         return (clip // 4, (clip // 2) % 2, clip % 2, seq)
+
+    def swap_outer(self, array, bit):
+        flip = self.strides[OUTER] << bit
+        return lax.ppermute(array, AXES, [(place, place ^ flip) for place in range(self.owners)])
+
+    def outer_bits(self):
+        return list(reversed(range(self.outer_size.bit_length() - 1)))
 
     def shift(self, array, axis, amount):
         size, stride = self.sizes[axis], self.strides[axis]
@@ -129,7 +136,6 @@
     ]
     pieces = [part for piece, more in zip(pieces, moved) for part in [piece] + more]
     far = [grid.shift(piece, CORE, 1) for piece in pieces]
-    pieces, far = yield pieces, far
     steps = steps + [[step[:CORE] + (1,) + step[CORE + 1 :] for step in found] for found in steps]
     outs = pl.pallas_call(
         functools.partial(place_kernel, grid, steps, splits),
@@ -180,8 +186,18 @@
     for turn in range(2):
         flying = yield [exchange(grid, part, order[turn]) for part, order in zip(parts, orders)]
         parts = [total_of(*entry).astype(jnp.bfloat16) for entry in flying]
-    kept, arrived = yield exchange(grid, join(parts), OUTER)
-    return total_of(kept, arrived).reshape(kept.shape[-2:])
+    outer = grid.digits()[OUTER]
+    for bit in grid.outer_bits():
+        upper = ((outer >> bit) & 1) == 1
+        low, high = parts
+        kept, sent = jnp.where(upper, high, low), jnp.where(upper, low, high)
+        kept, arrived = yield kept, [grid.swap_outer(sent, bit)]
+        part = total_of(kept, arrived)
+        if bit:
+            part = part.astype(jnp.bfloat16)
+            half = part.shape[0] // 2
+            parts = [part[:half], part[half:]]
+    return part.reshape(part.shape[-2:])
 
 
 def split_columns(rows_first, blocks):
@@ -196,105 +212,200 @@
     )
 
 
-def feed_shares_kernel(
-    grid, normed_ref, before_ref, mixed_ref, branch_ref, active_ref, down_ref, kept_ref, sent_ref
-):
-    step = pl.program_id(0)
+def store_shares(pair, total, low, columns):
     first = lax.axis_index("clip") % 2 == 0
+    for ref, here in zip(pair, (True, False)):
+        part = jnp.where(first == here, total[:, :, 0], total[:, :, 1])
+        part = part.reshape(-1, part.shape[-1]).astype(ref.dtype)
+        ref[pl.ds(low, part.shape[0]), columns] = part
+
+
+def up_shares_kernel(grid, normed_ref, before_ref, mixed_ref, branch_ref, kept, sent, turned):
+    step, ups = pl.program_id(0), pl.num_programs(0) - 1
     outer, _, _, seq = grid.sizes
     width = normed_ref.shape[1]
-    ups = pl.num_programs(0) - 1 - outer
-    rows = width // grid.owners
-
-    def store(total, low, column):
-        for ref, here in ((kept_ref, True), (sent_ref, False)):
-            part = jnp.where(first == here, total[:, :, 0], total[:, :, 1])
-            part = part.reshape(-1, width).astype(ref.dtype)
-            ref[pl.ds(low, part.shape[0]), pl.ds(column, width)] = part
-
-    def by_owner(total):
-        return total.reshape(outer, 2, 2, seq * rows, width)
+    shape = (outer, 2, 2, seq * width // grid.owners, width)
+
+    @pl.when(step == 0)
+    def _():
+        turned[...] = normed_ref[...].T
 
     @pl.when(step < ups)
     def _():
-        column = pl.multiple_of(step * width, 128)
-        store(by_owner(turned_product(normed_ref[...], before_ref[...])), 0, column)
+        total = times(turned[...], before_ref[...]).reshape(shape)
+        store_shares((kept, sent), total, 0, slice(None))
 
     @pl.when(step == ups)
     def _():
-        total = turned_product(mixed_ref[...], branch_ref[...])
-        store(by_owner(total), 0, pl.multiple_of(step * width, 128))
-
-    @pl.when(step > ups)
-    def _():
-        total = turned_product(active_ref[...], down_ref[...])
-        blocks = total.shape[0] // (4 * seq * rows)
-        total = total.reshape(1, 2, 2, seq, blocks, rows, width)
-        line = pl.multiple_of((step - ups - 1) * (2 * seq * rows), 2 * seq * rows)
-        for block in range(blocks):
-            store(
-                total[:, :, :, :, block].reshape(1, 2, 2, seq * rows, width),
-                line,
-                pl.multiple_of((ups + 1 + block) * width, 128),
-            )
-
-
-def feed_shares(grid, normed, before, mixed, branch, active, down):
+        total = turned_product(mixed_ref[...], branch_ref[...]).reshape(shape)
+        store_shares((kept, sent), total, 0, slice(None))
+
+
+def up_shares(grid, normed, before, mixed, branch):
     frames, width = normed.shape
-    units = before.shape[1]
-    blocks, rows = units // width, width // grid.owners
-    columns = 2 * units + width
-    if rows % 8 or grid.outer_size != blocks:
-        up = outer_total(normed, before)
-        out = outer_total(mixed, branch)
-        low = split_columns(outer_total(active, down).reshape(grid.owners, -1, width), blocks)
-        return by_core(grid, jnp.concatenate([up, out, low], axis=1))
+    blocks, rows = before.shape[1] // width, width // grid.owners
+    if rows % 8:
+        total = [outer_total(normed, before), outer_total(mixed, branch)]
+        return by_core(grid, jnp.concatenate(total, axis=1))
+    columns = before.shape[1] + width
     whole = pl.BlockSpec((frames, width), lambda i: (0, 0))
-    half = pl.BlockSpec((width // 2, columns), lambda i: (0, 0))
-    pair = pl.pallas_call(
-        functools.partial(feed_shares_kernel, grid),
-        grid=(2 * blocks + 1,),
+    half = pl.BlockSpec((width // 2, width), lambda i: (0, i))
+    parts = pl.pallas_call(
+        functools.partial(up_shares_kernel, grid),
+        grid=(blocks + 1,),
         in_specs=[
             whole,
             pl.BlockSpec((frames, width), lambda i: (0, jnp.minimum(i, blocks - 1))),
             whole,
             whole,
-            pl.BlockSpec((frames, width), lambda i: (0, jnp.maximum(i - blocks - 1, 0))),
-            whole,
         ],
         out_specs=[half, half],
         out_shape=[jax.ShapeDtypeStruct((width // 2, columns), jnp.bfloat16)] * 2,
+        scratch_shapes=[pltpu.VMEM((width, frames), jnp.bfloat16)],
         compiler_params=pltpu.CompilerParams(vmem_limit_bytes=VMEM_BYTES),
         cost_estimate=QUICK,
-        name="feed_shares",
-    )(normed, before, mixed, branch, active, down)
+        name="up_shares",
+    )(normed, before, mixed, branch)
     shape = (grid.outer_size, 2, 1, grid.seq_size, rows, columns)
-    return [part.reshape(shape) for part in pair]
-
-
-def mixing_shares_kernel(grid, near_ref, far_ref, query_ref, pair_ref, pair_far_ref, *outs):
+    return [part.reshape(shape) for part in parts]
+
+
+def both_shares_kernel(
+    grid, normed_ref, before_ref, mixed_ref, branch_ref, near_ref, far_ref, query_ref, pair_ref,
+    pair_far_ref, kept, sent, turned, turned_far,
+):
+    step, ups = pl.program_id(0), pl.num_programs(0) - 4
+    outer, _, _, seq = grid.sizes
+    width = normed_ref.shape[1]
+    shape = (outer, 2, 2, seq * width // grid.owners, width)
+
+    @pl.when(step == 0)
+    def _():
+        turned[...] = normed_ref[...].T
+
+    @pl.when(step < ups)
+    def _():
+        total = times(turned[...], before_ref[...]).reshape(shape)
+        store_shares((kept, sent), total, 0, slice(None))
+
+    @pl.when(step == ups)
+    def _():
+        total = turned_product(mixed_ref[...], branch_ref[...]).reshape(shape)
+        store_shares((kept, sent), total, 0, slice(None))
+
+    @pl.when(step == ups + 1)
+    def _():
+        turned[...] = near_ref[...].T
+        turned_far[...] = far_ref[...].T
+        total = times(turned[...], query_ref[...]).reshape(shape)
+        store_shares((kept, sent), total, 0, slice(None))
+
+    @pl.when(step > ups + 1)
+    def _():
+        total = times(turned[...], pair_ref[...]) + times(turned_far[...], pair_far_ref[...])
+        store_shares((kept, sent), total.reshape(shape), 0, slice(None))
+
+
+def both_shares(grid, normed, before, mixed, branch, near, far, query, pair, pair_far):
+    frames, width = normed.shape
+    blocks, rows = before.shape[1] // width, width // grid.owners
+    if rows % 8:
+        pairs = zip(
+            up_shares(grid, normed, before, mixed, branch),
+            mixing_shares(grid, near, far, query, pair, pair_far),
+        )
+        return [jnp.concatenate(pair, axis=-1) for pair in pairs]
+    columns = before.shape[1] + 4 * width
+    whole = pl.BlockSpec((frames, width), lambda i: (0, 0))
+    half = pl.BlockSpec((width // 2, width), lambda i: (0, i))
+
+    def late(i):
+        return (0, jnp.maximum(i - blocks - 2, 0))
+
+    parts = pl.pallas_call(
+        functools.partial(both_shares_kernel, grid),
+        grid=(blocks + 4,),
+        in_specs=[
+            whole,
+            pl.BlockSpec((frames, width), lambda i: (0, jnp.minimum(i, blocks - 1))),
+            whole,
+            whole,
+            whole,
+            pl.BlockSpec(far.shape, lambda i: (0, 0)),
+            whole,
+            pl.BlockSpec((frames, width), late),
+            pl.BlockSpec((far.shape[0], width), late),
+        ],
+        out_specs=[half, half],
+        out_shape=[jax.ShapeDtypeStruct((width // 2, columns), jnp.bfloat16)] * 2,
+        scratch_shapes=[
+            pltpu.VMEM((width, frames), jnp.bfloat16),
+            pltpu.VMEM((width, far.shape[0]), jnp.bfloat16),
+        ],
+        compiler_params=pltpu.CompilerParams(vmem_limit_bytes=VMEM_BYTES),
+        cost_estimate=QUICK,
+        name="both_shares",
+    )(normed, before, mixed, branch, near, far, query, pair, pair_far)
+    shape = (grid.outer_size, 2, 1, grid.seq_size, rows, columns)
+    return [part.reshape(shape) for part in parts]
+
+
+def low_shares_kernel(grid, rows, active_ref, down_ref, kept, sent):
+    seq = grid.seq_size
+    width = down_ref.shape[1]
+    total = turned_product(active_ref[...], down_ref[...])
+    blocks = total.shape[0] // (4 * seq * rows)
+    total = total.reshape(1, 2, 2, seq, blocks, rows, width)
+    for block in range(blocks):
+        part = total[:, :, :, :, block].reshape(1, 2, 2, seq * rows, width)
+        store_shares((kept, sent), part, 0, slice(block * width, (block + 1) * width))
+
+
+def low_shares(grid, active, down):
+    frames, width = down.shape
+    units = active.shape[1]
+    blocks, rows = units // width, width // grid.owners
+    if rows % 8:
+        total = outer_total(active, down).reshape(grid.owners, -1, width)
+        return by_core(grid, split_columns(total, blocks))
+    line = units // grid.outer_size
+    half = pl.BlockSpec((width // (2 * grid.outer_size), units), lambda i: (i, 0))
+    parts = pl.pallas_call(
+        functools.partial(low_shares_kernel, grid, rows),
+        grid=(grid.outer_size,),
+        in_specs=[
+            pl.BlockSpec((frames, line), lambda i: (0, i)),
+            pl.BlockSpec((frames, width), lambda i: (0, 0)),
+        ],
+        out_specs=[half, half],
+        out_shape=[jax.ShapeDtypeStruct((width // 2, units), jnp.bfloat16)] * 2,
+        compiler_params=pltpu.CompilerParams(vmem_limit_bytes=VMEM_BYTES),
+        cost_estimate=QUICK,
+        name="low_shares",
+    )(active, down)
+    shape = (grid.outer_size, 2, 1, grid.seq_size, rows, units)
+    return [part.reshape(shape) for part in parts]
+
+
+def mixing_shares_kernel(
+    grid, near_ref, far_ref, query_ref, pair_ref, pair_far_ref, kept, sent, turned, turned_far
+):
     step = pl.program_id(0)
-    first = lax.axis_index("clip") % 2 == 0
     outer, _, _, seq = grid.sizes
     width = near_ref.shape[1]
-    rows = width // grid.owners
-
-    def store(total):
-        total = total.reshape(outer, 2, 2, seq * rows, width)
-        for ref, here in zip(outs, (True, False)):
-            part = jnp.where(first == here, total[:, :, 0], total[:, :, 1])
-            ref[...] = part.reshape(-1, width).astype(ref.dtype)
+    shape = (outer, 2, 2, seq * width // grid.owners, width)
 
     @pl.when(step == 0)
     def _():
-        store(turned_product(near_ref[...], query_ref[...]))
+        turned[...] = near_ref[...].T
+        turned_far[...] = far_ref[...].T
+        total = times(turned[...], query_ref[...]).reshape(shape)
+        store_shares((kept, sent), total, 0, slice(None))
 
     @pl.when(step > 0)
     def _():
-        store(
-            turned_product(near_ref[...], pair_ref[...])
-            + turned_product(far_ref[...], pair_far_ref[...])
-        )
+        total = times(turned[...], pair_ref[...]) + times(turned_far[...], pair_far_ref[...])
+        store_shares((kept, sent), total.reshape(shape), 0, slice(None))
 
 
 def mixing_shares(grid, near, far, query, pair, pair_far):
@@ -323,6 +434,10 @@
         ],
         out_specs=[half, half],
         out_shape=[jax.ShapeDtypeStruct((width // 2, 3 * width), jnp.bfloat16)] * 2,
+        scratch_shapes=[
+            pltpu.VMEM((width, frames), jnp.bfloat16),
+            pltpu.VMEM((width, far.shape[0]), jnp.bfloat16),
+        ],
         compiler_params=pltpu.CompilerParams(vmem_limit_bytes=VMEM_BYTES),
         cost_estimate=QUICK,
         name="mixing_shares",
@@ -558,10 +673,22 @@
 
 def scatter_small(grid, totals):
     place = lax.axis_index("clip") * grid.seq_size + lax.axis_index("seq")
-    whole = jnp.stack([jnp.concatenate(layer) for layer in totals])
-    for axis in (CORE, SEQ, CROSS, OUTER):
+    lengths = [total.shape[0] for total in totals[0]]
+    starts = [sum(lengths[:index]) for index in range(len(lengths) + 1)]
+    whole = sum(
+        jnp.pad(
+            total[None],
+            ((layer, LAYERS - 1 - layer), (starts[index], starts[-1] - starts[index + 1])),
+        )
+        for layer in range(LAYERS)
+        for index, total in enumerate(totals[layer])
+    )
+    for axis in (CORE, SEQ, CROSS):
         whole, moved = yield whole, around(grid, whole, axis)
         whole = sum(moved, whole)
+    for bit in grid.outer_bits():
+        whole, moved = yield whole, grid.swap_outer(whole, bit)
+        whole = whole + moved
     pieces, offset = [], 0
     for total in totals[0]:
         amount = total.shape[0] // grid.owners
@@ -608,16 +735,18 @@
     hidden = traffic.tick(hidden)
     rest = traffic.add(gather_rows(grid, shards[0][1], tuple(behind)))
     normed, normed_far = normal(hidden, *small[0][:2])
-    hidden, normed, normed_far = traffic.tick(hidden, normed, normed_far)
-    hidden, normed, normed_far = traffic.tick(hidden, normed, normed_far)
-    second = traffic.add(
-        gather_rows(grid, jnp.concatenate(shards[1], axis=1), tuple(splits))
-    )
+    last = [jnp.concatenate([shards[1][0], shards[1][1][:, : width + units]], axis=1),
+            params[10][1].astype(jnp.bfloat16)]
+    hidden, normed, normed_far, last = traffic.tick(hidden, normed, normed_far, last)
+    wide, w_last = [lax.all_gather(part, AXES, axis=0, tiled=True) for part in last]
+    second = {"value": [wide[:, start:stop] for start, stop, _ in splits[:-1]] + [w_last]}
     hidden, normed, normed_far = traffic.tick(hidden, normed, normed_far)
     for layer in range(LAYERS):
         g1, s1, bm, bo, g2, s2, bu, bd = small[layer]
         keep = kept[layer]
         if layer == 0:
+            while "value" not in mixing:
+                hidden, normed, normed_far = traffic.tick(hidden, normed, normed_far)
             w_query, w_pair = mixing["value"]
         else:
             while "value" not in second:
@@ -656,7 +785,10 @@
             jnp.bfloat16
         )
         down_bias = column_total(grad_down)
-        grad_hidden, grad_down, grad_before = traffic.tick(grad_hidden, grad_down, grad_before)
+        low = low_shares(grid, keep["active"], grad_down)
+        if layer + 1 < LAYERS:
+            low, grad_hidden, grad_before = traffic.tick(low, grad_hidden, grad_before)
+            low_share = traffic.add(scatter_rows(grid, *low))
         up_bias = column_total(grad_before)
         grad_two = times_transposed(grad_before, keep["w_up"])
         pulled, gain_two, shift_two = normal_back(grad_two, keep["middle"], g2)
@@ -664,24 +796,33 @@
         grad_branch = grad_middle.astype(jnp.bfloat16)
         out_bias = column_total(grad_branch)
         grad_attended = times_transposed(grad_branch, keep["w_out"]).astype(jnp.bfloat16)
-        feed = feed_shares(
-            grid, keep["normed_two"], grad_before, keep["attended"], grad_branch,
-            keep["active"], grad_down,
-        )
-        feed, grad_middle, grad_attended = traffic.tick(feed, grad_middle, grad_attended)
-        feed_share = traffic.add(scatter_rows(grid, *feed))
+        operands = (keep["normed_two"], grad_before, keep["attended"], grad_branch)
+        if layer + 1 < LAYERS:
+            up = up_shares(grid, *operands)
+            up, grad_middle, grad_attended = traffic.tick(up, grad_middle, grad_attended)
+            up_share = traffic.add(scatter_rows(grid, *up))
+        else:
+            low, grad_middle, grad_attended = traffic.tick(low, grad_middle, grad_attended)
+            low_share = traffic.add(scatter_rows(grid, *low))
         grad_query, grad_pair, grad_far = attend_back(
             keep["query"], keep["pair"], keep["pair_far"], keep["logs"], grad_attended
         )
-        grad_query, grad_pair, grad_far = traffic.tick(grad_query, grad_pair, grad_far)
+        grad_query, grad_pair, grad_far, operands = traffic.tick(
+            grad_query, grad_pair, grad_far, operands
+        )
         far = times_transposed(grad_far, keep["w_pair"]).astype(jnp.bfloat16)
         arrived = [
             grid.shift(far[(amount - 1) * rows : amount * rows], SEQ, grid.seq_size - amount)
             for amount in range(1, grid.seq_size)
         ]
-        mixed = mixing_shares(
-            grid, keep["normed"], keep["normed_far"], grad_query, grad_pair, grad_far
-        )
+        far, grad_query, grad_pair, grad_far, operands = lax.optimization_barrier(
+            (far, grad_query, grad_pair, grad_far, operands)
+        )
+        attention = (keep["normed"], keep["normed_far"], grad_query, grad_pair, grad_far)
+        if layer + 1 == LAYERS:
+            mixed = both_shares(grid, *operands, *attention)
+        else:
+            mixed = mixing_shares(grid, *attention)
         mixing_bias = jnp.concatenate(
             [
                 column_total(grad_query),
@@ -691,12 +832,14 @@
         grad_normed = times_transposed(grad_query, keep["w_query"]) + times_transposed(
             grad_pair, keep["w_pair"]
         )
-        mixed, grad_normed, arrived = traffic.tick(mixed, grad_normed, arrived)
-        mixed_share = traffic.add(scatter_rows(grid, *mixed))
         grad_normed = total_of(grad_normed, arrived)
         pulled, gain_one, shift_one = normal_back(grad_normed, keep["hidden"], g1)
         grad_hidden = grad_middle + pulled
-        shares[layer] = (mixed_share, feed_share)
+        mixed, grad_hidden = traffic.tick(mixed, grad_hidden)
+        mixed_share = traffic.add(scatter_rows(grid, *mixed))
+        if layer + 1 == LAYERS:
+            up_share = mixed_share
+        shares[layer] = (mixed_share, up_share, low_share)
         totals[layer] = (
             gain_one, shift_one, mixing_bias, out_bias, gain_two, shift_two, up_bias, down_bias,
         )
@@ -704,11 +847,11 @@
     while traffic.active:
         grad_hidden = traffic.tick(grad_hidden)
     stacked = dict(zip(SMALL, owned["value"]))
-    stacked[2] = jnp.stack([layer[0]["value"] for layer in shares])
-    feeds = [layer[1]["value"] for layer in shares]
-    stacked[4] = jnp.stack([feed[:, units : units + width] for feed in feeds])
-    stacked[8] = jnp.stack([feed[:, :units] for feed in feeds])
-    lows = [feed[:, units + width :].reshape(-1, blocks, width) for feed in feeds]
+    values = [[share["value"] for share in layer] for layer in shares]
+    stacked[2] = jnp.stack([value[0][:, -3 * width :] for value in values])
+    stacked[4] = jnp.stack([value[1][:, units : units + width] for value in values])
+    stacked[8] = jnp.stack([value[1][:, :units] for value in values])
+    lows = [value[2].reshape(-1, blocks, width) for value in values]
     stacked[10] = jnp.stack([jnp.moveaxis(low, 1, 0).reshape(-1, width) for low in lows])
     return tuple(
         [hidden.reshape(frames.shape), grad_hidden.reshape(frames.shape)]

time: 664 us -> 609 us (0.917)
  starting transfers between devices: 121 us -> 72.7 us
  waiting for transfers between devices: 189 us -> 167 us
  Pallas kernels: 167 us -> 153 us
  between operations: 2.86 us -> 16.1 us
  matrix products: 72.9 us -> 83.6 us
    ppermute x81 -> x60, starting transfers between devices: 121 us -> 55.6 us  [shift(): return lax.ppermute(array, AXES, pairs)]
    ppermute x81 -> x60, waiting for transfers between devices: 189 us -> 125 us  [shift(): return lax.ppermute(array, AXES, pairs)]
    ppermute x0 -> x12, waiting for transfers between devices: none -> 37 us  [swap_outer(): lax.ppermute(array, AXES, [(place, place ^ flip) for place in range(self....]
    ppermute x0 -> x12, starting transfers between devices: none -> 16.8 us  [swap_outer(): lax.ppermute(array, AXES, [(place, place ^ flip) for place in range(self....]
    pallas_call x3 -> x2, Pallas kernels: 27.2 us -> 14.4 us  [gather_rows(): pl.pallas_call(functools.partial(place_kernel, grid, steps, splits), out_...]
    unnamed x219 -> x200, local copies, waits for them, and re-layouts: 20.1 us -> 10.5 us
    pallas_call x2 -> x1, Pallas kernels: 14.9 us -> 7.25 us  [mixing_shares(): pl.pallas_call(functools.partial(mixing_shares_kernel, grid), grid=(3,),...]
    pallas_call x2 -> x4, Pallas kernels: 30.3 us -> 37 us  [the longest x2 15 us: low_shares(): pl.pallas_call(functools.partial(low_shares_kernel, grid, rows), grid=(gr...]
  transfers between devices with their start and end apart: 81 -> 74, of which waited for: 31 -> 32; matrix products, arithmetic and copies ran while one was open for 14% -> 21% of each run, Pallas kernels for 18% -> 20%
where the time goes in v3:
time: 609 us; the launch traced here: 602 us
  waiting for transfers between devices  167 us (27%)
  Pallas kernels  153 us (25%)
  matrix products  83.6 us (14%)
  starting transfers between devices  72.7 us (12%)
  other arithmetic  62.2 us (10%)
  local copies, waits for them, and re-layouts  48.4 us (8%)
  between operations  16.1 us (3%)
    ppermute x60, waiting for transfers between devices, shift(): return lax.ppermute(array, AXES, pairs)  125 us
    ppermute x60, starting transfers between devices, shift(): return lax.ppermute(array, AXES, pairs)  55.6 us
    pallas_call x2, Pallas kernels, attend_back(): pl.pallas_call(attend_back_kernel, grid=(blocks,), in_specs=block_specs(f...  45.6 us
    dot_general x12, matrix products, times_transposed(): lax.dot_general(left, right, (((1,), (1,)), ((), ())), preferred_element_...  44.4 us
    dot_general x10, matrix products, times(): lax.dot_general(left, right, (((1,), (0,)), ((), ())), preferred_element_...  39.2 us
    ppermute x12, waiting for transfers between devices, swap_outer(): lax.ppermute(array, AXES, [(place, place ^ flip) for place in range(self....  37 us
    pallas_call x2, Pallas kernels, attend(): pl.pallas_call(attend_kernel, grid=(blocks,), in_specs=block_specs(frames...  28.9 us
    pallas_call x2, Pallas kernels, raise_width(): pl.pallas_call(raise_kernel, grid=(units // tile,), in_specs=[pl.BlockSpe...  19.7 us
  transfers between devices with their start and end apart: 74, of which 32 were waited for; matrix products, arithmetic and copies ran while one was open for 21% of the time, Pallas kernels for 20%

profile of v3, /device:TPU:0, one launch (start us, length us, event | category | flops | bytes accessed | tf_op | source)
XLA Modules:
  0.0 602.3 jit_solution(9268777713679854092)
XLA Ops:
  25.0 3.8 collective-permute-start.2
  48.9 8.8 %collective-permute-done.13 = bf16[1,24,6912]{2,1,0:T(8,128)(2,1)} collective-permute-done((bf16[1,24,6912]{2,1,0:T(8,128)(2,1)S(1)}, bf16[1,24,6912]{2,1,0:T(8,128)(2,1)}, u32[]{:S(2)}, u32[]{:S(2)}) %collective-permute-start.13) | collective-permute-done | bytes 331808 | tf_op jit(solution)/shard_map/ppermute | solution.py:45
  57.7 11.3 %collective-permute-done.11 = bf16[2,24,2304]{2,1,0:T(8,128)(2,1)} collective-permute-done((bf16[2,24,2304]{2,1,0:T(8,128)(2,1)S(1)}, bf16[2,24,2304]{2,1,0:T(8,128)(2,1)}, u32[]{:S(2)}, u32[]{:S(2)}) %collective-permute-start.11) | collective-permute-done | bytes 221216 | tf_op jit(solution)/shard_map/ppermute | solution.py:45
  81.3 5.8 collective-permute-done.15.refs_1_
  87.1 18.2 %collective-permute-done.16.refs_3_ = bf16[4,24,2304]{2,1,0:T(8,128)(2,1)} collective-permute-done((bf16[4,24,2304]{2,1,0:T(8,128)(2,1)S(1)}, bf16[4,24,2304]{2,1,0:T(8,128)(2,1)}, u32[]{:S(2)}, u32[]{:S(2)}) %collective-permute-start.16) | collective-permute-done | bytes 442400 | tf_op jit(solution)/shard_map/ppermute | solution.py:45
  113.9 4.5 place_rows.2
  118.4 4.4 fusion.1.k_ref.v_ref
  122.8 3.8 fusion.2.k_far_ref.v_far_ref
  128.4 14.4 %attend.2 = (bf16[512,768]{1,0:T(8,128)(2,1)}, f32[6,2,512]{2,1,0:T(2,128)}) custom-call(bf16[512,768]{1,0:T(8,128)(2,1)} %add_convert_fusion.11.q_ref, bf16[512,1536]{1,0:T(8,128)(2,1)} %fusion.1.k_ref.v_ref, bf16[512,1536]{1,0:T(8,128)(2,1)} %fusion.1.k_ref.v_ref, bf16[512,1536]{1,0:T(8,128)(2,1)} %fusion.2.k_far_ref.v_far_ref, ...), custom_call_target="tpu_custom_call" | custom-call | flops 1000 | bytes 1000 | tf_op jit(solution)/shard_map/attend/pallas_call | solution.py:544
  142.8 12.8 %collective-permute-done.23.refs_1_ = bf16[4,24,6912]{2,1,0:T(8,128)(2,1)S(1)} collective-permute-done((bf16[4,24,6912]{2,1,0:T(8,128)(2,1)S(1)}, bf16[4,24,6912]{2,1,0:T(8,128)(2,1)S(1)}, u32[]{:S(2)}, u32[]{:S(2)}) %collective-permute-start.23) | collective-permute-done | bytes 1327136 | tf_op jit(solution)/shard_map/ppermute | solution.py:45
  155.6 4.0 collective-permute-done.24.refs_3_
  162.7 5.7 collective-permute-done.26.refs_5_
  172.2 9.9 %place_rows.3 = (bf16[32,24,768]{2,1,0:T(8,128)(2,1)}, bf16[32,24,3072]{2,1,0:T(8,128)(2,1)}, bf16[128,24,768]{2,1,0:T(8,128)(2,1)}) custom-call(bf16[4,24,6912]{2,1,0:T(8,128)(2,1)} %copy-done.26, bf16[4,24,6912]{2,1,0:T(8,128)(2,1)} %copy-done.35, bf16[4,24,6912]{2,1,0:T(8,128)(2,1)} %copy-done.27, bf16[4,24,6912]{2,1,0:T(8,128)(2,1)} %collective-permute-done.24.refs_3_, ...), custom_call_target="tpu_custom_call" | custom-call | flops 1000 | bytes 1000 | tf_op jit(solution)/shard_map/place_rows/pallas_call | solution.py:140
  186.4 10.0 %raise_width.2 = (bf16[512,3072]{1,0:T(8,128)(2,1)}, f32[512,3072]{1,0:T(8,128)}) custom-call(bf16[512,768]{1,0:T(8,128)(2,1)} %add_convert_fusion.10.left_ref.normed_ref, bf16[768,3072]{1,0:T(8,128)(2,1)} %bitcast.136, f32[1,3072]{1,0:T(1,128)} %get-tuple-element.532.bias_ref), custom_call_target="tpu_custom_call" | custom-call | flops 1000 | bytes 1000 | tf_op jit(solution)/shard_map/raise_width/pallas_call | solution.py:620
  196.5 6.1 %fusion.36 = (f32[512]{0:T(512)S(1)}, f32[512,768]{1,0:T(8,128)S(1)}) fusion(f32[512,768]{1,0:T(8,128)S(1)} %get-tuple-element.536, f32[768]{0:T(1024)S(1)} %copy-done.78, bf16[512,3072]{1,0:T(8,128)(2,1)} %get-tuple-element.255.active_ref, bf16[3072,768]{1,0:T(8,128)(2,1)} %bitcast.160), kind=kOutput, calls=%fused_computation.272 | convolution fusion | flops 2417098240 | bytes 11015168 | tf_op jit(solution)/shard_map/dot_general | solution.py:462
  206.3 3.2 add_convert_fusion.8.q_ref
  209.5 4.4 fusion.3.k_ref.v_ref
  213.9 16.4 %collective-permute-done.29.far_ref = bf16[512,768]{1,0:T(8,128)(2,1)} collective-permute-done((bf16[512,768]{1,0:T(8,128)(2,1)}, bf16[512,768]{1,0:T(8,128)(2,1)}, u32[]{:S(2)}, u32[]{:S(2)}) %collective-permute-start.29) | collective-permute-done | bytes 786464 | tf_op jit(solution)/shard_map/ppermute | solution.py:45
  230.4 4.5 fusion.4.k_far_ref.v_far_ref
  234.9 4.8 all-gather.5.cloned.1.call-done
  239.7 7.8 %fusion.38 = f32[3072,512]{0,1:T(8,128)} fusion(bf16[3072,768]{1,0:T(8,128)(2,1)} %all-gather.5.cloned.1.call-done, bf16[512,768]{1,0:T(8,128)(2,1)} %get-tuple-element.447.down_ref), kind=kOutput, calls=%fused_computation.274 | convolution fusion | flops 2415919104 | bytes 11796480 | tf_op jit(solution)/shard_map/dot_general | solution.py:456
  247.5 14.4 %attend.3 = (bf16[512,768]{1,0:T(8,128)(2,1)}, f32[6,2,512]{2,1,0:T(2,128)}) custom-call(bf16[512,768]{1,0:T(8,128)(2,1)} %add_convert_fusion.8.q_ref, bf16[512,1536]{1,0:T(8,128)(2,1)} %fusion.3.k_ref.v_ref, bf16[512,1536]{1,0:T(8,128)(2,1)} %fusion.3.k_ref.v_ref, bf16[512,1536]{1,0:T(8,128)(2,1)} %fusion.4.k_far_ref.v_far_ref, ...), custom_call_target="tpu_custom_call" | custom-call | flops 1000 | bytes 1000 | tf_op jit(solution)/shard_map/attend/pallas_call | solution.py:544
  265.8 4.8 slice.287.right_ref
  270.6 9.8 %raise_width.3 = (bf16[512,3072]{1,0:T(8,128)(2,1)}, f32[512,3072]{1,0:T(8,128)}) custom-call(bf16[512,768]{1,0:T(8,128)(2,1)} %add_convert_fusion.7.left_ref.normed_ref, bf16[768,3072]{1,0:T(8,128)(2,1)} %slice.287.right_ref, f32[1,3072]{1,0:T(1,128)} %get-tuple-element.531.bias_ref), custom_call_target="tpu_custom_call" | custom-call | flops 1000 | bytes 1000 | tf_op jit(solution)/shard_map/raise_width/pallas_call | solution.py:620
  280.4 6.9 %low_shares.2 = (bf16[384,3072]{1,0:T(8,128)(2,1)}, bf16[384,3072]{1,0:T(8,128)(2,1)}) custom-call(bf16[512,3072]{1,0:T(8,128)(2,1)} %get-tuple-element.259.active_ref, bf16[512,768]{1,0:T(8,128)(2,1)} %get-tuple-element.447.down_ref), custom_call_target="tpu_custom_call" | custom-call | flops 1000 | bytes 1000 | tf_op jit(solution)/shard_map/low_shares/pallas_call | solution.py:373
  287.3 6.1 %convert_reduce_fusion = (f32[3072]{0:T(1024)S(1)}, bf16[512,3072]{1,0:T(8,128)(2,1)S(1)}) fusion(f32[512,3072]{1,0:T(8,128)} %get-tuple-element.265, f32[3072,512]{0,1:T(8,128)} %fusion.38), kind=kLoop, calls=%fused_computation.3 | loop fusion | flops 6288384 | bytes 15740928 | tf_op jit(solution)/shard_map/reduce_sum | solution.py:646
  293.4 6.5 %multiply_reduce_fusion = (f32[768]{0:T(1024)S(1)}, f32[512]{0:T(512)S(1)}, f32[512]{0:T(512)S(1)}, f32[768]{0:T(1024)S(1)}, f32[512,768]{1,0:T(8,128)S(1)}) fusion(f32[512,768]{1,0:T(8,128)S(1)} %get-tuple-element.540, f32[512]{0:T(512)S(1)} %add_rsqrt_fusion.1, f32[512]{0:T(512)S(1)} %broadcast_multiply_fusion.9, f32[768]{0:T(1024)S(1)} %get-tuple-element.422, ...), kind=kOutput, calls=%fused_computation.23 | convolution fusion | flops 2419455488 | bytes 11027456 | tf_op jit(solution)/shard_map/dot_general | solution.py:456
  301.7 3.3 convolution_convert_fusion.1.g_ref
  305.4 22.7 %attend_back.2 = (bf16[512,768]{1,0:T(8,128)(2,1)}, bf16[512,1536]{1,0:T(8,128)(2,1)}, bf16[512,1536]{1,0:T(8,128)(2,1)}) custom-call(bf16[512,768]{1,0:T(8,128)(2,1)} %add_convert_fusion.8.q_ref, bf16[512,1536]{1,0:T(8,128)(2,1)} %fusion.3.k_ref.v_ref, bf16[512,1536]{1,0:T(8,128)(2,1)} %fusion.3.k_ref.v_ref, bf16[512,1536]{1,0:T(8,128)(2,1)} %fusion.4.k_far_ref.v_far_ref, ...), custom_call_target="tpu_custom_call" | custom-call | flops 1000 | bytes 1000 | tf_op jit(solution)/shard_map/attend_back/pallas_call | solution.py:565
  328.1 4.6 fusion.11
  340.2 13.6 %both_shares.1 = (bf16[384,6144]{1,0:T(8,128)(2,1)}, bf16[384,6144]{1,0:T(8,128)(2,1)}) custom-call(bf16[512,768]{1,0:T(8,128)(2,1)} %add_convert_fusion.7.left_ref.normed_ref, bf16[512,3072]{1,0:T(8,128)(2,1)} %copy-done.7, bf16[512,768]{1,0:T(8,128)(2,1)} %get-tuple-element.281.mixed_ref, bf16[512,768]{1,0:T(8,128)(2,1)} %copy-done.23, ...), custom_call_target="tpu_custom_call" | custom-call | flops 1000 | bytes 1000 | tf_op jit(solution)/shard_map/both_shares/pallas_call | solution.py:325
  356.1 3.2 fusion.5
  366.9 6.3 %add_bitcast_fusion = f32[1,512,768]{2,1,0:T(8,128)} fusion(f32[512,768]{1,0:T(8,128)S(1)} %copy-done.4, bf16[512,3072]{1,0:T(8,128)(2,1)S(1)} %copy-done.19, bf16[3072,768]{1,0:T(8,128)(2,1)} %all-gather.5.cloned.1.call-done, f32[768]{0:T(1024)S(1)} %copy-done.75), kind=kOutput, calls=%fused_computation.46 | convolution fusion | flops 2416705536 | bytes 11013120 | tf_op jit(solution)/shard_map/dot_general | solution.py:462
  381.7 8.1 %low_shares.3 = (bf16[384,3072]{1,0:T(8,128)(2,1)}, bf16[384,3072]{1,0:T(8,128)(2,1)}) custom-call(bf16[512,3072]{1,0:T(8,128)(2,1)} %get-tuple-element.255.active_ref, bf16[512,768]{1,0:T(8,128)(2,1)} %copy-done.22), custom_call_target="tpu_custom_call" | custom-call | flops 1000 | bytes 1000 | tf_op jit(solution)/shard_map/low_shares/pallas_call | solution.py:373
  389.8 5.6 add_convert_fusion
  401.9 3.6 multiply_reduce_fusion.2
  406.6 3.2 collective-permute-start.37
  411.4 8.4 %up_shares.1 = (bf16[384,3840]{1,0:T(8,128)(2,1)}, bf16[384,3840]{1,0:T(8,128)(2,1)}) custom-call(bf16[512,768]{1,0:T(8,128)(2,1)} %add_convert_fusion.10.left_ref.normed_ref, bf16[512,3072]{1,0:T(8,128)(2,1)} %copy-done.5, bf16[512,768]{1,0:T(8,128)(2,1)} %get-tuple-element.248.mixed_ref, bf16[512,768]{1,0:T(8,128)(2,1)} %get-tuple-element.437.branch_ref), custom_call_target="tpu_custom_call" | custom-call | flops 1000 | bytes 1000 | tf_op jit(solution)/shard_map/up_shares/pallas_call | solution.py:253
  447.4 22.9 %attend_back.3 = (bf16[512,768]{1,0:T(8,128)(2,1)}, bf16[512,1536]{1,0:T(8,128)(2,1)}, bf16[512,1536]{1,0:T(8,128)(2,1)}) custom-call(bf16[512,768]{1,0:T(8,128)(2,1)} %add_convert_fusion.11.q_ref, bf16[512,1536]{1,0:T(8,128)(2,1)} %fusion.1.k_ref.v_ref, bf16[512,1536]{1,0:T(8,128)(2,1)} %fusion.1.k_ref.v_ref, bf16[512,1536]{1,0:T(8,128)(2,1)} %fusion.2.k_far_ref.v_far_ref, ...), custom_call_target="tpu_custom_call" | custom-call | flops 1000 | bytes 1000 | tf_op jit(solution)/shard_map/attend_back/pallas_call | solution.py:565
  470.4 4.7 convolution_convert_fusion.2
  476.7 7.3 %mixing_shares.1 = (bf16[384,2304]{1,0:T(8,128)(2,1)}, bf16[384,2304]{1,0:T(8,128)(2,1)}) custom-call(bf16[512,768]{1,0:T(8,128)(2,1)} %copy-done.21, bf16[512,768]{1,0:T(8,128)(2,1)} %collective-permute-done.9.far_ref, bf16[512,768]{1,0:T(8,128)(2,1)} %get-tuple-element.330.query_ref, bf16[512,1536]{1,0:T(8,128)(2,1)} %get-tuple-element.331.pair_ref, ...), custom_call_target="tpu_custom_call" | custom-call | flops 1000 | bytes 1000 | tf_op jit(solution)/shard_map/mixing_shares/pallas_call | solution.py:425
  502.0 12.1 %collective-permute-done.48 = bf16[2,1,1,1,24,6144]{5,4,3,2,1,0:T(8,128)(2,1)S(1)} collective-permute-done((bf16[2,1,1,1,24,6144]{5,4,3,2,1,0:T(8,128)(2,1)S(1)}, bf16[2,1,1,1,24,6144]{5,4,3,2,1,0:T(8,128)(2,1)S(1)}, u32[]{:S(2)}, u32[]{:S(2)}) %collective-permute-start.48) | collective-permute-done | bytes 589856 | tf_op jit(solution)/shard_map/ppermute | solution.py:34
  530.9 3.6 collective-permute-done.54
  534.5 4.8 collective-permute-done.56
  550.1 7.3 %collective-permute-done.63 = f32[2,9216]{1,0:T(2,128)S(1)} collective-permute-done((f32[2,9216]{1,0:T(2,128)S(1)}, f32[2,9216]{1,0:T(2,128)S(1)}, u32[]{:S(2)}, u32[]{:S(2)}) %collective-permute-start.63) | collective-permute-done | bytes 73760 | tf_op jit(solution)/shard_map/ppermute | solution.py:45
  557.5 4.0 collective-permute-done.60
  566.1 5.4 collective-permute-done.67
  575.7 11.0 %collective-permute-done.69 = f32[2,9216]{1,0:T(2,128)S(1)} collective-permute-done((f32[2,9216]{1,0:T(2,128)S(1)}, f32[2,9216]{1,0:T(2,128)S(1)}, u32[]{:S(2)}, u32[]{:S(2)}) %collective-permute-start.69) | collective-permute-done | bytes 73760 | tf_op jit(solution)/shard_map/ppermute | solution.py:34
  (536 shorter events, 207.6 us)
Async XLA Ops:
  7.2 199.1 %all-gather.3.cloned.1.call-start = ((), (), s32[]{:S(2)}) async-start(), calls=%async_computation | async-start | bytes 9732096 | tf_op jit(solution)/shard_map/all_gather | solution.py:741
  8.4 27.0 %collective-permute-start = (bf16[1,24,2304]{2,1,0:T(8,128)(2,1)S(1)}, bf16[1,24,2304]{2,1,0:T(8,128)(2,1)S(1)}, u32[]{:S(2)}, u32[]{:S(2)}) collective-permute-start(bf16[1,24,2304]{2,1,0:T(8,128)(2,1)S(1)} %bitcast.152), channel_id=1, source_target_pairs={{0,8},{1,9},{2,10},{3,11},{4,12},{5,13},{6,14},{7,15},{8,16},{9,17... | collective-permute-start | bytes 331784 | tf_op jit(solution)/shard_map/ppermute | solution.py:45
  11.5 25.0 %collective-permute-start.1 = (bf16[1,24,2304]{2,1,0:T(8,128)(2,1)S(1)}, bf16[1,24,2304]{2,1,0:T(8,128)(2,1)}, u32[]{:S(2)}, u32[]{:S(2)}) collective-permute-start(bf16[1,24,2304]{2,1,0:T(8,128)(2,1)S(1)} %bitcast.153), channel_id=1, source_target_pairs={{0,16},{1,17},{2,18},{3,19},{4,20},{5,21},{6,22},{7,23},{8,24},{9,... | collective-permute-start | bytes 331784 | tf_op jit(solution)/shard_map/ppermute | solution.py:45
  25.0 14.3 %collective-permute-start.2 = (bf16[1,24,2304]{2,1,0:T(8,128)(2,1)S(1)}, bf16[1,24,2304]{2,1,0:T(8,128)(2,1)S(1)}, u32[]{:S(2)}, u32[]{:S(2)}) collective-permute-start(bf16[1,24,2304]{2,1,0:T(8,128)(2,1)S(1)} %bitcast.154), channel_id=1, source_target_pairs={{0,24},{1,25},{2,26},{3,27},{4,28},{5,29},{6,30},{7,31},{8,0},{9,1... | collective-permute-start | bytes 331784 | tf_op jit(solution)/shard_map/ppermute | solution.py:45
  35.3 12.7 %collective-permute-start.12 = (bf16[1,24,6912]{2,1,0:T(8,128)(2,1)S(1)}, bf16[1,24,6912]{2,1,0:T(8,128)(2,1)}, u32[]{:S(2)}, u32[]{:S(2)}) collective-permute-start(bf16[1,24,6912]{2,1,0:T(8,128)(2,1)S(1)} %maximum_bitcast_fusion), channel_id=1, source_target_pairs={{0,8},{1,9},{2,10},{3,11},{4,12},{5,13},{6,14},{7,15},{8,16},{9,17... | collective-permute-start | bytes 995336 | tf_op jit(solution)/shard_map/ppermute | solution.py:45
  35.4 22.3 %collective-permute-start.13 = (bf16[1,24,6912]{2,1,0:T(8,128)(2,1)S(1)}, bf16[1,24,6912]{2,1,0:T(8,128)(2,1)}, u32[]{:S(2)}, u32[]{:S(2)}) collective-permute-start(bf16[1,24,6912]{2,1,0:T(8,128)(2,1)S(1)} %maximum_bitcast_fusion), channel_id=1, source_target_pairs={{0,16},{1,17},{2,18},{3,19},{4,20},{5,21},{6,22},{7,23},{8,24},{9,... | collective-permute-start | bytes 995336 | tf_op jit(solution)/shard_map/ppermute | solution.py:45
  36.5 21.2 %collective-permute-start.14 = (bf16[1,24,6912]{2,1,0:T(8,128)(2,1)S(1)}, bf16[1,24,6912]{2,1,0:T(8,128)(2,1)}, u32[]{:S(2)}, u32[]{:S(2)}) collective-permute-start(bf16[1,24,6912]{2,1,0:T(8,128)(2,1)S(1)} %maximum_bitcast_fusion), channel_id=1, source_target_pairs={{0,24},{1,25},{2,26},{3,27},{4,28},{5,29},{6,30},{7,31},{8,0},{9,1... | collective-permute-start | bytes 995336 | tf_op jit(solution)/shard_map/ppermute | solution.py:45
  42.1 15.6 %collective-permute-start.10 = (bf16[2,24,2304]{2,1,0:T(8,128)(2,1)S(1)}, bf16[2,24,2304]{2,1,0:T(8,128)(2,1)}, u32[]{:S(2)}, u32[]{:S(2)}) collective-permute-start(bf16[2,24,2304]{2,1,0:T(8,128)(2,1)S(1)} %constant_dynamic-update-slice_fusion.8), channel_id=1, source_target_pairs={{0,4},{1,5},{2,6},{3,7},{4,0},{5,1},{6,2},{7,3},{8,12},{9,13},{10,... | collective-permute-start | bytes 663560 | tf_op jit(solution)/shard_map/ppermute | solution.py:45
  44.8 24.3 %collective-permute-start.9 = (bf16[512,768]{1,0:T(8,128)(2,1)S(1)}, bf16[512,768]{1,0:T(8,128)(2,1)}, u32[]{:S(2)}, u32[]{:S(2)}) collective-permute-start(bf16[512,768]{1,0:T(8,128)(2,1)S(1)} %add_convert_fusion.12.near_ref), channel_id=1, source_target_pairs={{0,1},{1,0},{2,3},{3,2},{4,5},{5,4},{6,7},{7,6},{8,9},{9,8},{10,11... | collective-permute-start | bytes 2359304 | tf_op jit(solution)/shard_map/ppermute | solution.py:45
  48.1 20.9 %collective-permute-start.11 = (bf16[2,24,2304]{2,1,0:T(8,128)(2,1)S(1)}, bf16[2,24,2304]{2,1,0:T(8,128)(2,1)}, u32[]{:S(2)}, u32[]{:S(2)}) collective-permute-start(bf16[2,24,2304]{2,1,0:T(8,128)(2,1)S(1)} %constant_dynamic-update-slice_fusion.10), channel_id=1, source_target_pairs={{0,1},{1,0},{2,3},{3,2},{4,5},{5,4},{6,7},{7,6},{8,9},{9,8},{10,11... | collective-permute-start | bytes 663560 | tf_op jit(solution)/shard_map/ppermute | solution.py:45
  69.0 170.6 %all-gather.5.cloned.1.call-start = ((), (), s32[]{:S(2)}) async-start(), calls=%async_computation.1 | async-start | bytes 4866048 | tf_op jit(solution)/shard_map/all_gather | solution.py:741
  71.6 15.5 %collective-permute-start.15 = (bf16[4,24,2304]{2,1,0:T(8,128)(2,1)}, bf16[4,24,2304]{2,1,0:T(8,128)(2,1)}, u32[]{:S(2)}, u32[]{:S(2)}) collective-permute-start(bf16[4,24,2304]{2,1,0:T(8,128)(2,1)} %constant_dynamic-update-slice_fusion.12.refs_0_), channel_id=1, source_target_pairs={{0,1},{1,0},{2,3},{3,2},{4,5},{5,4},{6,7},{7,6},{8,9},{9,8},{10,11... | collective-permute-start | bytes 1327112 | tf_op jit(solution)/shard_map/ppermute | solution.py:45
  73.1 32.2 %collective-permute-start.17 = (bf16[2,24,6912]{2,1,0:T(8,128)(2,1)S(1)}, bf16[2,24,6912]{2,1,0:T(8,128)(2,1)}, u32[]{:S(2)}, u32[]{:S(2)}) collective-permute-start(bf16[2,24,6912]{2,1,0:T(8,128)(2,1)S(1)} %constant_dynamic-update-slice_fusion.16), channel_id=1, source_target_pairs={{0,4},{1,5},{2,6},{3,7},{4,0},{5,1},{6,2},{7,3},{8,12},{9,13},{10,... | collective-permute-start | bytes 1990664 | tf_op jit(solution)/shard_map/ppermute | solution.py:45
  77.0 28.3 %collective-permute-start.18 = (bf16[2,24,6912]{2,1,0:T(8,128)(2,1)}, bf16[2,24,6912]{2,1,0:T(8,128)(2,1)}, u32[]{:S(2)}, u32[]{:S(2)}) collective-permute-start(bf16[2,24,6912]{2,1,0:T(8,128)(2,1)} %constant_dynamic-update-slice_fusion.18), channel_id=1, source_target_pairs={{0,1},{1,0},{2,3},{3,2},{4,5},{5,4},{6,7},{7,6},{8,9},{9,8},{10,11... | collective-permute-start | bytes 1990664 | tf_op jit(solution)/shard_map/ppermute | solution.py:45
  79.8 25.6 %collective-permute-start.16 = (bf16[4,24,2304]{2,1,0:T(8,128)(2,1)S(1)}, bf16[4,24,2304]{2,1,0:T(8,128)(2,1)}, u32[]{:S(2)}, u32[]{:S(2)}) collective-permute-start(bf16[4,24,2304]{2,1,0:T(8,128)(2,1)S(1)} %constant_dynamic-update-slice_fusion.14.refs_2_), channel_id=1, source_target_pairs={{0,4},{1,5},{2,6},{3,7},{4,0},{5,1},{6,2},{7,3},{8,12},{9,13},{10,... | collective-permute-start | bytes 1327112 | tf_op jit(solution)/shard_map/ppermute | solution.py:45
  107.5 48.1 %collective-permute-start.23 = (bf16[4,24,6912]{2,1,0:T(8,128)(2,1)S(1)}, bf16[4,24,6912]{2,1,0:T(8,128)(2,1)S(1)}, u32[]{:S(2)}, u32[]{:S(2)}) collective-permute-start(bf16[4,24,6912]{2,1,0:T(8,128)(2,1)S(1)} %constant_dynamic-update-slice_fusion.20.refs_0_), channel_id=1, source_target_pairs={{0,1},{1,0},{2,3},{3,2},{4,5},{5,4},{6,7},{7,6},{8,9},{9,8},{10,11... | collective-permute-start | bytes 3981320 | tf_op jit(solution)/shard_map/ppermute | solution.py:45
  111.8 47.8 %collective-permute-start.24 = (bf16[4,24,6912]{2,1,0:T(8,128)(2,1)S(1)}, bf16[4,24,6912]{2,1,0:T(8,128)(2,1)}, u32[]{:S(2)}, u32[]{:S(2)}) collective-permute-start(bf16[4,24,6912]{2,1,0:T(8,128)(2,1)S(1)} %constant_dynamic-update-slice_fusion.22.refs_2_), channel_id=1, source_target_pairs={{0,4},{1,5},{2,6},{3,7},{4,0},{5,1},{6,2},{7,3},{8,12},{9,13},{10,... | collective-permute-start | bytes 3981320 | tf_op jit(solution)/shard_map/ppermute | solution.py:45
  204.4 25.9 %collective-permute-start.29 = (bf16[512,768]{1,0:T(8,128)(2,1)}, bf16[512,768]{1,0:T(8,128)(2,1)}, u32[]{:S(2)}, u32[]{:S(2)}) collective-permute-start(bf16[512,768]{1,0:T(8,128)(2,1)} %add_convert_fusion.9.near_ref), channel_id=1, source_target_pairs={{0,1},{1,0},{2,3},{3,2},{4,5},{5,4},{6,7},{7,6},{8,9},{9,8},{10,11... | collective-permute-start | bytes 2359304 | tf_op jit(solution)/shard_map/ppermute | solution.py:45
  304.9 23.2 %collective-permute-start.30 = (bf16[4,2,1,2,24,3072]{5,4,3,1,0,2:T(8,128)(2,1)}, bf16[4,2,1,2,24,3072]{5,4,3,1,0,2:T(8,128)(2,1)}, u32[]{:S(2)}, u32[]{:S(2)}) collective-permute-start(bf16[4,2,1,2,24,3072]{5,4,3,1,0,2:T(8,128)(2,1)} %bitcast.20), channel_id=1, source_target_pairs={{0,2},{1,3},{2,0},{3,1},{4,6},{5,7},{6,4},{7,5},{8,10},{9,11},{10,... | collective-permute-start | bytes 7077896 | tf_op jit(solution)/shard_map/ppermute | solution.py:45
  332.7 26.6 %collective-permute-start.31 = (bf16[512,768]{1,0:T(8,128)(2,1)}, bf16[512,768]{1,0:T(8,128)(2,1)}, u32[]{:S(2)}, u32[]{:S(2)}) collective-permute-start(bf16[512,768]{1,0:T(8,128)(2,1)} %fusion.11), channel_id=1, source_target_pairs={{0,1},{1,0},{2,3},{3,2},{4,5},{5,4},{6,7},{7,6},{8,9},{9,8},{10,11... | collective-permute-start | bytes 2359304 | tf_op jit(solution)/shard_map/ppermute | solution.py:45
  337.4 24.8 %collective-permute-start.32 = (bf16[2,1,1,2,24,3072]{5,4,3,1,0,2:T(8,128)(2,1)}, bf16[2,1,1,2,24,3072]{5,4,3,1,0,2:T(8,128)(2,1)}, u32[]{:S(2)}, u32[]{:S(2)}) collective-permute-start(bf16[2,1,1,2,24,3072]{5,4,3,1,0,2:T(8,128)(2,1)} %get-tuple-element.485), channel_id=1, source_target_pairs={{0,4},{1,5},{2,6},{3,7},{4,0},{5,1},{6,2},{7,3},{8,12},{9,13},{10,... | collective-permute-start | bytes 1769480 | tf_op jit(solution)/shard_map/ppermute | solution.py:45
  338.7 26.6 %collective-permute-start.33 = (bf16[2,2,1,1,24,3072]{5,4,3,1,0,2:T(8,128)(2,1)}, bf16[2,2,1,1,24,3072]{5,4,3,1,0,2:T(8,128)(2,1)}, u32[]{:S(2)}, u32[]{:S(2)}) collective-permute-start(bf16[2,2,1,1,24,3072]{5,4,3,1,0,2:T(8,128)(2,1)} %get-tuple-element.483), channel_id=1, source_target_pairs={{0,1},{1,0},{2,3},{3,2},{4,5},{5,4},{6,7},{7,6},{8,9},{9,8},{10,11... | collective-permute-start | bytes 1769480 | tf_op jit(solution)/shard_map/ppermute | solution.py:45
  365.4 24.4 %collective-permute-start.36 = (bf16[4,2,1,2,24,6144]{5,4,3,2,1,0:T(8,128)(2,1)}, bf16[4,2,1,2,24,6144]{5,4,3,2,1,0:T(8,128)(2,1)}, u32[]{:S(2)}, u32[]{:S(2)}) collective-permute-start(bf16[4,2,1,2,24,6144]{5,4,3,2,1,0:T(8,128)(2,1)} %bitcast.26), channel_id=1, source_target_pairs={{0,2},{1,3},{2,0},{3,1},{4,6},{5,7},{6,4},{7,5},{8,10},{9,11},{10,... | collective-permute-start | bytes 14155784 | tf_op jit(solution)/shard_map/ppermute | solution.py:45
  375.3 14.5 %collective-permute-start.34 = (bf16[2,1,1,1,24,3072]{5,4,3,1,0,2:T(8,128)(2,1)}, bf16[2,1,1,1,24,3072]{5,4,3,1,0,2:T(8,128)(2,1)}, u32[]{:S(2)}, u32[]{:S(2)}) collective-permute-start(bf16[2,1,1,1,24,3072]{5,4,3,1,0,2:T(8,128)(2,1)} %get-tuple-element.505), channel_id=1, source_target_pairs={{0,1},{1,0},{2,3},{3,2},{4,5},{5,4},{6,7},{7,6},{8,9},{9,8},{10,11... | collective-permute-start | bytes 884744 | tf_op jit(solution)/shard_map/ppermute | solution.py:45
  397.5 28.1 %collective-permute-start.38 = (bf16[2,1,1,2,24,6144]{5,4,3,2,1,0:T(8,128)(2,1)}, bf16[2,1,1,2,24,6144]{5,4,3,2,1,0:T(8,128)(2,1)}, u32[]{:S(2)}, u32[]{:S(2)}) collective-permute-start(bf16[2,1,1,2,24,6144]{5,4,3,2,1,0:T(8,128)(2,1)} %get-tuple-element.459), channel_id=1, source_target_pairs={{0,4},{1,5},{2,6},{3,7},{4,0},{5,1},{6,2},{7,3},{8,12},{9,13},{10,... | collective-permute-start | bytes 3538952 | tf_op jit(solution)/shard_map/ppermute | solution.py:45
  400.6 27.9 %collective-permute-start.39 = (bf16[2,2,1,1,24,6144]{5,4,3,2,1,0:T(8,128)(2,1)}, bf16[2,2,1,1,24,6144]{5,4,3,2,1,0:T(8,128)(2,1)}, u32[]{:S(2)}, u32[]{:S(2)}) collective-permute-start(bf16[2,2,1,1,24,6144]{5,4,3,2,1,0:T(8,128)(2,1)} %get-tuple-element.457), channel_id=1, source_target_pairs={{0,1},{1,0},{2,3},{3,2},{4,5},{5,4},{6,7},{7,6},{8,9},{9,8},{10,11... | collective-permute-start | bytes 3538952 | tf_op jit(solution)/shard_map/ppermute | solution.py:45
  401.8 26.7 %collective-permute-start.40 = (bf16[4,2,1,2,24,3072]{5,4,3,1,0,2:T(8,128)(2,1)}, bf16[4,2,1,2,24,3072]{5,4,3,1,0,2:T(8,128)(2,1)}, u32[]{:S(2)}, u32[]{:S(2)}) collective-permute-start(bf16[4,2,1,2,24,3072]{5,4,3,1,0,2:T(8,128)(2,1)} %bitcast.25), channel_id=1, source_target_pairs={{0,2},{1,3},{2,0},{3,1},{4,6},{5,7},{6,4},{7,5},{8,10},{9,11},{10,... | collective-permute-start | bytes 7077896 | tf_op jit(solution)/shard_map/ppermute | solution.py:45
  406.6 17.2 %collective-permute-start.37 = (bf16[2,1,1,1,24,3072]{5,4,3,1,0,2:T(8,128)(2,1)S(1)}, bf16[2,1,1,1,24,3072]{5,4,3,1,0,2:T(8,128)(2,1)S(1)}, u32[]{:S(2)}, u32[]{:S(2)}) collective-permute-start(bf16[2,1,1,1,24,3072]{5,4,3,1,0,2:T(8,128)(2,1)S(1)} %get-tuple-element.481), channel_id=1, source_target_pairs={{0,16},{1,17},{2,18},{3,19},{4,20},{5,21},{6,22},{7,23},{8,24},{9,... | collective-permute-start | bytes 884744 | tf_op jit(solution)/shard_map/ppermute | solution.py:34
  428.6 15.8 %collective-permute-start.41 = (bf16[1,1,1,1,24,3072]{5,4,3,1,0,2:T(8,128)(2,1)S(1)}, bf16[1,1,1,1,24,3072]{5,4,3,1,0,2:T(8,128)(2,1)S(1)}, u32[]{:S(2)}, u32[]{:S(2)}) collective-permute-start(bf16[1,1,1,1,24,3072]{5,4,3,1,0,2:T(8,128)(2,1)S(1)} %get-tuple-element.515), channel_id=1, source_target_pairs={{0,8},{1,9},{2,10},{3,11},{4,12},{5,13},{6,14},{7,15},{8,0},{9,1},... | collective-permute-start | bytes 442376 | tf_op jit(solution)/shard_map/ppermute | solution.py:34
  433.8 36.5 %collective-permute-start.42 = (bf16[2,1,1,1,24,6144]{5,4,3,2,1,0:T(8,128)(2,1)}, bf16[2,1,1,1,24,6144]{5,4,3,2,1,0:T(8,128)(2,1)}, u32[]{:S(2)}, u32[]{:S(2)}) collective-permute-start(bf16[2,1,1,1,24,6144]{5,4,3,2,1,0:T(8,128)(2,1)} %get-tuple-element.479), channel_id=1, source_target_pairs={{0,1},{1,0},{2,3},{3,2},{4,5},{5,4},{6,7},{7,6},{8,9},{9,8},{10,11... | collective-permute-start | bytes 1769480 | tf_op jit(solution)/shard_map/ppermute | solution.py:45
  437.8 32.5 %collective-permute-start.43 = (bf16[2,1,1,1,24,6144]{5,4,3,2,1,0:T(8,128)(2,1)}, bf16[2,1,1,1,24,6144]{5,4,3,2,1,0:T(8,128)(2,1)}, u32[]{:S(2)}, u32[]{:S(2)}) collective-permute-start(bf16[2,1,1,1,24,6144]{5,4,3,2,1,0:T(8,128)(2,1)} %get-tuple-element.477), channel_id=1, source_target_pairs={{0,4},{1,5},{2,6},{3,7},{4,0},{5,1},{6,2},{7,3},{8,12},{9,13},{10,... | collective-permute-start | bytes 1769480 | tf_op jit(solution)/shard_map/ppermute | solution.py:45
  438.3 32.1 %collective-permute-start.46 = (bf16[4,2,1,2,24,3840]{5,4,3,2,1,0:T(8,128)(2,1)}, bf16[4,2,1,2,24,3840]{5,4,3,2,1,0:T(8,128)(2,1)S(1)}, u32[]{:S(2)}, u32[]{:S(2)}) collective-permute-start(bf16[4,2,1,2,24,3840]{5,4,3,2,1,0:T(8,128)(2,1)} %bitcast.30), channel_id=1, source_target_pairs={{0,2},{1,3},{2,0},{3,1},{4,6},{5,7},{6,4},{7,5},{8,10},{9,11},{10,... | collective-permute-start | bytes 8847368 | tf_op jit(solution)/shard_map/ppermute | solution.py:45
  442.4 27.9 %collective-permute-start.44 = (bf16[2,1,1,2,24,3072]{5,4,3,1,0,2:T(8,128)(2,1)}, bf16[2,1,1,2,24,3072]{5,4,3,1,0,2:T(8,128)(2,1)S(1)}, u32[]{:S(2)}, u32[]{:S(2)}) collective-permute-start(bf16[2,1,1,2,24,3072]{5,4,3,1,0,2:T(8,128)(2,1)} %get-tuple-element.475), channel_id=1, source_target_pairs={{0,4},{1,5},{2,6},{3,7},{4,0},{5,1},{6,2},{7,3},{8,12},{9,13},{10,... | collective-permute-start | bytes 1769480 | tf_op jit(solution)/shard_map/ppermute | solution.py:45
  444.4 25.9 %collective-permute-start.45 = (bf16[2,2,1,1,24,3072]{5,4,3,1,0,2:T(8,128)(2,1)}, bf16[2,2,1,1,24,3072]{5,4,3,1,0,2:T(8,128)(2,1)}, u32[]{:S(2)}, u32[]{:S(2)}) collective-permute-start(bf16[2,2,1,1,24,3072]{5,4,3,1,0,2:T(8,128)(2,1)} %get-tuple-element.473), channel_id=1, source_target_pairs={{0,1},{1,0},{2,3},{3,2},{4,5},{5,4},{6,7},{7,6},{8,9},{9,8},{10,11... | collective-permute-start | bytes 1769480 | tf_op jit(solution)/shard_map/ppermute | solution.py:45
  475.0 20.7 %collective-permute-start.47 = (bf16[512,768]{1,0:T(8,128)(2,1)}, bf16[512,768]{1,0:T(8,128)(2,1)}, u32[]{:S(2)}, u32[]{:S(2)}) collective-permute-start(bf16[512,768]{1,0:T(8,128)(2,1)} %convolution_convert_fusion.2), channel_id=1, source_target_pairs={{0,1},{1,0},{2,3},{3,2},{4,5},{5,4},{6,7},{7,6},{8,9},{9,8},{10,11... | collective-permute-start | bytes 2359304 | tf_op jit(solution)/shard_map/ppermute | solution.py:45
  486.1 28.0 %collective-permute-start.48 = (bf16[2,1,1,1,24,6144]{5,4,3,2,1,0:T(8,128)(2,1)S(1)}, bf16[2,1,1,1,24,6144]{5,4,3,2,1,0:T(8,128)(2,1)S(1)}, u32[]{:S(2)}, u32[]{:S(2)}) collective-permute-start(bf16[2,1,1,1,24,6144]{5,4,3,2,1,0:T(8,128)(2,1)S(1)} %get-tuple-element.453), channel_id=1, source_target_pairs={{0,16},{1,17},{2,18},{3,19},{4,20},{5,21},{6,22},{7,23},{8,24},{9,... | collective-permute-start | bytes 1769480 | tf_op jit(solution)/shard_map/ppermute | solution.py:34
  487.1 14.9 %collective-permute-start.49 = (bf16[2,1,1,1,24,3072]{5,4,3,1,0,2:T(8,128)(2,1)S(1)}, bf16[2,1,1,1,24,3072]{5,4,3,1,0,2:T(8,128)(2,1)S(1)}, u32[]{:S(2)}, u32[]{:S(2)}) collective-permute-start(bf16[2,1,1,1,24,3072]{5,4,3,1,0,2:T(8,128)(2,1)S(1)} %get-tuple-element.501), channel_id=1, source_target_pairs={{0,1},{1,0},{2,3},{3,2},{4,5},{5,4},{6,7},{7,6},{8,9},{9,8},{10,11... | collective-permute-start | bytes 884744 | tf_op jit(solution)/shard_map/ppermute | solution.py:45
  489.2 12.8 %collective-permute-start.50 = (bf16[2,1,1,1,24,3072]{5,4,3,1,0,2:T(8,128)(2,1)S(1)}, bf16[2,1,1,1,24,3072]{5,4,3,1,0,2:T(8,128)(2,1)S(1)}, u32[]{:S(2)}, u32[]{:S(2)}) collective-permute-start(bf16[2,1,1,1,24,3072]{5,4,3,1,0,2:T(8,128)(2,1)S(1)} %get-tuple-element.499), channel_id=1, source_target_pairs={{0,4},{1,5},{2,6},{3,7},{4,0},{5,1},{6,2},{7,3},{8,12},{9,13},{10,... | collective-permute-start | bytes 884744 | tf_op jit(solution)/shard_map/ppermute | solution.py:45
  491.4 22.7 %collective-permute-start.51 = (bf16[2,1,1,2,24,3840]{5,4,3,2,1,0:T(8,128)(2,1)S(1)}, bf16[2,1,1,2,24,3840]{5,4,3,2,1,0:T(8,128)(2,1)S(1)}, u32[]{:S(2)}, u32[]{:S(2)}) collective-permute-start(bf16[2,1,1,2,24,3840]{5,4,3,2,1,0:T(8,128)(2,1)S(1)} %get-tuple-element.469), channel_id=1, source_target_pairs={{0,4},{1,5},{2,6},{3,7},{4,0},{5,1},{6,2},{7,3},{8,12},{9,13},{10,... | collective-permute-start | bytes 2211848 | tf_op jit(solution)/shard_map/ppermute | solution.py:45
  495.8 21.0 %collective-permute-start.52 = (bf16[2,2,1,1,24,3840]{5,4,3,2,1,0:T(8,128)(2,1)S(1)}, bf16[2,2,1,1,24,3840]{5,4,3,2,1,0:T(8,128)(2,1)S(1)}, u32[]{:S(2)}, u32[]{:S(2)}) collective-permute-start(bf16[2,2,1,1,24,3840]{5,4,3,2,1,0:T(8,128)(2,1)S(1)} %get-tuple-element.467), channel_id=1, source_target_pairs={{0,1},{1,0},{2,3},{3,2},{4,5},{5,4},{6,7},{7,6},{8,9},{9,8},{10,11... | collective-permute-start | bytes 2211848 | tf_op jit(solution)/shard_map/ppermute | solution.py:45
  517.8 13.1 %collective-permute-start.53 = (bf16[1,1,1,1,24,6144]{5,4,3,2,1,0:T(8,128)(2,1)}, bf16[1,1,1,1,24,6144]{5,4,3,2,1,0:T(8,128)(2,1)}, u32[]{:S(2)}, u32[]{:S(2)}) collective-permute-start(bf16[1,1,1,1,24,6144]{5,4,3,2,1,0:T(8,128)(2,1)} %get-tuple-element.497), channel_id=1, source_target_pairs={{0,8},{1,9},{2,10},{3,11},{4,12},{5,13},{6,14},{7,15},{8,0},{9,1},... | collective-permute-start | bytes 884744 | tf_op jit(solution)/shard_map/ppermute | solution.py:34
  518.9 15.6 %collective-permute-start.54 = (bf16[2,1,1,1,24,3072]{5,4,3,1,0,2:T(8,128)(2,1)}, bf16[2,1,1,1,24,3072]{5,4,3,1,0,2:T(8,128)(2,1)}, u32[]{:S(2)}, u32[]{:S(2)}) collective-permute-start(bf16[2,1,1,1,24,3072]{5,4,3,1,0,2:T(8,128)(2,1)} %get-tuple-element.471), channel_id=1, source_target_pairs={{0,16},{1,17},{2,18},{3,19},{4,20},{5,21},{6,22},{7,23},{8,24},{9,... | collective-permute-start | bytes 884744 | tf_op jit(solution)/shard_map/ppermute | solution.py:34
  524.1 15.2 %collective-permute-start.57 = (bf16[4,2,1,2,24,2304]{5,4,3,2,1,0:T(8,128)(2,1)}, bf16[4,2,1,2,24,2304]{5,4,3,2,1,0:T(8,128)(2,1)S(1)}, u32[]{:S(2)}, u32[]{:S(2)}) collective-permute-start(bf16[4,2,1,2,24,2304]{5,4,3,2,1,0:T(8,128)(2,1)} %bitcast.34), channel_id=1, source_target_pairs={{0,2},{1,3},{2,0},{3,1},{4,6},{5,7},{6,4},{7,5},{8,10},{9,11},{10,... | collective-permute-start | bytes 5308424 | tf_op jit(solution)/shard_map/ppermute | solution.py:45
  543.2 18.3 %collective-permute-start.60 = (bf16[2,1,1,1,24,3840]{5,4,3,2,1,0:T(8,128)(2,1)S(1)}, bf16[2,1,1,1,24,3840]{5,4,3,2,1,0:T(8,128)(2,1)S(1)}, u32[]{:S(2)}, u32[]{:S(2)}) collective-permute-start(bf16[2,1,1,1,24,3840]{5,4,3,2,1,0:T(8,128)(2,1)S(1)} %get-tuple-element.465), channel_id=1, source_target_pairs={{0,16},{1,17},{2,18},{3,19},{4,20},{5,21},{6,22},{7,23},{8,24},{9,... | collective-permute-start | bytes 1105928 | tf_op jit(solution)/shard_map/ppermute | solution.py:34
  544.2 17.3 %collective-permute-start.61 = (bf16[2,1,1,2,24,2304]{5,4,3,2,1,0:T(8,128)(2,1)S(1)}, bf16[2,1,1,2,24,2304]{5,4,3,2,1,0:T(8,128)(2,1)S(1)}, u32[]{:S(2)}, u32[]{:S(2)}) collective-permute-start(bf16[2,1,1,2,24,2304]{5,4,3,2,1,0:T(8,128)(2,1)S(1)} %get-tuple-element.491), channel_id=1, source_target_pairs={{0,4},{1,5},{2,6},{3,7},{4,0},{5,1},{6,2},{7,3},{8,12},{9,13},{10,... | collective-permute-start | bytes 1327112 | tf_op jit(solution)/shard_map/ppermute | solution.py:45
  544.8 16.7 %collective-permute-start.62 = (bf16[2,2,1,1,24,2304]{5,4,3,2,1,0:T(8,128)(2,1)S(1)}, bf16[2,2,1,1,24,2304]{5,4,3,2,1,0:T(8,128)(2,1)S(1)}, u32[]{:S(2)}, u32[]{:S(2)}) collective-permute-start(bf16[2,2,1,1,24,2304]{5,4,3,2,1,0:T(8,128)(2,1)S(1)} %get-tuple-element.489), channel_id=1, source_target_pairs={{0,1},{1,0},{2,3},{3,2},{4,5},{5,4},{6,7},{7,6},{8,9},{9,8},{10,11... | collective-permute-start | bytes 1327112 | tf_op jit(solution)/shard_map/ppermute | solution.py:45
  571.7 15.0 %collective-permute-start.68 = (bf16[2,1,1,1,24,2304]{5,4,3,2,1,0:T(8,128)(2,1)S(1)}, bf16[2,1,1,1,24,2304]{5,4,3,2,1,0:T(8,128)(2,1)S(1)}, u32[]{:S(2)}, u32[]{:S(2)}) collective-permute-start(bf16[2,1,1,1,24,2304]{5,4,3,2,1,0:T(8,128)(2,1)S(1)} %get-tuple-element.487), channel_id=1, source_target_pairs={{0,16},{1,17},{2,18},{3,19},{4,20},{5,21},{6,22},{7,23},{8,24},{9,... | collective-permute-start | bytes 663560 | tf_op jit(solution)/shard_map/ppermute | solution.py:34
  573.7 13.0 %collective-permute-start.69 = (f32[2,9216]{1,0:T(2,128)S(1)}, f32[2,9216]{1,0:T(2,128)S(1)}, u32[]{:S(2)}, u32[]{:S(2)}) collective-permute-start(f32[2,9216]{1,0:T(2,128)S(1)} %add.724), channel_id=1, source_target_pairs={{0,16},{1,17},{2,18},{3,19},{4,20},{5,21},{6,22},{7,23},{8,24},{9,... | collective-permute-start | bytes 221192 | tf_op jit(solution)/shard_map/ppermute | solution.py:34
  (118 other events, 1025.4 us)
Sparse Core Ops, SparseCore 0:
  69.2 101.8 all-gather.2
  174.6 65.0 all-gather.4

commit v4 on v3

--- a/solution.py
+++ b/solution.py
@@ -177,7 +177,7 @@
     return [lax.dynamic_slice_in_dim(total, place, 1, CORE) for place in (core, 1 - core)]
 
 
-def scatter_rows(grid, kept, sent):
+def scatter_rows(grid, kept, sent, last=False):
     kept, arrived = yield kept, [grid.shift(sent, CORE, 1)]
     part = total_of(kept, arrived).astype(jnp.bfloat16)
     half = grid.outer_size // 2
@@ -186,6 +186,9 @@
     for turn in range(2):
         flying = yield [exchange(grid, part, order[turn]) for part, order in zip(parts, orders)]
         parts = [total_of(*entry).astype(jnp.bfloat16) for entry in flying]
+    if last:
+        kept, arrived = yield exchange(grid, join(parts), OUTER)
+        return total_of(kept, arrived).reshape(kept.shape[-2:])
     outer = grid.digits()[OUTER]
     for bit in grid.outer_bits():
         upper = ((outer >> bit) & 1) == 1
@@ -659,10 +662,11 @@
     place = lax.axis_index("clip") * grid.seq_size + lax.axis_index("seq")
     lanes = []
     for slot in SMALL:
-        shard = params[slot].astype(jnp.bfloat16)
-        empty = jnp.zeros((LAYERS, shard.shape[1] * grid.owners), jnp.bfloat16)
+        shard = params[slot]
+        empty = jnp.zeros((LAYERS, shard.shape[1] * grid.owners), jnp.float32)
         lanes.append(lax.dynamic_update_slice_in_dim(empty, shard, place * shard.shape[1], 1))
-    whole = everywhere(grid, jnp.concatenate(lanes, axis=1)).astype(jnp.float32)
+    packed = jnp.concatenate(lanes, axis=1).astype(jnp.bfloat16)
+    whole = everywhere(grid, packed).astype(jnp.float32)
     found, offset = [[] for _ in range(LAYERS)], 0
     for lane in lanes:
         for layer in range(LAYERS):
@@ -675,20 +679,27 @@
     place = lax.axis_index("clip") * grid.seq_size + lax.axis_index("seq")
     lengths = [total.shape[0] for total in totals[0]]
     starts = [sum(lengths[:index]) for index in range(len(lengths) + 1)]
+    amount = starts[-1]
     whole = sum(
         jnp.pad(
-            total[None],
-            ((layer, LAYERS - 1 - layer), (starts[index], starts[-1] - starts[index + 1])),
+            total,
+            (
+                layer * amount + starts[index],
+                (LAYERS - layer) * amount - starts[index + 1],
+            ),
         )
         for layer in range(LAYERS)
         for index, total in enumerate(totals[layer])
     )
-    for axis in (CORE, SEQ, CROSS):
-        whole, moved = yield whole, around(grid, whole, axis)
-        whole = sum(moved, whole)
+    whole = sum(around(grid, whole, CORE), whole)
+    whole, moved = yield whole, around(grid, whole, SEQ)
+    whole = sum(moved, whole)
+    whole, moved = yield whole, around(grid, whole, CROSS)
+    whole = sum(moved, whole)
     for bit in grid.outer_bits():
         whole, moved = yield whole, grid.swap_outer(whole, bit)
         whole = whole + moved
+    whole = whole.reshape(LAYERS, -1)
     pieces, offset = [], 0
     for total in totals[0]:
         amount = total.shape[0] // grid.owners
@@ -836,7 +847,7 @@
         pulled, gain_one, shift_one = normal_back(grad_normed, keep["hidden"], g1)
         grad_hidden = grad_middle + pulled
         mixed, grad_hidden = traffic.tick(mixed, grad_hidden)
-        mixed_share = traffic.add(scatter_rows(grid, *mixed))
+        mixed_share = traffic.add(scatter_rows(grid, *mixed, layer == 0))
         if layer + 1 == LAYERS:
             up_share = mixed_share
         shares[layer] = (mixed_share, up_share, low_share)

time: 609 us -> 603 us (level)
  waiting for transfers between devices: 167 us -> 156 us
    ppermute x12 -> x10, waiting for transfers between devices: 37 us -> 25.8 us  [swap_outer(): lax.ppermute(array, AXES, [(place, place ^ flip) for place in range(self....]
    ppermute x60 -> x63, starting transfers between devices: 55.6 us -> 61.3 us  [shift(): return lax.ppermute(array, AXES, pairs)]
    ppermute x12 -> x10, starting transfers between devices: 16.8 us -> 14.4 us  [swap_outer(): lax.ppermute(array, AXES, [(place, place ^ flip) for place in range(self....]
    ppermute x60 -> x63, waiting for transfers between devices: 125 us -> 126 us  [shift(): return lax.ppermute(array, AXES, pairs)]
  transfers between devices with their start and end apart: 74 -> 75, of which waited for: 32 -> 30; matrix products, arithmetic and copies ran while one was open for 21% -> 21% of each run, Pallas kernels for 20% -> 20%
where the time goes in v4:
time: 603 us; the launch traced here: 597 us
  waiting for transfers between devices  156 us (26%)
  Pallas kernels  153 us (25%)
  matrix products  88.1 us (15%)
  starting transfers between devices  75.9 us (13%)
  other arithmetic  57.8 us (10%)
  local copies, waits for them, and re-layouts  50.2 us (8%)
  between operations  15.9 us (3%)
    ppermute x63, waiting for transfers between devices, shift(): return lax.ppermute(array, AXES, pairs)  126 us
    ppermute x63, starting transfers between devices, shift(): return lax.ppermute(array, AXES, pairs)  61.3 us
    dot_general x12, matrix products, times_transposed(): lax.dot_general(left, right, (((1,), (1,)), ((), ())), preferred_element_...  48.2 us
    pallas_call x2, Pallas kernels, attend_back(): pl.pallas_call(attend_back_kernel, grid=(blocks,), in_specs=block_specs(f...  45.6 us
    dot_general x10, matrix products, times(): lax.dot_general(left, right, (((1,), (0,)), ((), ())), preferred_element_...  39.8 us
    pallas_call x2, Pallas kernels, attend(): pl.pallas_call(attend_kernel, grid=(blocks,), in_specs=block_specs(frames...  28.9 us
    ppermute x10, waiting for transfers between devices, swap_outer(): lax.ppermute(array, AXES, [(place, place ^ flip) for place in range(self....  25.8 us
    pallas_call x2, Pallas kernels, raise_width(): pl.pallas_call(raise_kernel, grid=(units // tile,), in_specs=[pl.BlockSpe...  19.8 us
  transfers between devices with their start and end apart: 75, of which 30 were waited for; matrix products, arithmetic and copies ran while one was open for 21% of the time, Pallas kernels for 20%

profile of v4, /device:TPU:0, one launch (start us, length us, event | category | flops | bytes accessed | tf_op | source)
XLA Modules:
  0.0 597.2 jit_solution(5503526527166082766)
XLA Ops:
  24.8 3.7 collective-permute-start.2
  48.7 8.7 %collective-permute-done.13 = bf16[1,24,6912]{2,1,0:T(8,128)(2,1)} collective-permute-done((bf16[1,24,6912]{2,1,0:T(8,128)(2,1)S(1)}, bf16[1,24,6912]{2,1,0:T(8,128)(2,1)}, u32[]{:S(2)}, u32[]{:S(2)}) %collective-permute-start.13) | collective-permute-done | bytes 331808 | tf_op jit(solution)/shard_map/ppermute | solution.py:45
  57.5 11.3 %collective-permute-done.11 = bf16[2,24,2304]{2,1,0:T(8,128)(2,1)} collective-permute-done((bf16[2,24,2304]{2,1,0:T(8,128)(2,1)S(1)}, bf16[2,24,2304]{2,1,0:T(8,128)(2,1)}, u32[]{:S(2)}, u32[]{:S(2)}) %collective-permute-start.11) | collective-permute-done | bytes 221216 | tf_op jit(solution)/shard_map/ppermute | solution.py:45
  81.1 5.8 collective-permute-done.15.refs_1_
  86.9 18.2 %collective-permute-done.16.refs_3_ = bf16[4,24,2304]{2,1,0:T(8,128)(2,1)} collective-permute-done((bf16[4,24,2304]{2,1,0:T(8,128)(2,1)S(1)}, bf16[4,24,2304]{2,1,0:T(8,128)(2,1)}, u32[]{:S(2)}, u32[]{:S(2)}) %collective-permute-start.16) | collective-permute-done | bytes 442400 | tf_op jit(solution)/shard_map/ppermute | solution.py:45
  113.7 4.5 place_rows.2
  118.2 4.4 fusion.1.k_ref.v_ref
  122.6 3.8 fusion.2.k_far_ref.v_far_ref
  128.1 14.4 %attend.2 = (bf16[512,768]{1,0:T(8,128)(2,1)}, f32[6,2,512]{2,1,0:T(2,128)}) custom-call(bf16[512,768]{1,0:T(8,128)(2,1)} %add_convert_fusion.11.q_ref, bf16[512,1536]{1,0:T(8,128)(2,1)} %fusion.1.k_ref.v_ref, bf16[512,1536]{1,0:T(8,128)(2,1)} %fusion.1.k_ref.v_ref, bf16[512,1536]{1,0:T(8,128)(2,1)} %fusion.2.k_far_ref.v_far_ref, ...), custom_call_target="tpu_custom_call" | custom-call | flops 1000 | bytes 1000 | tf_op jit(solution)/shard_map/attend/pallas_call | solution.py:547
  142.5 12.9 %collective-permute-done.23.refs_1_ = bf16[4,24,6912]{2,1,0:T(8,128)(2,1)S(1)} collective-permute-done((bf16[4,24,6912]{2,1,0:T(8,128)(2,1)S(1)}, bf16[4,24,6912]{2,1,0:T(8,128)(2,1)S(1)}, u32[]{:S(2)}, u32[]{:S(2)}) %collective-permute-start.23) | collective-permute-done | bytes 1327136 | tf_op jit(solution)/shard_map/ppermute | solution.py:45
  155.4 4.0 collective-permute-done.24.refs_3_
  162.4 5.7 collective-permute-done.26.refs_5_
  172.0 9.9 %place_rows.3 = (bf16[32,24,768]{2,1,0:T(8,128)(2,1)}, bf16[32,24,3072]{2,1,0:T(8,128)(2,1)}, bf16[128,24,768]{2,1,0:T(8,128)(2,1)}) custom-call(bf16[4,24,6912]{2,1,0:T(8,128)(2,1)} %copy-done.26, bf16[4,24,6912]{2,1,0:T(8,128)(2,1)} %copy-done.37, bf16[4,24,6912]{2,1,0:T(8,128)(2,1)} %copy-done.27, bf16[4,24,6912]{2,1,0:T(8,128)(2,1)} %collective-permute-done.24.refs_3_, ...), custom_call_target="tpu_custom_call" | custom-call | flops 1000 | bytes 1000 | tf_op jit(solution)/shard_map/place_rows/pallas_call | solution.py:140
  186.0 10.0 %raise_width.2 = (bf16[512,3072]{1,0:T(8,128)(2,1)}, f32[512,3072]{1,0:T(8,128)}) custom-call(bf16[512,768]{1,0:T(8,128)(2,1)} %add_convert_fusion.10.left_ref.normed_ref, bf16[768,3072]{1,0:T(8,128)(2,1)} %bitcast.134, f32[1,3072]{1,0:T(1,128)} %get-tuple-element.526.bias_ref), custom_call_target="tpu_custom_call" | custom-call | flops 1000 | bytes 1000 | tf_op jit(solution)/shard_map/raise_width/pallas_call | solution.py:623
  196.0 6.1 %fusion.56 = (f32[512]{0:T(512)S(1)}, f32[512,768]{1,0:T(8,128)S(1)}) fusion(f32[512,768]{1,0:T(8,128)S(1)} %get-tuple-element.530, f32[768]{0:T(1024)S(1)} %copy-done.83, bf16[512,3072]{1,0:T(8,128)(2,1)} %get-tuple-element.252.active_ref, bf16[3072,768]{1,0:T(8,128)(2,1)} %bitcast.154), kind=kOutput, calls=%fused_computation.298 | convolution fusion | flops 2417098240 | bytes 11015168 | tf_op jit(solution)/shard_map/dot_general | solution.py:465
  209.1 4.4 fusion.3.k_ref.v_ref
  213.5 16.3 %collective-permute-done.29.far_ref = bf16[512,768]{1,0:T(8,128)(2,1)} collective-permute-done((bf16[512,768]{1,0:T(8,128)(2,1)}, bf16[512,768]{1,0:T(8,128)(2,1)}, u32[]{:S(2)}, u32[]{:S(2)}) %collective-permute-start.29) | collective-permute-done | bytes 786464 | tf_op jit(solution)/shard_map/ppermute | solution.py:45
  229.8 4.5 fusion.4.k_far_ref.v_far_ref
  234.3 4.9 all-gather.5.cloned.1.call-done
  239.2 7.8 %fusion.58 = f32[3072,512]{0,1:T(8,128)} fusion(bf16[3072,768]{1,0:T(8,128)(2,1)} %all-gather.5.cloned.1.call-done, bf16[512,768]{1,0:T(8,128)(2,1)} %get-tuple-element.441.down_ref), kind=kOutput, calls=%fused_computation.300 | convolution fusion | flops 2415919104 | bytes 11796480 | tf_op jit(solution)/shard_map/dot_general | solution.py:459
  247.0 14.4 %attend.3 = (bf16[512,768]{1,0:T(8,128)(2,1)}, f32[6,2,512]{2,1,0:T(2,128)}) custom-call(bf16[512,768]{1,0:T(8,128)(2,1)} %add_convert_fusion.8.q_ref, bf16[512,1536]{1,0:T(8,128)(2,1)} %fusion.3.k_ref.v_ref, bf16[512,1536]{1,0:T(8,128)(2,1)} %fusion.3.k_ref.v_ref, bf16[512,1536]{1,0:T(8,128)(2,1)} %fusion.4.k_far_ref.v_far_ref, ...), custom_call_target="tpu_custom_call" | custom-call | flops 1000 | bytes 1000 | tf_op jit(solution)/shard_map/attend/pallas_call | solution.py:547
  265.4 4.9 slice.279.right_ref
  270.3 9.9 %raise_width.3 = (bf16[512,3072]{1,0:T(8,128)(2,1)}, f32[512,3072]{1,0:T(8,128)}) custom-call(bf16[512,768]{1,0:T(8,128)(2,1)} %add_convert_fusion.7.left_ref.normed_ref, bf16[768,3072]{1,0:T(8,128)(2,1)} %slice.279.right_ref, f32[1,3072]{1,0:T(1,128)} %get-tuple-element.525.bias_ref), custom_call_target="tpu_custom_call" | custom-call | flops 1000 | bytes 1000 | tf_op jit(solution)/shard_map/raise_width/pallas_call | solution.py:623
  280.2 6.9 %low_shares.2 = (bf16[384,3072]{1,0:T(8,128)(2,1)}, bf16[384,3072]{1,0:T(8,128)(2,1)}) custom-call(bf16[512,3072]{1,0:T(8,128)(2,1)} %get-tuple-element.256.active_ref, bf16[512,768]{1,0:T(8,128)(2,1)} %get-tuple-element.441.down_ref), custom_call_target="tpu_custom_call" | custom-call | flops 1000 | bytes 1000 | tf_op jit(solution)/shard_map/low_shares/pallas_call | solution.py:376
  287.1 6.1 %convert_reduce_fusion = (f32[3072]{0:T(1024)S(1)}, bf16[512,3072]{1,0:T(8,128)(2,1)S(1)}) fusion(f32[512,3072]{1,0:T(8,128)} %get-tuple-element.262, f32[3072,512]{0,1:T(8,128)} %fusion.58), kind=kLoop, calls=%fused_computation.3 | loop fusion | flops 6288384 | bytes 15740928 | tf_op jit(solution)/shard_map/reduce_sum | solution.py:649
  293.2 7.1 %multiply_reduce_fusion = (f32[768]{0:T(1024)S(1)}, f32[512]{0:T(512)S(1)}, f32[512]{0:T(512)S(1)}, f32[768]{0:T(1024)}, f32[512,768]{1,0:T(8,128)S(1)}) fusion(f32[512,768]{1,0:T(8,128)S(1)} %get-tuple-element.534, f32[512]{0:T(512)S(1)} %add_rsqrt_fusion.1, f32[512]{0:T(512)S(1)} %broadcast_multiply_fusion.9, f32[768]{0:T(1024)S(1)} %get-tuple-element.416, ...), kind=kOutput, calls=%fused_computation.23 | convolution fusion | flops 2419455488 | bytes 11027456 | tf_op jit(solution)/shard_map/dot_general | solution.py:459
  302.1 3.3 convolution_convert_fusion.1.g_ref
  305.6 22.7 %attend_back.2 = (bf16[512,768]{1,0:T(8,128)(2,1)}, bf16[512,1536]{1,0:T(8,128)(2,1)}, bf16[512,1536]{1,0:T(8,128)(2,1)}) custom-call(bf16[512,768]{1,0:T(8,128)(2,1)} %add_convert_fusion.8.q_ref, bf16[512,1536]{1,0:T(8,128)(2,1)} %fusion.3.k_ref.v_ref, bf16[512,1536]{1,0:T(8,128)(2,1)} %fusion.3.k_ref.v_ref, bf16[512,1536]{1,0:T(8,128)(2,1)} %fusion.4.k_far_ref.v_far_ref, ...), custom_call_target="tpu_custom_call" | custom-call | flops 1000 | bytes 1000 | tf_op jit(solution)/shard_map/attend_back/pallas_call | solution.py:568
  328.3 4.6 fusion.11
  340.6 13.7 %both_shares.1 = (bf16[384,6144]{1,0:T(8,128)(2,1)}, bf16[384,6144]{1,0:T(8,128)(2,1)}) custom-call(bf16[512,768]{1,0:T(8,128)(2,1)} %add_convert_fusion.7.left_ref.normed_ref, bf16[512,3072]{1,0:T(8,128)(2,1)} %copy-done.8, bf16[512,768]{1,0:T(8,128)(2,1)} %get-tuple-element.278.mixed_ref, bf16[512,768]{1,0:T(8,128)(2,1)} %copy-done.23, ...), custom_call_target="tpu_custom_call" | custom-call | flops 1000 | bytes 1000 | tf_op jit(solution)/shard_map/both_shares/pallas_call | solution.py:328
  367.0 7.1 %add_bitcast_fusion = f32[1,512,768]{2,1,0:T(8,128)} fusion(f32[512,768]{1,0:T(8,128)S(1)} %copy-done.4, bf16[512,3072]{1,0:T(8,128)(2,1)} %get-tuple-element.256.active_ref, bf16[3072,768]{1,0:T(8,128)(2,1)} %all-gather.5.cloned.1.call-done, f32[768]{0:T(1024)S(1)} %copy-done.80), kind=kOutput, calls=%fused_computation.46 | convolution fusion | flops 2416705536 | bytes 11013120 | tf_op jit(solution)/shard_map/dot_general | solution.py:465
  379.9 6.4 %multiply_convert_fusion.before_ref = bf16[512,3072]{1,0:T(8,128)(2,1)S(1)} fusion(f32[512,3072]{1,0:T(8,128)} %get-tuple-element.291, bf16[512,768]{1,0:T(8,128)(2,1)S(1)} %get-tuple-element.434.down_ref, bf16[3072,768]{1,0:T(8,128)(2,1)} %bitcast.155), kind=kOutput, calls=%fused_computation.5 | convolution fusion | flops 2419064832 | bytes 14942208 | tf_op jit(solution)/shard_map/dot_general | solution.py:459
  386.4 8.0 %low_shares.3 = (bf16[384,3072]{1,0:T(8,128)(2,1)}, bf16[384,3072]{1,0:T(8,128)(2,1)}) custom-call(bf16[512,3072]{1,0:T(8,128)(2,1)} %get-tuple-element.252.active_ref, bf16[512,768]{1,0:T(8,128)(2,1)} %copy-done.22), custom_call_target="tpu_custom_call" | custom-call | flops 1000 | bytes 1000 | tf_op jit(solution)/shard_map/low_shares/pallas_call | solution.py:376
  394.5 5.7 add_convert_fusion
  406.1 3.6 multiply_reduce_fusion.2
  409.8 3.2 collective-permute-start.37
  414.6 8.4 %up_shares.1 = (bf16[384,3840]{1,0:T(8,128)(2,1)}, bf16[384,3840]{1,0:T(8,128)(2,1)}) custom-call(bf16[512,768]{1,0:T(8,128)(2,1)} %add_convert_fusion.10.left_ref.normed_ref, bf16[512,3072]{1,0:T(8,128)(2,1)} %copy-done.6, bf16[512,768]{1,0:T(8,128)(2,1)} %get-tuple-element.245.mixed_ref, bf16[512,768]{1,0:T(8,128)(2,1)} %get-tuple-element.431.branch_ref), custom_call_target="tpu_custom_call" | custom-call | flops 1000 | bytes 1000 | tf_op jit(solution)/shard_map/up_shares/pallas_call | solution.py:256
  427.0 3.5 collective-permute-done.38
  449.5 22.9 %attend_back.3 = (bf16[512,768]{1,0:T(8,128)(2,1)}, bf16[512,1536]{1,0:T(8,128)(2,1)}, bf16[512,1536]{1,0:T(8,128)(2,1)}) custom-call(bf16[512,768]{1,0:T(8,128)(2,1)} %add_convert_fusion.11.q_ref, bf16[512,1536]{1,0:T(8,128)(2,1)} %fusion.1.k_ref.v_ref, bf16[512,1536]{1,0:T(8,128)(2,1)} %fusion.1.k_ref.v_ref, bf16[512,1536]{1,0:T(8,128)(2,1)} %fusion.2.k_far_ref.v_far_ref, ...), custom_call_target="tpu_custom_call" | custom-call | flops 1000 | bytes 1000 | tf_op jit(solution)/shard_map/attend_back/pallas_call | solution.py:568
  473.4 4.6 convolution_convert_fusion.2
  479.5 7.3 %mixing_shares.1 = (bf16[384,2304]{1,0:T(8,128)(2,1)}, bf16[384,2304]{1,0:T(8,128)(2,1)}) custom-call(bf16[512,768]{1,0:T(8,128)(2,1)} %copy-done.21, bf16[512,768]{1,0:T(8,128)(2,1)} %collective-permute-done.9.far_ref, bf16[512,768]{1,0:T(8,128)(2,1)} %get-tuple-element.327.query_ref, bf16[512,1536]{1,0:T(8,128)(2,1)} %get-tuple-element.328.pair_ref, ...), custom_call_target="tpu_custom_call" | custom-call | flops 1000 | bytes 1000 | tf_op jit(solution)/shard_map/mixing_shares/pallas_call | solution.py:428
  504.8 11.8 %collective-permute-done.48 = bf16[2,1,1,1,24,6144]{5,4,3,2,1,0:T(8,128)(2,1)S(1)} collective-permute-done((bf16[2,1,1,1,24,6144]{5,4,3,2,1,0:T(8,128)(2,1)S(1)}, bf16[2,1,1,1,24,6144]{5,4,3,2,1,0:T(8,128)(2,1)S(1)}, u32[]{:S(2)}, u32[]{:S(2)}) %collective-permute-start.48) | collective-permute-done | bytes 589856 | tf_op jit(solution)/shard_map/ppermute | solution.py:34
  516.7 3.3 collective-permute-done.52
  531.9 4.8 collective-permute-done.59
  538.5 7.2 %collective-permute-done.56 = bf16[2,1,1,1,24,3840]{5,4,3,2,1,0:T(8,128)(2,1)} collective-permute-done((bf16[2,1,1,1,24,3840]{5,4,3,2,1,0:T(8,128)(2,1)}, bf16[2,1,1,1,24,3840]{5,4,3,2,1,0:T(8,128)(2,1)}, u32[]{:S(2)}, u32[]{:S(2)}) %collective-permute-start.56) | collective-permute-done | bytes 368672 | tf_op jit(solution)/shard_map/ppermute | solution.py:45
  555.8 4.6 collective-permute-done.64
  560.4 4.5 collective-permute-done.61
  582.1 5.2 collective-permute-done.72
  (511 shorter events, 204.4 us)
Async XLA Ops:
  7.2 198.7 %all-gather.3.cloned.1.call-start = ((), (), s32[]{:S(2)}) async-start(), calls=%async_computation | async-start | bytes 9732096 | tf_op jit(solution)/shard_map/all_gather | solution.py:752
  8.4 26.8 %collective-permute-start = (bf16[1,24,2304]{2,1,0:T(8,128)(2,1)S(1)}, bf16[1,24,2304]{2,1,0:T(8,128)(2,1)S(1)}, u32[]{:S(2)}, u32[]{:S(2)}) collective-permute-start(bf16[1,24,2304]{2,1,0:T(8,128)(2,1)S(1)} %bitcast.150), channel_id=1, source_target_pairs={{0,8},{1,9},{2,10},{3,11},{4,12},{5,13},{6,14},{7,15},{8,16},{9,17... | collective-permute-start | bytes 331784 | tf_op jit(solution)/shard_map/ppermute | solution.py:45
  11.5 24.8 %collective-permute-start.1 = (bf16[1,24,2304]{2,1,0:T(8,128)(2,1)S(1)}, bf16[1,24,2304]{2,1,0:T(8,128)(2,1)}, u32[]{:S(2)}, u32[]{:S(2)}) collective-permute-start(bf16[1,24,2304]{2,1,0:T(8,128)(2,1)S(1)} %bitcast.151), channel_id=1, source_target_pairs={{0,16},{1,17},{2,18},{3,19},{4,20},{5,21},{6,22},{7,23},{8,24},{9,... | collective-permute-start | bytes 331784 | tf_op jit(solution)/shard_map/ppermute | solution.py:45
  24.8 14.2 %collective-permute-start.2 = (bf16[1,24,2304]{2,1,0:T(8,128)(2,1)S(1)}, bf16[1,24,2304]{2,1,0:T(8,128)(2,1)S(1)}, u32[]{:S(2)}, u32[]{:S(2)}) collective-permute-start(bf16[1,24,2304]{2,1,0:T(8,128)(2,1)S(1)} %bitcast.152), channel_id=1, source_target_pairs={{0,24},{1,25},{2,26},{3,27},{4,28},{5,29},{6,30},{7,31},{8,0},{9,1... | collective-permute-start | bytes 331784 | tf_op jit(solution)/shard_map/ppermute | solution.py:45
  35.1 12.7 %collective-permute-start.12 = (bf16[1,24,6912]{2,1,0:T(8,128)(2,1)S(1)}, bf16[1,24,6912]{2,1,0:T(8,128)(2,1)}, u32[]{:S(2)}, u32[]{:S(2)}) collective-permute-start(bf16[1,24,6912]{2,1,0:T(8,128)(2,1)S(1)} %maximum_bitcast_fusion), channel_id=1, source_target_pairs={{0,8},{1,9},{2,10},{3,11},{4,12},{5,13},{6,14},{7,15},{8,16},{9,17... | collective-permute-start | bytes 995336 | tf_op jit(solution)/shard_map/ppermute | solution.py:45
  35.2 22.3 %collective-permute-start.13 = (bf16[1,24,6912]{2,1,0:T(8,128)(2,1)S(1)}, bf16[1,24,6912]{2,1,0:T(8,128)(2,1)}, u32[]{:S(2)}, u32[]{:S(2)}) collective-permute-start(bf16[1,24,6912]{2,1,0:T(8,128)(2,1)S(1)} %maximum_bitcast_fusion), channel_id=1, source_target_pairs={{0,16},{1,17},{2,18},{3,19},{4,20},{5,21},{6,22},{7,23},{8,24},{9,... | collective-permute-start | bytes 995336 | tf_op jit(solution)/shard_map/ppermute | solution.py:45
  36.3 21.2 %collective-permute-start.14 = (bf16[1,24,6912]{2,1,0:T(8,128)(2,1)S(1)}, bf16[1,24,6912]{2,1,0:T(8,128)(2,1)}, u32[]{:S(2)}, u32[]{:S(2)}) collective-permute-start(bf16[1,24,6912]{2,1,0:T(8,128)(2,1)S(1)} %maximum_bitcast_fusion), channel_id=1, source_target_pairs={{0,24},{1,25},{2,26},{3,27},{4,28},{5,29},{6,30},{7,31},{8,0},{9,1... | collective-permute-start | bytes 995336 | tf_op jit(solution)/shard_map/ppermute | solution.py:45
  41.9 15.6 %collective-permute-start.10 = (bf16[2,24,2304]{2,1,0:T(8,128)(2,1)S(1)}, bf16[2,24,2304]{2,1,0:T(8,128)(2,1)}, u32[]{:S(2)}, u32[]{:S(2)}) collective-permute-start(bf16[2,24,2304]{2,1,0:T(8,128)(2,1)S(1)} %constant_dynamic-update-slice_fusion.8), channel_id=1, source_target_pairs={{0,4},{1,5},{2,6},{3,7},{4,0},{5,1},{6,2},{7,3},{8,12},{9,13},{10,... | collective-permute-start | bytes 663560 | tf_op jit(solution)/shard_map/ppermute | solution.py:45
  44.5 24.3 %collective-permute-start.9 = (bf16[512,768]{1,0:T(8,128)(2,1)S(1)}, bf16[512,768]{1,0:T(8,128)(2,1)}, u32[]{:S(2)}, u32[]{:S(2)}) collective-permute-start(bf16[512,768]{1,0:T(8,128)(2,1)S(1)} %add_convert_fusion.12.near_ref), channel_id=1, source_target_pairs={{0,1},{1,0},{2,3},{3,2},{4,5},{5,4},{6,7},{7,6},{8,9},{9,8},{10,11... | collective-permute-start | bytes 2359304 | tf_op jit(solution)/shard_map/ppermute | solution.py:45
  47.8 20.9 %collective-permute-start.11 = (bf16[2,24,2304]{2,1,0:T(8,128)(2,1)S(1)}, bf16[2,24,2304]{2,1,0:T(8,128)(2,1)}, u32[]{:S(2)}, u32[]{:S(2)}) collective-permute-start(bf16[2,24,2304]{2,1,0:T(8,128)(2,1)S(1)} %constant_dynamic-update-slice_fusion.10), channel_id=1, source_target_pairs={{0,1},{1,0},{2,3},{3,2},{4,5},{5,4},{6,7},{7,6},{8,9},{9,8},{10,11... | collective-permute-start | bytes 663560 | tf_op jit(solution)/shard_map/ppermute | solution.py:45
  68.8 170.4 %all-gather.5.cloned.1.call-start = ((), (), s32[]{:S(2)}) async-start(), calls=%async_computation.1 | async-start | bytes 4866048 | tf_op jit(solution)/shard_map/all_gather | solution.py:752
  71.4 15.5 %collective-permute-start.15 = (bf16[4,24,2304]{2,1,0:T(8,128)(2,1)}, bf16[4,24,2304]{2,1,0:T(8,128)(2,1)}, u32[]{:S(2)}, u32[]{:S(2)}) collective-permute-start(bf16[4,24,2304]{2,1,0:T(8,128)(2,1)} %constant_dynamic-update-slice_fusion.12.refs_0_), channel_id=1, source_target_pairs={{0,1},{1,0},{2,3},{3,2},{4,5},{5,4},{6,7},{7,6},{8,9},{9,8},{10,11... | collective-permute-start | bytes 1327112 | tf_op jit(solution)/shard_map/ppermute | solution.py:45
  72.9 32.3 %collective-permute-start.17 = (bf16[2,24,6912]{2,1,0:T(8,128)(2,1)S(1)}, bf16[2,24,6912]{2,1,0:T(8,128)(2,1)}, u32[]{:S(2)}, u32[]{:S(2)}) collective-permute-start(bf16[2,24,6912]{2,1,0:T(8,128)(2,1)S(1)} %constant_dynamic-update-slice_fusion.16), channel_id=1, source_target_pairs={{0,4},{1,5},{2,6},{3,7},{4,0},{5,1},{6,2},{7,3},{8,12},{9,13},{10,... | collective-permute-start | bytes 1990664 | tf_op jit(solution)/shard_map/ppermute | solution.py:45
  76.8 28.3 %collective-permute-start.18 = (bf16[2,24,6912]{2,1,0:T(8,128)(2,1)}, bf16[2,24,6912]{2,1,0:T(8,128)(2,1)}, u32[]{:S(2)}, u32[]{:S(2)}) collective-permute-start(bf16[2,24,6912]{2,1,0:T(8,128)(2,1)} %constant_dynamic-update-slice_fusion.18), channel_id=1, source_target_pairs={{0,1},{1,0},{2,3},{3,2},{4,5},{5,4},{6,7},{7,6},{8,9},{9,8},{10,11... | collective-permute-start | bytes 1990664 | tf_op jit(solution)/shard_map/ppermute | solution.py:45
  79.5 25.6 %collective-permute-start.16 = (bf16[4,24,2304]{2,1,0:T(8,128)(2,1)S(1)}, bf16[4,24,2304]{2,1,0:T(8,128)(2,1)}, u32[]{:S(2)}, u32[]{:S(2)}) collective-permute-start(bf16[4,24,2304]{2,1,0:T(8,128)(2,1)S(1)} %constant_dynamic-update-slice_fusion.14.refs_2_), channel_id=1, source_target_pairs={{0,4},{1,5},{2,6},{3,7},{4,0},{5,1},{6,2},{7,3},{8,12},{9,13},{10,... | collective-permute-start | bytes 1327112 | tf_op jit(solution)/shard_map/ppermute | solution.py:45
  107.4 48.0 %collective-permute-start.23 = (bf16[4,24,6912]{2,1,0:T(8,128)(2,1)S(1)}, bf16[4,24,6912]{2,1,0:T(8,128)(2,1)S(1)}, u32[]{:S(2)}, u32[]{:S(2)}) collective-permute-start(bf16[4,24,6912]{2,1,0:T(8,128)(2,1)S(1)} %constant_dynamic-update-slice_fusion.20.refs_0_), channel_id=1, source_target_pairs={{0,1},{1,0},{2,3},{3,2},{4,5},{5,4},{6,7},{7,6},{8,9},{9,8},{10,11... | collective-permute-start | bytes 3981320 | tf_op jit(solution)/shard_map/ppermute | solution.py:45
  111.5 47.8 %collective-permute-start.24 = (bf16[4,24,6912]{2,1,0:T(8,128)(2,1)S(1)}, bf16[4,24,6912]{2,1,0:T(8,128)(2,1)}, u32[]{:S(2)}, u32[]{:S(2)}) collective-permute-start(bf16[4,24,6912]{2,1,0:T(8,128)(2,1)S(1)} %constant_dynamic-update-slice_fusion.22.refs_2_), channel_id=1, source_target_pairs={{0,4},{1,5},{2,6},{3,7},{4,0},{5,1},{6,2},{7,3},{8,12},{9,13},{10,... | collective-permute-start | bytes 3981320 | tf_op jit(solution)/shard_map/ppermute | solution.py:45
  204.0 25.8 %collective-permute-start.29 = (bf16[512,768]{1,0:T(8,128)(2,1)}, bf16[512,768]{1,0:T(8,128)(2,1)}, u32[]{:S(2)}, u32[]{:S(2)}) collective-permute-start(bf16[512,768]{1,0:T(8,128)(2,1)} %add_convert_fusion.9.near_ref), channel_id=1, source_target_pairs={{0,1},{1,0},{2,3},{3,2},{4,5},{5,4},{6,7},{7,6},{8,9},{9,8},{10,11... | collective-permute-start | bytes 2359304 | tf_op jit(solution)/shard_map/ppermute | solution.py:45
  305.4 23.0 %collective-permute-start.30 = (bf16[4,2,1,2,24,3072]{5,4,3,1,0,2:T(8,128)(2,1)}, bf16[4,2,1,2,24,3072]{5,4,3,1,0,2:T(8,128)(2,1)}, u32[]{:S(2)}, u32[]{:S(2)}) collective-permute-start(bf16[4,2,1,2,24,3072]{5,4,3,1,0,2:T(8,128)(2,1)} %bitcast.20), channel_id=1, source_target_pairs={{0,2},{1,3},{2,0},{3,1},{4,6},{5,7},{6,4},{7,5},{8,10},{9,11},{10,... | collective-permute-start | bytes 7077896 | tf_op jit(solution)/shard_map/ppermute | solution.py:45
  332.9 26.7 %collective-permute-start.31 = (bf16[512,768]{1,0:T(8,128)(2,1)}, bf16[512,768]{1,0:T(8,128)(2,1)S(1)}, u32[]{:S(2)}, u32[]{:S(2)}) collective-permute-start(bf16[512,768]{1,0:T(8,128)(2,1)} %fusion.11), channel_id=1, source_target_pairs={{0,1},{1,0},{2,3},{3,2},{4,5},{5,4},{6,7},{7,6},{8,9},{9,8},{10,11... | collective-permute-start | bytes 2359304 | tf_op jit(solution)/shard_map/ppermute | solution.py:45
  337.7 25.0 %collective-permute-start.32 = (bf16[2,1,1,2,24,3072]{5,4,3,1,0,2:T(8,128)(2,1)}, bf16[2,1,1,2,24,3072]{5,4,3,1,0,2:T(8,128)(2,1)}, u32[]{:S(2)}, u32[]{:S(2)}) collective-permute-start(bf16[2,1,1,2,24,3072]{5,4,3,1,0,2:T(8,128)(2,1)} %get-tuple-element.479), channel_id=1, source_target_pairs={{0,4},{1,5},{2,6},{3,7},{4,0},{5,1},{6,2},{7,3},{8,12},{9,13},{10,... | collective-permute-start | bytes 1769480 | tf_op jit(solution)/shard_map/ppermute | solution.py:45
  339.4 26.2 %collective-permute-start.33 = (bf16[2,2,1,1,24,3072]{5,4,3,1,0,2:T(8,128)(2,1)}, bf16[2,2,1,1,24,3072]{5,4,3,1,0,2:T(8,128)(2,1)}, u32[]{:S(2)}, u32[]{:S(2)}) collective-permute-start(bf16[2,2,1,1,24,3072]{5,4,3,1,0,2:T(8,128)(2,1)} %get-tuple-element.477), channel_id=1, source_target_pairs={{0,1},{1,0},{2,3},{3,2},{4,5},{5,4},{6,7},{7,6},{8,9},{9,8},{10,11... | collective-permute-start | bytes 1769480 | tf_op jit(solution)/shard_map/ppermute | solution.py:45
  365.6 28.9 %collective-permute-start.36 = (bf16[4,2,1,2,24,6144]{5,4,3,2,1,0:T(8,128)(2,1)}, bf16[4,2,1,2,24,6144]{5,4,3,2,1,0:T(8,128)(2,1)}, u32[]{:S(2)}, u32[]{:S(2)}) collective-permute-start(bf16[4,2,1,2,24,6144]{5,4,3,2,1,0:T(8,128)(2,1)} %bitcast.26), channel_id=1, source_target_pairs={{0,2},{1,3},{2,0},{3,1},{4,6},{5,7},{6,4},{7,5},{8,10},{9,11},{10,... | collective-permute-start | bytes 14155784 | tf_op jit(solution)/shard_map/ppermute | solution.py:45
  376.1 18.3 %collective-permute-start.34 = (bf16[2,1,1,1,24,3072]{5,4,3,1,0,2:T(8,128)(2,1)}, bf16[2,1,1,1,24,3072]{5,4,3,1,0,2:T(8,128)(2,1)S(1)}, u32[]{:S(2)}, u32[]{:S(2)}) collective-permute-start(bf16[2,1,1,1,24,3072]{5,4,3,1,0,2:T(8,128)(2,1)} %get-tuple-element.497), channel_id=1, source_target_pairs={{0,1},{1,0},{2,3},{3,2},{4,5},{5,4},{6,7},{7,6},{8,9},{9,8},{10,11... | collective-permute-start | bytes 884744 | tf_op jit(solution)/shard_map/ppermute | solution.py:45
  379.1 15.3 %collective-permute-start.35 = (bf16[2,1,1,1,24,3072]{5,4,3,1,0,2:T(8,128)(2,1)}, bf16[2,1,1,1,24,3072]{5,4,3,1,0,2:T(8,128)(2,1)S(1)}, u32[]{:S(2)}, u32[]{:S(2)}) collective-permute-start(bf16[2,1,1,1,24,3072]{5,4,3,1,0,2:T(8,128)(2,1)} %get-tuple-element.495), channel_id=1, source_target_pairs={{0,4},{1,5},{2,6},{3,7},{4,0},{5,1},{6,2},{7,3},{8,12},{9,13},{10,... | collective-permute-start | bytes 884744 | tf_op jit(solution)/shard_map/ppermute | solution.py:45
  402.3 28.1 %collective-permute-start.38 = (bf16[2,1,1,2,24,6144]{5,4,3,2,1,0:T(8,128)(2,1)}, bf16[2,1,1,2,24,6144]{5,4,3,2,1,0:T(8,128)(2,1)}, u32[]{:S(2)}, u32[]{:S(2)}) collective-permute-start(bf16[2,1,1,2,24,6144]{5,4,3,2,1,0:T(8,128)(2,1)} %get-tuple-element.453), channel_id=1, source_target_pairs={{0,4},{1,5},{2,6},{3,7},{4,0},{5,1},{6,2},{7,3},{8,12},{9,13},{10,... | collective-permute-start | bytes 3538952 | tf_op jit(solution)/shard_map/ppermute | solution.py:45
  405.0 27.9 %collective-permute-start.39 = (bf16[2,2,1,1,24,6144]{5,4,3,2,1,0:T(8,128)(2,1)}, bf16[2,2,1,1,24,6144]{5,4,3,2,1,0:T(8,128)(2,1)}, u32[]{:S(2)}, u32[]{:S(2)}) collective-permute-start(bf16[2,2,1,1,24,6144]{5,4,3,2,1,0:T(8,128)(2,1)} %get-tuple-element.451), channel_id=1, source_target_pairs={{0,1},{1,0},{2,3},{3,2},{4,5},{5,4},{6,7},{7,6},{8,9},{9,8},{10,11... | collective-permute-start | bytes 3538952 | tf_op jit(solution)/shard_map/ppermute | solution.py:45
  406.1 26.8 %collective-permute-start.40 = (bf16[4,2,1,2,24,3072]{5,4,3,1,0,2:T(8,128)(2,1)}, bf16[4,2,1,2,24,3072]{5,4,3,1,0,2:T(8,128)(2,1)}, u32[]{:S(2)}, u32[]{:S(2)}) collective-permute-start(bf16[4,2,1,2,24,3072]{5,4,3,1,0,2:T(8,128)(2,1)} %bitcast.25), channel_id=1, source_target_pairs={{0,2},{1,3},{2,0},{3,1},{4,6},{5,7},{6,4},{7,5},{8,10},{9,11},{10,... | collective-permute-start | bytes 7077896 | tf_op jit(solution)/shard_map/ppermute | solution.py:45
  409.8 17.2 %collective-permute-start.37 = (bf16[2,1,1,1,24,3072]{5,4,3,1,0,2:T(8,128)(2,1)S(1)}, bf16[2,1,1,1,24,3072]{5,4,3,1,0,2:T(8,128)(2,1)S(1)}, u32[]{:S(2)}, u32[]{:S(2)}) collective-permute-start(bf16[2,1,1,1,24,3072]{5,4,3,1,0,2:T(8,128)(2,1)S(1)} %get-tuple-element.475), channel_id=1, source_target_pairs={{0,16},{1,17},{2,18},{3,19},{4,20},{5,21},{6,22},{7,23},{8,24},{9,... | collective-permute-start | bytes 884744 | tf_op jit(solution)/shard_map/ppermute | solution.py:34
  432.9 14.7 %collective-permute-start.41 = (bf16[1,1,1,1,24,3072]{5,4,3,1,0,2:T(8,128)(2,1)S(1)}, bf16[1,1,1,1,24,3072]{5,4,3,1,0,2:T(8,128)(2,1)S(1)}, u32[]{:S(2)}, u32[]{:S(2)}) collective-permute-start(bf16[1,1,1,1,24,3072]{5,4,3,1,0,2:T(8,128)(2,1)S(1)} %get-tuple-element.511), channel_id=1, source_target_pairs={{0,8},{1,9},{2,10},{3,11},{4,12},{5,13},{6,14},{7,15},{8,0},{9,1},... | collective-permute-start | bytes 442376 | tf_op jit(solution)/shard_map/ppermute | solution.py:34
  437.0 35.5 %collective-permute-start.42 = (bf16[2,1,1,1,24,6144]{5,4,3,2,1,0:T(8,128)(2,1)S(1)}, bf16[2,1,1,1,24,6144]{5,4,3,2,1,0:T(8,128)(2,1)}, u32[]{:S(2)}, u32[]{:S(2)}) collective-permute-start(bf16[2,1,1,1,24,6144]{5,4,3,2,1,0:T(8,128)(2,1)S(1)} %get-tuple-element.473), channel_id=1, source_target_pairs={{0,1},{1,0},{2,3},{3,2},{4,5},{5,4},{6,7},{7,6},{8,9},{9,8},{10,11... | collective-permute-start | bytes 1769480 | tf_op jit(solution)/shard_map/ppermute | solution.py:45
  440.8 31.7 %collective-permute-start.43 = (bf16[2,1,1,1,24,6144]{5,4,3,2,1,0:T(8,128)(2,1)S(1)}, bf16[2,1,1,1,24,6144]{5,4,3,2,1,0:T(8,128)(2,1)}, u32[]{:S(2)}, u32[]{:S(2)}) collective-permute-start(bf16[2,1,1,1,24,6144]{5,4,3,2,1,0:T(8,128)(2,1)S(1)} %get-tuple-element.471), channel_id=1, source_target_pairs={{0,4},{1,5},{2,6},{3,7},{4,0},{5,1},{6,2},{7,3},{8,12},{9,13},{10,... | collective-permute-start | bytes 1769480 | tf_op jit(solution)/shard_map/ppermute | solution.py:45
  441.3 31.2 %collective-permute-start.46 = (bf16[4,2,1,2,24,3840]{5,4,3,2,1,0:T(8,128)(2,1)}, bf16[4,2,1,2,24,3840]{5,4,3,2,1,0:T(8,128)(2,1)}, u32[]{:S(2)}, u32[]{:S(2)}) collective-permute-start(bf16[4,2,1,2,24,3840]{5,4,3,2,1,0:T(8,128)(2,1)} %bitcast.30), channel_id=1, source_target_pairs={{0,2},{1,3},{2,0},{3,1},{4,6},{5,7},{6,4},{7,5},{8,10},{9,11},{10,... | collective-permute-start | bytes 8847368 | tf_op jit(solution)/shard_map/ppermute | solution.py:45
  445.4 27.1 %collective-permute-start.44 = (bf16[2,1,1,2,24,3072]{5,4,3,1,0,2:T(8,128)(2,1)S(1)}, bf16[2,1,1,2,24,3072]{5,4,3,1,0,2:T(8,128)(2,1)S(1)}, u32[]{:S(2)}, u32[]{:S(2)}) collective-permute-start(bf16[2,1,1,2,24,3072]{5,4,3,1,0,2:T(8,128)(2,1)S(1)} %get-tuple-element.469), channel_id=1, source_target_pairs={{0,4},{1,5},{2,6},{3,7},{4,0},{5,1},{6,2},{7,3},{8,12},{9,13},{10,... | collective-permute-start | bytes 1769480 | tf_op jit(solution)/shard_map/ppermute | solution.py:45
  447.6 24.9 %collective-permute-start.45 = (bf16[2,2,1,1,24,3072]{5,4,3,1,0,2:T(8,128)(2,1)}, bf16[2,2,1,1,24,3072]{5,4,3,1,0,2:T(8,128)(2,1)S(1)}, u32[]{:S(2)}, u32[]{:S(2)}) collective-permute-start(bf16[2,2,1,1,24,3072]{5,4,3,1,0,2:T(8,128)(2,1)} %get-tuple-element.467), channel_id=1, source_target_pairs={{0,1},{1,0},{2,3},{3,2},{4,5},{5,4},{6,7},{7,6},{8,9},{9,8},{10,11... | collective-permute-start | bytes 1769480 | tf_op jit(solution)/shard_map/ppermute | solution.py:45
  477.9 20.7 %collective-permute-start.47 = (bf16[512,768]{1,0:T(8,128)(2,1)}, bf16[512,768]{1,0:T(8,128)(2,1)}, u32[]{:S(2)}, u32[]{:S(2)}) collective-permute-start(bf16[512,768]{1,0:T(8,128)(2,1)} %convolution_convert_fusion.2), channel_id=1, source_target_pairs={{0,1},{1,0},{2,3},{3,2},{4,5},{5,4},{6,7},{7,6},{8,9},{9,8},{10,11... | collective-permute-start | bytes 2359304 | tf_op jit(solution)/shard_map/ppermute | solution.py:45
  488.7 28.0 %collective-permute-start.48 = (bf16[2,1,1,1,24,6144]{5,4,3,2,1,0:T(8,128)(2,1)S(1)}, bf16[2,1,1,1,24,6144]{5,4,3,2,1,0:T(8,128)(2,1)S(1)}, u32[]{:S(2)}, u32[]{:S(2)}) collective-permute-start(bf16[2,1,1,1,24,6144]{5,4,3,2,1,0:T(8,128)(2,1)S(1)} %get-tuple-element.447), channel_id=1, source_target_pairs={{0,16},{1,17},{2,18},{3,19},{4,20},{5,21},{6,22},{7,23},{8,24},{9,... | collective-permute-start | bytes 1769480 | tf_op jit(solution)/shard_map/ppermute | solution.py:34
  489.6 15.2 %collective-permute-start.49 = (bf16[2,1,1,1,24,3072]{5,4,3,1,0,2:T(8,128)(2,1)S(1)}, bf16[2,1,1,1,24,3072]{5,4,3,1,0,2:T(8,128)(2,1)S(1)}, u32[]{:S(2)}, u32[]{:S(2)}) collective-permute-start(bf16[2,1,1,1,24,3072]{5,4,3,1,0,2:T(8,128)(2,1)S(1)} %get-tuple-element.493), channel_id=1, source_target_pairs={{0,1},{1,0},{2,3},{3,2},{4,5},{5,4},{6,7},{7,6},{8,9},{9,8},{10,11... | collective-permute-start | bytes 884744 | tf_op jit(solution)/shard_map/ppermute | solution.py:45
  490.7 14.2 %collective-permute-start.50 = (bf16[2,1,1,1,24,3072]{5,4,3,1,0,2:T(8,128)(2,1)S(1)}, bf16[2,1,1,1,24,3072]{5,4,3,1,0,2:T(8,128)(2,1)S(1)}, u32[]{:S(2)}, u32[]{:S(2)}) collective-permute-start(bf16[2,1,1,1,24,3072]{5,4,3,1,0,2:T(8,128)(2,1)S(1)} %get-tuple-element.491), channel_id=1, source_target_pairs={{0,4},{1,5},{2,6},{3,7},{4,0},{5,1},{6,2},{7,3},{8,12},{9,13},{10,... | collective-permute-start | bytes 884744 | tf_op jit(solution)/shard_map/ppermute | solution.py:45
  494.7 22.0 %collective-permute-start.51 = (bf16[2,1,1,2,24,3840]{5,4,3,2,1,0:T(8,128)(2,1)S(1)}, bf16[2,1,1,2,24,3840]{5,4,3,2,1,0:T(8,128)(2,1)S(1)}, u32[]{:S(2)}, u32[]{:S(2)}) collective-permute-start(bf16[2,1,1,2,24,3840]{5,4,3,2,1,0:T(8,128)(2,1)S(1)} %get-tuple-element.463), channel_id=1, source_target_pairs={{0,4},{1,5},{2,6},{3,7},{4,0},{5,1},{6,2},{7,3},{8,12},{9,13},{10,... | collective-permute-start | bytes 2211848 | tf_op jit(solution)/shard_map/ppermute | solution.py:45
  498.6 21.3 %collective-permute-start.52 = (bf16[2,2,1,1,24,3840]{5,4,3,2,1,0:T(8,128)(2,1)S(1)}, bf16[2,2,1,1,24,3840]{5,4,3,2,1,0:T(8,128)(2,1)S(1)}, u32[]{:S(2)}, u32[]{:S(2)}) collective-permute-start(bf16[2,2,1,1,24,3840]{5,4,3,2,1,0:T(8,128)(2,1)S(1)} %get-tuple-element.461), channel_id=1, source_target_pairs={{0,1},{1,0},{2,3},{3,2},{4,5},{5,4},{6,7},{7,6},{8,9},{9,8},{10,11... | collective-permute-start | bytes 2211848 | tf_op jit(solution)/shard_map/ppermute | solution.py:45
  521.0 17.5 %collective-permute-start.53 = (bf16[1,1,1,1,24,6144]{5,4,3,2,1,0:T(8,128)(2,1)}, bf16[1,1,1,1,24,6144]{5,4,3,2,1,0:T(8,128)(2,1)}, u32[]{:S(2)}, u32[]{:S(2)}) collective-permute-start(bf16[1,1,1,1,24,6144]{5,4,3,2,1,0:T(8,128)(2,1)} %get-tuple-element.489), channel_id=1, source_target_pairs={{0,8},{1,9},{2,10},{3,11},{4,12},{5,13},{6,14},{7,15},{8,0},{9,1},... | collective-permute-start | bytes 884744 | tf_op jit(solution)/shard_map/ppermute | solution.py:34
  521.9 16.6 %collective-permute-start.54 = (bf16[2,1,1,1,24,3072]{5,4,3,1,0,2:T(8,128)(2,1)}, bf16[2,1,1,1,24,3072]{5,4,3,1,0,2:T(8,128)(2,1)}, u32[]{:S(2)}, u32[]{:S(2)}) collective-permute-start(bf16[2,1,1,1,24,3072]{5,4,3,1,0,2:T(8,128)(2,1)} %get-tuple-element.465), channel_id=1, source_target_pairs={{0,16},{1,17},{2,18},{3,19},{4,20},{5,21},{6,22},{7,23},{8,24},{9,... | collective-permute-start | bytes 884744 | tf_op jit(solution)/shard_map/ppermute | solution.py:34
  525.5 13.0 %collective-permute-start.55 = (bf16[2,1,1,1,24,3840]{5,4,3,2,1,0:T(8,128)(2,1)}, bf16[2,1,1,1,24,3840]{5,4,3,2,1,0:T(8,128)(2,1)}, u32[]{:S(2)}, u32[]{:S(2)}) collective-permute-start(bf16[2,1,1,1,24,3840]{5,4,3,2,1,0:T(8,128)(2,1)} %get-tuple-element.487), channel_id=1, source_target_pairs={{0,1},{1,0},{2,3},{3,2},{4,5},{5,4},{6,7},{7,6},{8,9},{9,8},{10,11... | collective-permute-start | bytes 1105928 | tf_op jit(solution)/shard_map/ppermute | solution.py:45
  526.5 19.2 %collective-permute-start.57 = (bf16[4,2,1,2,24,2304]{5,4,3,2,1,0:T(8,128)(2,1)}, bf16[4,2,1,2,24,2304]{5,4,3,2,1,0:T(8,128)(2,1)S(1)}, u32[]{:S(2)}, u32[]{:S(2)}) collective-permute-start(bf16[4,2,1,2,24,2304]{5,4,3,2,1,0:T(8,128)(2,1)} %bitcast.34), channel_id=1, source_target_pairs={{0,2},{1,3},{2,0},{3,1},{4,6},{5,7},{6,4},{7,5},{8,10},{9,11},{10,... | collective-permute-start | bytes 5308424 | tf_op jit(solution)/shard_map/ppermute | solution.py:45
  548.3 16.5 %collective-permute-start.61 = (bf16[2,1,1,1,24,3840]{5,4,3,2,1,0:T(8,128)(2,1)S(1)}, bf16[2,1,1,1,24,3840]{5,4,3,2,1,0:T(8,128)(2,1)S(1)}, u32[]{:S(2)}, u32[]{:S(2)}) collective-permute-start(bf16[2,1,1,1,24,3840]{5,4,3,2,1,0:T(8,128)(2,1)S(1)} %get-tuple-element.459), channel_id=1, source_target_pairs={{0,16},{1,17},{2,18},{3,19},{4,20},{5,21},{6,22},{7,23},{8,24},{9,... | collective-permute-start | bytes 1105928 | tf_op jit(solution)/shard_map/ppermute | solution.py:34
  549.6 15.3 %collective-permute-start.62 = (bf16[2,1,1,2,24,2304]{5,4,3,2,1,0:T(8,128)(2,1)S(1)}, bf16[2,1,1,2,24,2304]{5,4,3,2,1,0:T(8,128)(2,1)S(1)}, u32[]{:S(2)}, u32[]{:S(2)}) collective-permute-start(bf16[2,1,1,2,24,2304]{5,4,3,2,1,0:T(8,128)(2,1)S(1)} %get-tuple-element.483), channel_id=1, source_target_pairs={{0,4},{1,5},{2,6},{3,7},{4,0},{5,1},{6,2},{7,3},{8,12},{9,13},{10,... | collective-permute-start | bytes 1327112 | tf_op jit(solution)/shard_map/ppermute | solution.py:45
  550.6 14.3 %collective-permute-start.63 = (bf16[2,2,1,1,24,2304]{5,4,3,2,1,0:T(8,128)(2,1)S(1)}, bf16[2,2,1,1,24,2304]{5,4,3,2,1,0:T(8,128)(2,1)S(1)}, u32[]{:S(2)}, u32[]{:S(2)}) collective-permute-start(bf16[2,2,1,1,24,2304]{5,4,3,2,1,0:T(8,128)(2,1)S(1)} %get-tuple-element.481), channel_id=1, source_target_pairs={{0,1},{1,0},{2,3},{3,2},{4,5},{5,4},{6,7},{7,6},{8,9},{9,8},{10,11... | collective-permute-start | bytes 1327112 | tf_op jit(solution)/shard_map/ppermute | solution.py:45
  (118 other events, 952.0 us)
Sparse Core Ops, SparseCore 0:
  68.9 101.8 all-gather.2
  174.3 64.8 all-gather.4
